TPU v7x, 512 devices: a whole 4x8x8 slice. The times are simulated.
512 devices in a mesh: head: 16 (over y_lo, z), key: 32 (over x, y_hi, core).
Axes of the slice: x: 4, y: 8 (y_hi: 4, y_lo: 2; y = y_hi * 2 + y_lo), z: 8, core: 2. Of those that a mesh axis runs over, the one named last changes fastest.
Arguments:
- query_pos: int32 [256], replicated, may hold values from 16384 to 65535
- mla_query: bfloat16 [128, 256, 576], P('head'), may hold values from -94 to 94
- latent_keys: bfloat16 [65536, 576], P('key'), may hold values from -7 to 7
- index_query: bfloat16 [256, 64, 128], P('head'), may hold values from -48 to 48
- index_keys: bfloat16 [65536, 128], P('key'), may hold values from -7 to 7
- index_weights: float32 [256, 64], P('head'), may hold values from -1.8 to 1.8
Outputs:
- query_grads: float32 [256, 64, 128], P('head')
- key_grads: float32 [65536, 128], P(('key', 'head'))
All inputs are finite; a program needn't handle non-finite values.
Results may differ from a plain program's by a relative error of at most 0.014.
Values sent between devices are 32-bit elements; how exact they have to be, the bound alone decides.
No kernel may reach another device: no remote copies, remote signals or barrier semaphores. Data moves between devices by JAX's collectives and lax.ppermute only.
A program may use at most 128 MiB of HBM per device.

v0:
```python
import jax
import jax.numpy as jnp
from jax import lax
from jax.sharding import Mesh
from jax.sharding import PartitionSpec as P

HEADS = 128
KEY = ("key_0", "key_1", "key_2")
KEY_HEAD = ("key_0", "key_1", "key_2", "head")


attn_scale = 192.0 ** (-0.5)
index_scale = 128.0 ** (-0.5)
masked_fill = -1e30


def sent_to_all(shard, axis):
    size = lax.axis_size(axis)
    return lax.all_to_all(
        jnp.broadcast_to(shard[None], (size, *shard.shape)), axis, 0, 0, tiled=True
    )


def all_in_one(shard, axis):
    leaves = jax.tree.leaves(shard)
    turns = sorted(range(len(leaves)), key=lambda k: -leaves[k].size)
    width = (1, *leaves[turns[0]].shape)[-1]
    lines = [
        jnp.pad(leaves[k].reshape(-1), (0, -leaves[k].size % width)).reshape(-1, width)
        for k in turns
    ]
    both, at, found = (sent_to_all(jnp.concatenate(lines), axis), 0, {})
    for k, line in zip(turns, lines):
        piece = both[:, at : at + len(line)].reshape(len(both), -1)
        found[k] = piece[:, : leaves[k].size].reshape(-1, *leaves[k].shape)
        at += len(line)
    numbers = iter(range(len(leaves)))
    return jax.tree.map(lambda _: found[next(numbers)], shard)


def folded_in_pairs(pieces, combine):
    while len(jax.tree.leaves(pieces)[0]) > 1:
        pieces = jax.vmap(combine)(
            *(jax.tree.map(lambda part: part[side::2], pieces) for side in (0, 1))
        )
    return jax.tree.map(lambda part: part[0], pieces)


def combined_all(shard, axis, combine):
    pieces = all_in_one(shard, axis)
    return folded_in_pairs(pieces, combine)


def cut_along(shard, dim, size):
    before, after = (shard.shape[:dim], shard.shape[dim + 1 :])
    return jnp.moveaxis(shard.reshape(*before, size, -1, *after), dim, 0)


def sum_at_owner(shard, axis, dim):
    parts = cut_along(shard, dim, lax.axis_size(axis))
    arrived = lax.all_to_all(parts, axis, split_axis=0, concat_axis=0, tiled=True)
    return arrived.sum(axis=0)


def padded_to(lines, size):
    spare = -len(lines) % size
    return jnp.pad(lines, [(0, spare)] + [(0, 0)] * (lines.ndim - 1))


def laid_out(parts, dim):
    shape = list(parts.shape[1:])
    shape[dim] *= parts.shape[0]
    return jnp.moveaxis(parts, 0, dim).reshape(shape)


def whole_of(shard, axes, dim):
    far, near = axes
    initial = sent_to_all(shard, far)
    parts = jnp.swapaxes(sent_to_all(initial, near), 0, 1)
    return laid_out(parts.reshape(-1, *shard.shape), dim)


def summed_rows(shard, axes, dim):
    far, near = axes
    parts = cut_along(shard, dim, lax.axis_size(far))
    nearer = sum_at_owner(parts, near, dim + 1)
    arrived = lax.all_to_all(nearer, far, split_axis=0, concat_axis=0, tiled=True)
    return arrived.sum(axis=0)


def total_of(shard, axes):
    lines = shard.reshape(-1, shard.shape[-1])
    padded = padded_to(lines, lax.axis_size(axes[0]) * lax.axis_size(axes[1]))
    whole = whole_of(summed_rows(padded, axes, 0), axes, 0)
    return lax.slice_in_dim(whole, 0, len(lines)).reshape(shard.shape)


def combine_stats(earlier, latter):
    highest = jnp.maximum(earlier[0], latter[0])
    summed = earlier[1] * jnp.exp(earlier[0] - highest) + latter[1] * jnp.exp(latter[0] - highest)
    return (highest, summed)


def shards(query_pos, mla_query, latent_keys, index_query, index_keys, index_weights):
    key_dev = latent_keys.shape[0]
    rows_dev = index_query.shape[0]
    key_start = lax.axis_index(KEY) * key_dev
    key_ids = key_start + jnp.arange(key_dev, dtype=jnp.int32)
    visible = key_ids[None, :] <= query_pos[:, None]
    scores = (
        jnp.einsum("hrc,kc->hrk", mla_query, latent_keys, preferred_element_type=jnp.float32)
        * attn_scale
    )
    masked = jnp.where(visible[None], scores, masked_fill)
    local_max = jnp.max(masked, axis=-1)
    local_sum = jnp.sum(
        jnp.where(visible[None], jnp.exp(masked - local_max[..., None]), 0.0), axis=-1
    )
    highest, overall = combined_all((local_max, local_sum), KEY, combine_stats)
    weights = jnp.where(visible[None], jnp.exp(masked - highest[..., None]), 0.0)
    weights = weights / overall[..., None]
    head_share = jnp.sum(weights / HEADS, axis=0)
    row_start = lax.axis_index("head") * rows_dev
    target = sum_at_owner(head_share, "head", 0)
    row_pos = lax.dynamic_slice_in_dim(query_pos, row_start, rows_dev, 0)
    seen = key_ids[None, :] <= row_pos[:, None]
    index_dots = jnp.einsum(
        "rjd,kd->rjk", index_query, index_keys, preferred_element_type=jnp.float32
    )
    logits = index_scale * jnp.einsum(
        "rj,rjk->rk", index_weights, jnp.maximum(index_dots, 0.0), precision=lax.Precision.HIGHEST
    )
    masked_logits = jnp.where(seen, logits, masked_fill)
    row_max = jnp.max(masked_logits, axis=-1)
    row_sum = jnp.sum(jnp.where(seen, jnp.exp(masked_logits - row_max[:, None]), 0.0), axis=-1)
    row_high, row_total = combined_all((row_max, row_sum), KEY, combine_stats)
    index_probs = jnp.where(seen, jnp.exp(masked_logits - row_high[:, None]), 0.0)
    index_probs = index_probs / row_total[:, None]
    key_count = lax.axis_size(KEY) * key_dev
    slope = (index_probs - target) * key_count
    coef = jnp.where(
        index_dots > 0, slope[:, None, :] * index_weights[:, :, None] * index_scale, 0.0
    ).astype(jnp.bfloat16)
    grad_keys = jnp.einsum("rjk,rjd->kd", coef, index_query, preferred_element_type=jnp.float32)
    grad_rows = jnp.einsum("rjk,kd->rjd", coef, index_keys, preferred_element_type=jnp.float32)
    key_grads = sum_at_owner(grad_keys, "head", 0)
    query_grads = total_of(grad_rows, (("key_0", "key_1"), "key_2"))
    return (query_grads, key_grads)


def solution(mesh):
    finer = Mesh(
        mesh.devices.reshape(mesh.shape["head"], 4, 4, 2), ("head", "key_0", "key_1", "key_2")
    )
    return jax.shard_map(
        shards,
        mesh=finer,
        in_specs=(
            P(),
            P("head", None, None),
            P(KEY, None),
            P("head", None, None),
            P(KEY, None),
            P("head", None),
        ),
        out_specs=(P("head", None, None), P(KEY_HEAD, None)),
        check_vma=False,
    )
```

profile of v0, /device:TPU:8, one launch (start us, length us, event | category | flops | bytes accessed | tf_op | source)
XLA Modules:
  0.0 216.1 jit_solution(12538106095297390884)
XLA Ops:
  0.7 1.2 broadcast_compare_fusion
  2.3 10.4 %fusion = (f32[8,256]{1,0:T(8,128)S(1)}, f32[8,256,2048]{2,1,0:T(8,128)S(1)}) fusion(pred[256,2048]{1,0:T(8,128)(4,1)S(1)} %broadcast_compare_fusion, bf16[8,256,576]{1,2,0:T(8,128)(2,1)S(1)} %copy-done, bf16[2048,576]{0,1:T(8,128)(2,1)} %param.8), kind=kOutput, calls=%fused_computation.3 | convolution fusion | flops 4844419072 | bytes 22028288 | tf_op jit(solution)/shard_map/hrc,kc->hrk/dot_general | solution.py:111
  12.8 5.1 %select_reduce_fusion = f32[8,256]{1,0:T(8,128)S(1)} fusion(f32[8,256,2048]{2,1,0:T(8,128)S(1)} %get-tuple-element.27, f32[8,256]{1,0:T(8,128)S(1)} %get-tuple-element.26, pred[256,2048]{1,0:T(8,128)(4,1)S(1)} %broadcast_compare_fusion), kind=kLoop, calls=%fused_computation.1 | loop fusion | flops 20969472 | bytes 17317888 | tf_op jit(solution)/shard_map/reduce_sum | solution.py:116
  19.3 9.2 %all-to-all-start.1 = ((f32[32,16,256]{2,1,0:T(8,128)}), f32[32,16,256]{2,1,0:T(8,128)S(1)}, u32[]{:S(2)}, u32[]{:S(2)}) async-start(f32[32,16,256]{2,1,0:T(8,128)} %broadcast_in_dim.73), calls=%async_computation.1 | async-start | bytes 1048576 | tf_op jit(solution)/shard_map/all_to_all | solution.py:19
  28.6 6.4 %fusion.3 = (u16[64,2048]{1,0:T(8,128)(2,1)}, f32[16,64,2048]{2,1,0:T(8,128)}) fusion(bf16[16,64,128]{2,1,0:T(8,128)(2,1)} %param.9, bf16[2048,128]{1,0:T(8,128)(2,1)} %param.10), kind=kOutput, calls=%fused_computation.9 | convolution fusion | flops 547225600 | bytes 9437184 | tf_op jit(solution)/shard_map/rjd,kd->rjk/dot_general | solution.py:127
  35.0 6.9 %fusion.1 = f32[16,1,2048]{2,1,0:T(1,128)S(1)} fusion(f32[16,64,1]{1,2,0:T(1,128)S(1)} %bitcast.63, f32[16,64,2048]{2,1,0:T(8,128)} %get-tuple-element.29), kind=kOutput, calls=%fused_computation.7 | convolution fusion | flops 27262976 | bytes 8523776 | tf_op jit(solution)/shard_map/rj,rjk->rk/dot_general | solution.py:130
  42.9 2.7 %all-to-all-done.1 = f32[32,16,256]{2,1,0:T(8,128)S(1)} async-done(((f32[32,16,256]{2,1,0:T(8,128)}), f32[32,16,256]{2,1,0:T(8,128)S(1)}, u32[]{:S(2)}, u32[]{:S(2)}) %all-to-all-start.1) | async-done | bytes 524320 | tf_op jit(solution)/shard_map/all_to_all | solution.py:19
  45.7 1.3 broadcast_in_dim.69
  46.9 7.0 %all-to-all-start = ((f32[32,2,16]{2,1,0:T(2,128)}), f32[32,2,16]{2,1,0:T(2,128)}, u32[]{:S(2)}, u32[]{:S(2)}) async-start(f32[32,2,16]{2,1,0:T(2,128)} %broadcast_in_dim.69), calls=%async_computation | async-start | bytes 65536 | tf_op jit(solution)/shard_map/all_to_all | solution.py:19
  54.2 10.4 %multiply_reduce_fusion = f32[256,2048]{1,0:T(8,128)} fusion(f32[8,256,2048]{2,1,0:T(8,128)} %copy-done.1, f32[8,256]{1,0:T(8,128)S(1)} %get-tuple-element.23, f32[8,256]{1,0:T(8,128)S(1)} %get-tuple-element.22, pred[256,2048]{1,0:T(8,128)(4,1)S(1)} %broadcast_compare_fusion), kind=kLoop, calls=%fused_computation | loop fusion | flops 28835840 | bytes 19415040 | tf_op jit(solution)/shard_map/reduce_sum | solution.py:122
  64.6 11.8 %all-to-all-start.2 = ((f32[16,16,2048]{2,1,0:T(8,128)}), f32[16,16,2048]{2,1,0:T(8,128)}, u32[]{:S(2)}, u32[]{:S(2)}) async-start(f32[16,16,2048]{2,1,0:T(8,128)} %bitcast.54), calls=%async_computation.2 | async-start | bytes 4194304 | tf_op jit(solution)/shard_map/all_to_all | solution.py:61
  76.4 0.9 fusion.29
  77.7 52.2 %all-to-all-done.2 = f32[16,16,2048]{2,1,0:T(8,128)} async-done(((f32[16,16,2048]{2,1,0:T(8,128)}), f32[16,16,2048]{2,1,0:T(8,128)}, u32[]{:S(2)}, u32[]{:S(2)}) %all-to-all-start.2) | async-done | bytes 2097184 | tf_op jit(solution)/shard_map/all_to_all | solution.py:61
  129.8 1.7 reduce_sum.66
  132.3 2.5 %fusion.6 = f32[16,64,128]{2,1,0:T(8,128)S(1)} fusion(f32[16,64]{1,0:T(8,128)S(1)} %copy-done.4, f32[16,2048]{1,0:T(8,128)S(1)} %fusion.17, u16[64,2048]{1,0:T(8,128)(2,1)} %get-tuple-element.28, bf16[2048,128]{1,0:T(8,128)(2,1)S(1)} %copy-done.2), kind=kOutput, calls=%fused_computation.12 | convolution fusion | flops 553648128 | bytes 1445888 | tf_op jit(solution)/shard_map/rjk,kd->rjd/dot_general | solution.py:145
  134.9 4.2 %all_to_all.40 = f32[2,16,32,128]{3,2,1,0:T(8,128)S(1)} all-to-all(f32[2,16,32,128]{3,2,1,0:T(8,128)S(1)} %bitcast.55), channel_id=1, replica_groups=mesh['head'=16,'key_0'=4,'key_1'=4,'key_2'=2] {'key_2'}, dimensions={0} | all-to-all | bytes 1048576 | tf_op jit(solution)/shard_map/all_to_all | solution.py:61
  139.1 22.4 %all_to_all.41 = f32[16,32,128]{2,1,0:T(8,128)S(1)} all-to-all(f32[16,32,128]{2,1,0:T(8,128)S(1)} %reduce_sum.67), channel_id=1, replica_groups=mesh['head'=16,'key_0'=4,'key_1'=4,'key_2'=2] {'key_0','key_1'}, dimensions={0} | all-to-all | bytes 524288 | tf_op jit(solution)/shard_map/all_to_all | solution.py:87
  162.2 3.5 %all-to-all-start.5 = ((f32[16,32,128]{2,1,0:T(8,128)}), f32[16,32,128]{2,1,0:T(8,128)S(1)}, u32[]{:S(2)}, u32[]{:S(2)}) async-start(f32[16,32,128]{2,1,0:T(8,128)} %broadcast_in_dim.74), calls=%async_computation.5 | async-start | bytes 524288 | tf_op jit(solution)/shard_map/all_to_all | solution.py:19
  165.8 3.9 %fusion.5 = f32[2048,128,1]{1,0,2:T(8,128)} fusion(bf16[16,64,128]{2,1,0:T(8,128)(2,1)} %param.9, f32[16,64]{1,0:T(8,128)S(1)} %copy-done.4, f32[16,2048]{1,0:T(8,128)} %copy-done.3, u16[64,2048]{1,0:T(8,128)(2,1)} %get-tuple-element.28), kind=kOutput, calls=%fused_computation.11 | convolution fusion | flops 553648128 | bytes 1708032 | tf_op jit(solution)/shard_map/rjk,rjd->kd/dot_general | solution.py:144
  169.7 9.2 %all-to-all-done.5 = f32[16,32,128]{2,1,0:T(8,128)S(1)} async-done(((f32[16,32,128]{2,1,0:T(8,128)}), f32[16,32,128]{2,1,0:T(8,128)S(1)}, u32[]{:S(2)}, u32[]{:S(2)}) %all-to-all-start.5) | async-done | bytes 262176 | tf_op jit(solution)/shard_map/all_to_all | solution.py:19
  179.0 4.9 %all_to_all.42 = f32[2,16,32,128]{3,2,1,0:T(8,128)} all-to-all(f32[2,16,32,128]{3,2,1,0:T(8,128)S(1)} %broadcast_in_dim.75), channel_id=1, replica_groups=mesh['head'=16,'key_0'=4,'key_1'=4,'key_2'=2] {'key_2'}, dimensions={0} | all-to-all | bytes 1048576 | tf_op jit(solution)/shard_map/all_to_all | solution.py:19
  183.9 5.0 %all-to-all-start.7 = ((f32[16,128,128]{2,1,0:T(8,128)}), f32[16,128,128]{2,1,0:T(8,128)S(1)}, u32[]{:S(2)}, u32[]{:S(2)}) async-start(f32[16,128,128]{2,1,0:T(8,128)} %bitcast.56), calls=%async_computation.7 | async-start | bytes 2097152 | tf_op jit(solution)/shard_map/all_to_all | solution.py:61
  189.0 1.9 copy.15
  190.8 24.6 %all-to-all-done.7 = f32[16,128,128]{2,1,0:T(8,128)S(1)} async-done(((f32[16,128,128]{2,1,0:T(8,128)}), f32[16,128,128]{2,1,0:T(8,128)S(1)}, u32[]{:S(2)}, u32[]{:S(2)}) %all-to-all-start.7) | async-done | bytes 1048608 | tf_op jit(solution)/shard_map/all_to_all | solution.py:61
  (56 shorter events, 5.8 us)
Async XLA Ops:
  0.6 1.7 copy-start
  12.7 5.7 %copy-start.1 = (f32[8,256,2048]{2,1,0:T(8,128)}, f32[8,256,2048]{2,1,0:T(8,128)S(1)}, u32[]{:S(2)}) copy-start(f32[8,256,2048]{2,1,0:T(8,128)S(1)} %get-tuple-element.27) | copy-start | bytes 50331652
  18.5 16.5 %copy-start.6 = (s32[256]{0:T(256)S(1)}, s32[256]{0:T(256)}, u32[]{:S(2)}) copy-start(s32[256]{0:T(256)} %param.6) | copy-start | bytes 3076
  18.5 16.6 %copy-start.4 = (f32[16,64]{1,0:T(8,128)S(1)}, f32[16,64]{1,0:T(8,128)}, u32[]{:S(2)}) copy-start(f32[16,64]{1,0:T(8,128)} %param.11) | copy-start | bytes 12292
  19.3 26.4 %all-to-all-start.1 = ((f32[32,16,256]{2,1,0:T(8,128)}), f32[32,16,256]{2,1,0:T(8,128)S(1)}, u32[]{:S(2)}, u32[]{:S(2)}) async-start(f32[32,16,256]{2,1,0:T(8,128)} %broadcast_in_dim.73), calls=%async_computation.1 | async-start | bytes 1048576 | tf_op jit(solution)/shard_map/all_to_all | solution.py:19
  35.0 7.3 %copy-start.5 = (s32[16]{0:T(128)}, s32[16]{0:T(128)S(1)}, u32[]{:S(2)}) copy-start(s32[16]{0:T(128)S(1)} %dynamic_slice.3) | copy-start | bytes 196
  46.9 17.7 %all-to-all-start = ((f32[32,2,16]{2,1,0:T(2,128)}), f32[32,2,16]{2,1,0:T(2,128)}, u32[]{:S(2)}, u32[]{:S(2)}) async-start(f32[32,2,16]{2,1,0:T(2,128)} %broadcast_in_dim.69), calls=%async_computation | async-start | bytes 65536 | tf_op jit(solution)/shard_map/all_to_all | solution.py:19
  54.2 78.1 %copy-start.2 = (bf16[2048,128]{1,0:T(8,128)(2,1)S(1)}, bf16[2048,128]{1,0:T(8,128)(2,1)}, u32[]{:S(2)}) copy-start(bf16[2048,128]{1,0:T(8,128)(2,1)} %param.10) | copy-start | bytes 1572868
  64.6 65.2 %all-to-all-start.2 = ((f32[16,16,2048]{2,1,0:T(8,128)}), f32[16,16,2048]{2,1,0:T(8,128)}, u32[]{:S(2)}, u32[]{:S(2)}) async-start(f32[16,16,2048]{2,1,0:T(8,128)} %bitcast.54), calls=%async_computation.2 | async-start | bytes 4194304 | tf_op jit(solution)/shard_map/all_to_all | solution.py:61
  132.2 2.6 %copy-start.3 = (f32[16,2048]{1,0:T(8,128)}, f32[16,2048]{1,0:T(8,128)S(1)}, u32[]{:S(2)}) copy-start(f32[16,2048]{1,0:T(8,128)S(1)} %fusion.17) | copy-start | bytes 393220
  162.2 16.7 %all-to-all-start.5 = ((f32[16,32,128]{2,1,0:T(8,128)}), f32[16,32,128]{2,1,0:T(8,128)S(1)}, u32[]{:S(2)}, u32[]{:S(2)}) async-start(f32[16,32,128]{2,1,0:T(8,128)} %broadcast_in_dim.74), calls=%async_computation.5 | async-start | bytes 524288 | tf_op jit(solution)/shard_map/all_to_all | solution.py:19
  183.9 31.5 %all-to-all-start.7 = ((f32[16,128,128]{2,1,0:T(8,128)}), f32[16,128,128]{2,1,0:T(8,128)S(1)}, u32[]{:S(2)}, u32[]{:S(2)}) async-start(f32[16,128,128]{2,1,0:T(8,128)} %bitcast.56), calls=%async_computation.7 | async-start | bytes 2097152 | tf_op jit(solution)/shard_map/all_to_all | solution.py:61
where the time goes:
time: 217 us; the launch traced here: 216 us
  waiting for transfers between devices  88.7 us (41%)
  starting transfers between devices  36.6 us (17%)
  blocking collectives  31.5 us (15%)
  matrix products  30.2 us (14%)
  other arithmetic  21 us (10%)
  local copies, waits for them, and re-layouts  7.21 us (3%)
    all_to_all x2, waiting for transfers between devices, sum_at_owner(): lax.all_to_all(parts, axis, split_axis=0, concat_axis=0, tiled=True)  76.8 us
    all_to_all x1, blocking collectives, summed_rows(): lax.all_to_all(nearer, far, split_axis=0, concat_axis=0, tiled=True)  22.4 us
    all_to_all x3, starting transfers between devices, sent_to_all(): lax.all_to_all(jnp.broadcast_to(shard[None], (size, *shard.shape)), axis,...  19.8 us
    all_to_all x2, starting transfers between devices, sum_at_owner(): lax.all_to_all(parts, axis, split_axis=0, concat_axis=0, tiled=True)  16.8 us
    all_to_all x3, waiting for transfers between devices, sent_to_all(): lax.all_to_all(jnp.broadcast_to(shard[None], (size, *shard.shape)), axis,...  12 us
    reduce_sum x1, other arithmetic, shards(): head_share = jnp.sum(weights / HEADS, axis=0)  10.4 us
    dot_general x1, matrix products, shards(): jnp.einsum('hrc,kc->hrk', mla_query, latent_keys, preferred_element_type=...  10.4 us
    dot_general x1, matrix products, shards(): jnp.einsum('rj,rjk->rk', index_weights, jnp.maximum(index_dots, 0.0), pre...  6.91 us
  transfers between devices with their start and end apart: 5, of which 4 were waited for; matrix products, arithmetic and copies ran while one was open for 15% of the time, Pallas kernels for 0%

commit v1 on v0

v1 whole, which is shorter than its diff:
```python
import math

import jax
import jax.numpy as jnp
from jax import lax
from jax.experimental import pallas as pl
from jax.experimental.pallas import tpu as pltpu
from jax.sharding import Mesh
from jax.sharding import PartitionSpec as P

HEADS = 128
KEY = ("x", "yh", "core")
FAR = ("x", "yh")
HEAD = ("yl", "z")
LOG2E = math.log2(math.e)
attn_scale = 192.0 ** (-0.5) * LOG2E
index_scale = 128.0 ** (-0.5)
masked_fill = -1e30
NT = (((1,), (1,)), ((), ()))
NN = (((1,), (0,)), ((), ()))
TN = (((0,), (0,)), ((), ()))


def dot(a, b, dims):
    return lax.dot_general(a, b, dims, preferred_element_type=jnp.float32)


def params(semantics=("arbitrary",)):
    return pltpu.CompilerParams(
        dimension_semantics=semantics, vmem_limit_bytes=48 * 1024 * 1024
    )


def score_stats_kernel(pos_ref, q_ref, k_ref, out_ref, *, tile):
    head = pl.program_id(0)
    keys = k_ref.shape[0]
    pos = pos_ref[...]
    q = q_ref[0]
    highs, sums = [], []
    for start in range(0, keys, tile):
        scores = dot(k_ref[start : start + tile, :], q, NT) * attn_scale
        ids = lax.broadcasted_iota(jnp.int32, scores.shape, 0)
        scores = jnp.where(ids <= pos - start, scores, masked_fill)
        high = jnp.max(scores, axis=0, keepdims=True)
        highs.append(high)
        sums.append(jnp.sum(jnp.exp2(scores - high), axis=0, keepdims=True))
    high = highs[0]
    for other in highs[1:]:
        high = jnp.maximum(high, other)
    total = sum(s * jnp.exp2(h - high) for h, s in zip(highs, sums))
    line = high + jnp.log2(total)
    out_ref[:, pl.ds(head, 1), :] = jnp.broadcast_to(line[None], (out_ref.shape[0], 1, line.shape[1]))


def score_stats(rel_pos, q, k, copies):
    heads, rows, width = q.shape
    keys = k.shape[0]
    return pl.pallas_call(
        lambda *refs: score_stats_kernel(*refs, tile=512),
        grid=(heads,),
        in_specs=[
            pl.BlockSpec((1, rows), lambda h: (0, 0)),
            pl.BlockSpec((1, rows, width), lambda h: (h, 0, 0)),
            pl.BlockSpec((keys, width), lambda h: (0, 0)),
        ],
        out_specs=pl.BlockSpec((copies, heads, rows), lambda h: (0, 0, 0)),
        out_shape=jax.ShapeDtypeStruct((copies, heads, rows), jnp.float32),
        compiler_params=params(),
        cost_estimate=pl.CostEstimate(
            flops=2 * heads * rows * keys * width, transcendentals=heads * rows * keys, bytes_accessed=6 << 20
        ),
        name="score_stats",
    )(rel_pos.reshape(1, rows), q, k)


def head_share_kernel(stats_ref, pos_ref, q_ref, k_ref, out_ref, col_ref):
    heads = q_ref.shape[0]
    tile = k_ref.shape[0]
    step = pl.program_id(0)

    @pl.when(step == 0)
    def _():
        stats = stats_ref[...]
        high = jnp.max(stats, axis=0)
        total = jnp.sum(jnp.exp2(stats - high[None]), axis=0)
        line = high + jnp.log2(total) + math.log2(HEADS)
        col_ref[:, :heads] = jnp.transpose(line)

    k = k_ref[...]
    total = None
    for head in range(heads):
        scores = dot(q_ref[head], k, NT)
        part = jnp.exp2(scores * attn_scale - col_ref[:, head : head + 1])
        total = part if total is None else total + part
    ids = lax.broadcasted_iota(jnp.int32, total.shape, 1) + step * tile
    out_ref[...] = jnp.where(ids <= pos_ref[...], total, 0.0)


def head_share(stats, rel_pos, q, k):
    heads, rows, width = q.shape
    keys = k.shape[0]
    copies = stats.shape[0]
    tile = 256
    return pl.pallas_call(
        head_share_kernel,
        grid=(keys // tile,),
        in_specs=[
            pl.BlockSpec((copies, heads, rows), lambda t: (0, 0, 0)),
            pl.BlockSpec((rows, 1), lambda t: (0, 0)),
            pl.BlockSpec((heads, rows, width), lambda t: (0, 0, 0)),
            pl.BlockSpec((tile, width), lambda t: (t, 0)),
        ],
        out_specs=pl.BlockSpec((rows, tile), lambda t: (0, t)),
        out_shape=jax.ShapeDtypeStruct((rows, keys), jnp.float32),
        scratch_shapes=[pltpu.VMEM((rows, 128), jnp.float32)],
        compiler_params=params(),
        cost_estimate=pl.CostEstimate(
            flops=2 * heads * rows * keys * width, transcendentals=heads * rows * keys, bytes_accessed=8 << 20
        ),
        name="head_share",
    )(stats, rel_pos.reshape(rows, 1), q, k)


def index_logits_kernel(pos_ref, q_ref, w_ref, k_ref, logit_ref, stat_ref):
    rows = pos_ref.shape[0]
    iheads = q_ref.shape[0] // rows
    keys = k_ref.shape[0]
    tile = 512
    for start in range(0, keys, tile):
        k = k_ref[start : start + tile, :]
        lines = []
        for row in range(rows):
            own = slice(row * iheads, (row + 1) * iheads)
            dots = dot(q_ref[own, :], k, NT)
            lines.append(
                jnp.sum(jnp.maximum(dots, 0.0) * w_ref[own, :], axis=0, keepdims=True)
            )
        logits = jnp.concatenate(lines, axis=0) * (index_scale * LOG2E)
        ids = lax.broadcasted_iota(jnp.int32, logits.shape, 1) + start
        logit_ref[:, start : start + tile] = jnp.where(ids <= pos_ref[...], logits, masked_fill)
    logits = logit_ref[...]
    high = jnp.max(logits, axis=1, keepdims=True)
    total = jnp.sum(jnp.exp2(logits - high), axis=1, keepdims=True)
    stat_ref[...] = jnp.broadcast_to(high + jnp.log2(total), stat_ref.shape)


def index_logits(row_pos, q, w, k):
    rows, iheads, width = q.shape
    keys = k.shape[0]
    return pl.pallas_call(
        index_logits_kernel,
        out_shape=(
            jax.ShapeDtypeStruct((rows, keys), jnp.float32),
            jax.ShapeDtypeStruct((rows, 128), jnp.float32),
        ),
        compiler_params=pltpu.CompilerParams(vmem_limit_bytes=48 * 1024 * 1024),
        cost_estimate=pl.CostEstimate(
            flops=2 * rows * iheads * keys * width, transcendentals=rows * keys, bytes_accessed=1 << 20
        ),
        name="index_logits",
    )(row_pos.reshape(rows, 1), q.reshape(rows * iheads, width), w.reshape(rows * iheads, 1), k)


def gradients_kernel(parts_ref, logit_ref, stat_ref, q_ref, w_ref, k_ref, rows_ref, keys_ref, *, count):
    step = pl.program_id(0)
    rows = logit_ref.shape[0]
    iheads = q_ref.shape[0] // rows
    target = jnp.sum(parts_ref[...], axis=0)
    probs = jnp.exp2(logit_ref[...] - stat_ref[...])
    slope = (probs - target) * count
    k = k_ref[...]
    coefs = []
    for row in range(rows):
        own = slice(row * iheads, (row + 1) * iheads)
        dots = dot(q_ref[own, :], k, NT)
        coef = jnp.where(dots > 0, slope[row : row + 1, :] * w_ref[own, :] * index_scale, 0.0)
        coefs.append(coef.astype(jnp.bfloat16))
    coef = jnp.concatenate(coefs, axis=0)
    keys_ref[...] = dot(coef, q_ref[...], TN)
    part = dot(coef, k, NN)

    @pl.when(step == 0)
    def _():
        rows_ref[...] = part

    @pl.when(step > 0)
    def _():
        rows_ref[...] += part


def gradients(parts, logits, stat, q, w, k, count):
    rows, iheads, width = q.shape
    keys = k.shape[0]
    tile = 512
    flat = rows * iheads
    return pl.pallas_call(
        lambda *refs: gradients_kernel(*refs, count=float(count)),
        grid=(keys // tile,),
        in_specs=[
            pl.BlockSpec((parts.shape[0], rows, tile), lambda t: (0, 0, t)),
            pl.BlockSpec((rows, tile), lambda t: (0, t)),
            pl.BlockSpec((rows, 1), lambda t: (0, 0)),
            pl.BlockSpec((flat, width), lambda t: (0, 0)),
            pl.BlockSpec((flat, 1), lambda t: (0, 0)),
            pl.BlockSpec((tile, width), lambda t: (t, 0)),
        ],
        out_specs=(
            pl.BlockSpec((flat, width), lambda t: (0, 0)),
            pl.BlockSpec((tile, width), lambda t: (t, 0)),
        ),
        out_shape=(
            jax.ShapeDtypeStruct((flat, width), jnp.float32),
            jax.ShapeDtypeStruct((keys, width), jnp.float32),
        ),
        compiler_params=params(),
        cost_estimate=pl.CostEstimate(
            flops=6 * flat * keys * width, transcendentals=rows * keys, bytes_accessed=4 << 20
        ),
        name="gradients",
    )(parts, logits, stat, q.reshape(flat, width), w.reshape(flat, 1), k)


def exchanged(parts, axis):
    return lax.all_to_all(parts, axis, split_axis=0, concat_axis=0, tiled=True)


def spread(shard, axis):
    size = lax.axis_size(axis)
    return exchanged(jnp.broadcast_to(shard[None], (size, *shard.shape)), axis)


def summed(shard, axis):
    size = lax.axis_size(axis)
    return exchanged(shard.reshape(size, -1, shard.shape[-1]), axis).sum(axis=0)


def shards(query_pos, mla_query, latent_keys, index_query, index_keys, index_weights):
    keys = latent_keys.shape[0]
    rows = index_query.shape[0]
    heads_axis = lax.axis_size(HEAD)
    rel_pos = query_pos - lax.axis_index(KEY) * keys
    row_pos = lax.dynamic_slice_in_dim(rel_pos, lax.axis_index(HEAD) * rows, rows, 0)
    own_stats = score_stats(rel_pos, mla_query, latent_keys, lax.axis_size(KEY))
    all_stats = exchanged(own_stats, KEY)
    logits, row_stat = index_logits(row_pos, index_query, index_weights, index_keys)
    share = head_share(all_stats, rel_pos, mla_query, latent_keys)
    parts = exchanged(share.reshape(heads_axis, rows, keys), HEAD)
    row_stats = spread(row_stat[:, 0].reshape(1, rows), KEY)
    high = jnp.max(row_stats, axis=0)
    row_total = high + jnp.log2(jnp.sum(jnp.exp2(row_stats - high), axis=0))
    grad_rows, grad_keys = gradients(
        parts, logits, row_total.reshape(rows, 1), index_query, index_weights, index_keys,
        lax.axis_size(KEY) * keys,
    )
    key_grads = summed(grad_keys, HEAD)
    mine = summed(summed(grad_rows, "core"), FAR)
    near = spread(mine, FAR).reshape(-1, mine.shape[-1])
    query_grads = spread(near, "core").reshape(index_query.shape)
    return (query_grads, key_grads)


def solution(mesh):
    finer = Mesh(mesh.devices.reshape(2, 8, 4, 4, 2), ("yl", "z", "x", "yh", "core"))
    return jax.shard_map(
        shards,
        mesh=finer,
        in_specs=(
            P(),
            P(HEAD, None, None),
            P(KEY, None),
            P(HEAD, None, None),
            P(KEY, None),
            P(HEAD, None),
        ),
        out_specs=(P(HEAD, None, None), P(KEY + HEAD, None)),
        check_vma=False,
    )
```

time: 217 us -> 214 us (0.986)
  the two profiles are of different devices: /device:TPU:8 before, /device:TPU:72 now
where the time goes in v1:
time: 214 us; the launch traced here: 213 us
  waiting for transfers between devices  85.3 us (40%)
  blocking collectives  47.4 us (22%)
  Pallas kernels  32 us (15%)
  starting transfers between devices  30.4 us (14%)
  local copies, waits for them, and re-layouts  16.7 us (8%)
    all_to_all x4, waiting for transfers between devices, exchanged(): return lax.all_to_all(parts, axis, split_axis=0, concat_axis=0, tiled=True)  85.3 us
    all_to_all x4, blocking collectives, exchanged(): return lax.all_to_all(parts, axis, split_axis=0, concat_axis=0, tiled=True)  47.4 us
    all_to_all x4, starting transfers between devices, exchanged(): return lax.all_to_all(parts, axis, split_axis=0, concat_axis=0, tiled=True)  30.4 us
    unnamed x23, local copies, waits for them, and re-layouts  15 us
    pallas_call x1, Pallas kernels, score_stats(): pl.pallas_call(lambda *refs: score_stats_kernel(*refs, tile=512), grid=(h...  11.6 us
    pallas_call x1, Pallas kernels, head_share(): pl.pallas_call(head_share_kernel, grid=(keys // tile,), in_specs=[pl.Bloc...  9.87 us
    pallas_call x1, Pallas kernels, gradients(): pl.pallas_call(lambda *refs: gradients_kernel(*refs, count=float(count)),...  7.29 us
  transfers between devices with their start and end apart: 4, of which 3 were waited for; matrix products, arithmetic and copies ran while one was open for 1% of the time, Pallas kernels for 6%

profile of v1, /device:TPU:72, one launch (start us, length us, event | category | flops | bytes accessed | tf_op | source)
XLA Modules:
  0.0 213.5 jit_solution(7635388841908615243)
XLA Ops:
  0.6 3.1 %copy.44.refs_1_.q_ref = bf16[8,256,576]{2,1,0:T(8,128)(2,1)S(1)} copy(bf16[8,256,576]{1,2,0:T(8,128)(2,1)} %param.7) | data formatting | bytes 4718592 | tf_op args[1]
  3.7 4.3 %copy.45.refs_2_.k_ref = bf16[2048,576]{1,0:T(8,128)(2,1)} copy(bf16[2048,576]{0,1:T(8,128)(2,1)} %param.8) | data formatting | bytes 4718592 | tf_op args[2]
  8.1 1.7 copy-done
  9.8 11.6 %score_stats.1 = f32[32,8,256]{2,1,0:T(8,128)} custom-call(s32[1,256]{1,0:T(1,128)S(1)} %bitcast.15, bf16[8,256,576]{2,1,0:T(8,128)(2,1)S(1)} %copy.44.refs_1_.q_ref, bf16[2048,576]{1,0:T(8,128)(2,1)S(1)} %copy-done), custom_call_target="tpu_custom_call" | custom-call | flops 4831838208 | bytes 6291456 | tf_op jit(solution)/shard_map/score_stats/pallas_call | solution.py:58
  21.5 9.1 %all-to-all-start = ((f32[32,8,256]{2,1,0:T(8,128)}), f32[32,8,256]{2,1,0:T(8,128)S(1)}, u32[]{:S(2)}, u32[]{:S(2)}) async-start(f32[32,8,256]{2,1,0:T(8,128)} %score_stats.1), calls=%async_computation | async-start | bytes 524288 | tf_op jit(solution)/shard_map/all_to_all | solution.py:224
  31.3 1.0 copy-done.2
  32.4 0.9 copy-done.4
  33.3 3.2 %index_logits.1 = (f32[16,2048]{1,0:T(8,128)S(1)}, f32[16,128]{1,0:T(8,128)S(1)}) custom-call(s32[16,1]{1,0:T(8,128)S(1)} %copy.49.pos_ref, bf16[1024,128]{1,0:T(8,128)(2,1)S(1)} %bitcast.17, f32[1024,1]{1,0:T(8,128)S(1)} %reshape.86.w_ref.refs_4_, bf16[2048,128]{1,0:T(8,128)(2,1)S(1)} %copy-done.2), custom_call_target="tpu_custom_call" | custom-call | flops 536870912 | bytes 1048576 | tf_op jit(solution)/shard_map/index_logits/pallas_call | solution.py:150
  37.3 6.0 %all-to-all-done.stats_ref = f32[32,8,256]{2,1,0:T(8,128)S(1)} async-done(((f32[32,8,256]{2,1,0:T(8,128)}), f32[32,8,256]{2,1,0:T(8,128)S(1)}, u32[]{:S(2)}, u32[]{:S(2)}) %all-to-all-start) | async-done | bytes 262176 | tf_op jit(solution)/shard_map/all_to_all | solution.py:224
  44.0 4.2 %all-to-all-start.2 = ((f32[32,1,16]{2,1,0:T(1,128)}), f32[32,1,16]{2,1,0:T(1,128)S(1)}, u32[]{:S(2)}, u32[]{:S(2)}) async-start(f32[32,1,16]{2,1,0:T(1,128)} %broadcast_in_dim.22), calls=%async_computation.2 | async-start | bytes 32768 | tf_op jit(solution)/shard_map/all_to_all | solution.py:224
  48.2 9.9 %head_share.1 = f32[256,2048]{1,0:T(8,128)S(1)} custom-call(f32[32,8,256]{2,1,0:T(8,128)S(1)} %all-to-all-done.stats_ref, s32[256,1]{1,0:T(8,128)S(1)} %copy.46.pos_ref, bf16[8,256,576]{2,1,0:T(8,128)(2,1)S(1)} %copy.44.refs_1_.q_ref, bf16[2048,576]{1,0:T(8,128)(2,1)} %copy.45.refs_2_.k_ref), custom_call_target="tpu_custom_call" | custom-call | flops 4831838208 | bytes 8388608 | tf_op jit(solution)/shard_map/head_share/pallas_call | solution.py:104
  58.1 1.3 copy-done.1
  59.4 11.3 %all-to-all-start.1 = ((f32[16,16,2048]{2,1,0:T(8,128)}), f32[16,16,2048]{2,1,0:T(8,128)S(1)}, u32[]{:S(2)}, u32[]{:S(2)}) async-start(f32[16,16,2048]{2,1,0:T(8,128)} %bitcast.13), calls=%async_computation.1 | async-start | bytes 4194304 | tf_op jit(solution)/shard_map/all_to_all | solution.py:224
  71.1 51.8 %all-to-all-done.1.refs_0_ = f32[16,16,2048]{2,1,0:T(8,128)S(1)} async-done(((f32[16,16,2048]{2,1,0:T(8,128)}), f32[16,16,2048]{2,1,0:T(8,128)S(1)}, u32[]{:S(2)}, u32[]{:S(2)}) %all-to-all-start.1) | async-done | bytes 2097184 | tf_op jit(solution)/shard_map/all_to_all | solution.py:224
  122.9 1.0 copy-done.3
  123.9 7.3 %gradients.1 = (f32[1024,128]{1,0:T(8,128)S(1)}, f32[2048,128]{1,0:T(8,128)}) custom-call(f32[16,16,2048]{2,1,0:T(8,128)S(1)} %all-to-all-done.1.refs_0_, f32[16,2048]{1,0:T(8,128)S(1)} %copy-done.7, f32[16,1]{1,0:T(8,128)S(1)} %copy.53.refs_2_, bf16[1024,128]{1,0:T(8,128)(2,1)S(1)} %bitcast.18, f32[1024,1]{1,0:T(8,128)S(1)} %reshape.86.w_ref.refs_4_, ...), custom_call_target="tpu_custom_call" | custom-call | flops 1610612736 | bytes 4194304 | tf_op jit(solution)/shard_map/gradients/pallas_call | solution.py:196
  131.2 4.1 %all_to_all.40 = f32[2,512,128]{2,1,0:T(8,128)S(1)} all-to-all(f32[2,512,128]{2,1,0:T(8,128)S(1)} %bitcast.14), channel_id=1, replica_groups=mesh['yl'=2,'z'=8,'x'=4,'yh'=4,'core'=2] {'core'}, dimensions={0} | all-to-all | bytes 1048576 | tf_op jit(solution)/shard_map/all_to_all | solution.py:224
  135.4 22.7 %all_to_all.41 = f32[16,32,128]{2,1,0:T(8,128)S(1)} all-to-all(f32[16,32,128]{2,1,0:T(8,128)S(1)} %bitcast.21), channel_id=1, replica_groups=mesh['yl'=2,'z'=8,'x'=4,'yh'=4,'core'=2] {'x','yh'}, dimensions={0} | all-to-all | bytes 524288 | tf_op jit(solution)/shard_map/all_to_all | solution.py:224
  158.2 16.4 %all_to_all.42 = f32[16,32,128]{2,1,0:T(8,128)S(1)} all-to-all(f32[16,32,128]{2,1,0:T(8,128)S(1)} %broadcast_in_dim.23), channel_id=1, replica_groups=mesh['yl'=2,'z'=8,'x'=4,'yh'=4,'core'=2] {'x','yh'}, dimensions={0} | all-to-all | bytes 524288 | tf_op jit(solution)/shard_map/all_to_all | solution.py:224
  174.6 4.2 %all_to_all.43 = f32[2,512,128]{2,1,0:T(8,128)S(1)} all-to-all(f32[2,512,128]{2,1,0:T(8,128)S(1)} %broadcast_in_dim.25), channel_id=1, replica_groups=mesh['yl'=2,'z'=8,'x'=4,'yh'=4,'core'=2] {'core'}, dimensions={0} | all-to-all | bytes 1048576 | tf_op jit(solution)/shard_map/all_to_all | solution.py:224
  178.7 5.9 %all-to-all-start.7 = ((f32[16,128,128]{2,1,0:T(8,128)}), f32[16,128,128]{2,1,0:T(8,128)S(1)}, u32[]{:S(2)}, u32[]{:S(2)}) async-start(f32[16,128,128]{2,1,0:T(8,128)} %bitcast.10), calls=%async_computation.7 | async-start | bytes 2097152 | tf_op jit(solution)/shard_map/all_to_all | solution.py:224
  184.6 27.4 %all-to-all-done.7 = f32[16,128,128]{2,1,0:T(8,128)S(1)} async-done(((f32[16,128,128]{2,1,0:T(8,128)}), f32[16,128,128]{2,1,0:T(8,128)S(1)}, u32[]{:S(2)}, u32[]{:S(2)}) %all-to-all-start.7) | async-done | bytes 1048608 | tf_op jit(solution)/shard_map/all_to_all | solution.py:224
  212.0 0.7 reduce_sum.39
  212.7 0.8 copy.57
  (32 shorter events, 2.7 us)
Async XLA Ops:
  3.7 4.3 %copy-start.9 = (s32[256]{0:T(256)S(1)}, s32[256]{0:T(256)}, u32[]{:S(2)}) copy-start(s32[256]{0:T(256)} %param.6) | copy-start | bytes 3076
  8.1 1.7 copy-start
  9.8 21.0 %copy-start.8 = (f32[16,64]{1,0:T(8,128)S(1)}, f32[16,64]{1,0:T(8,128)}, u32[]{:S(2)}) copy-start(f32[16,64]{1,0:T(8,128)} %param.11) | copy-start | bytes 12292
  21.5 21.9 %all-to-all-start = ((f32[32,8,256]{2,1,0:T(8,128)}), f32[32,8,256]{2,1,0:T(8,128)S(1)}, u32[]{:S(2)}, u32[]{:S(2)}) async-start(f32[32,8,256]{2,1,0:T(8,128)} %score_stats.1), calls=%async_computation | async-start | bytes 524288 | tf_op jit(solution)/shard_map/all_to_all | solution.py:224
  31.3 1.0 copy-start.2
  32.4 0.9 copy-start.4
  36.5 0.7 copy-start.6
  44.0 15.4 %all-to-all-start.2 = ((f32[32,1,16]{2,1,0:T(1,128)}), f32[32,1,16]{2,1,0:T(1,128)S(1)}, u32[]{:S(2)}, u32[]{:S(2)}) async-start(f32[32,1,16]{2,1,0:T(1,128)} %broadcast_in_dim.22), calls=%async_computation.2 | async-start | bytes 32768 | tf_op jit(solution)/shard_map/all_to_all | solution.py:224
  58.0 1.3 copy-start.1
  59.4 63.5 %copy-start.5 = (bf16[16,64,128]{2,1,0:T(8,128)(2,1)S(1)}, bf16[16,64,128]{2,1,0:T(8,128)(2,1)}, u32[]{:S(2)}) copy-start(bf16[16,64,128]{2,1,0:T(8,128)(2,1)} %param.9) | copy-start | bytes 786436
  59.4 63.5 %copy-start.7 = (f32[16,2048]{1,0:T(8,128)S(1)}, f32[16,2048]{1,0:T(8,128)}, u32[]{:S(2)}) copy-start(f32[16,2048]{1,0:T(8,128)} %copy-done.6) | copy-start | bytes 393220
  59.4 63.5 %all-to-all-start.1 = ((f32[16,16,2048]{2,1,0:T(8,128)}), f32[16,16,2048]{2,1,0:T(8,128)S(1)}, u32[]{:S(2)}, u32[]{:S(2)}) async-start(f32[16,16,2048]{2,1,0:T(8,128)} %bitcast.13), calls=%async_computation.1 | async-start | bytes 4194304 | tf_op jit(solution)/shard_map/all_to_all | solution.py:224
  122.9 1.0 copy-start.3
  178.7 33.3 %all-to-all-start.7 = ((f32[16,128,128]{2,1,0:T(8,128)}), f32[16,128,128]{2,1,0:T(8,128)S(1)}, u32[]{:S(2)}, u32[]{:S(2)}) async-start(f32[16,128,128]{2,1,0:T(8,128)} %bitcast.10), calls=%async_computation.7 | async-start | bytes 2097152 | tf_op jit(solution)/shard_map/all_to_all | solution.py:224

commit v2 on v1

v2 whole, which is shorter than its diff:
```python
import functools
import math

import jax
import jax.numpy as jnp
from jax import lax
from jax.experimental import pallas as pl
from jax.experimental.pallas import tpu as pltpu
from jax.sharding import Mesh
from jax.sharding import PartitionSpec as P

HEADS = 128
LANES = 128
KEY = ("x", "yh", "core")
HEAD = ("yl", "zh", "zl")
RING = ("zh", "zl")
SIDE = ("x", "core")
LOG2E = math.log2(math.e)
attn_scale = 192.0 ** (-0.5) * LOG2E
index_scale = 128.0 ** (-0.5)
masked_fill = -1e30
NT = (((1,), (1,)), ((), ()))
NN = (((1,), (0,)), ((), ()))
TN = (((0,), (0,)), ((), ()))


def dot(a, b, dims):
    return lax.dot_general(a, b, dims, preferred_element_type=jnp.float32)


def params(semantics=("arbitrary",)):
    return pltpu.CompilerParams(
        dimension_semantics=semantics, vmem_limit_bytes=48 * 1024 * 1024
    )


def score_stats_kernel(pos_ref, q_ref, k_ref, out_ref, rows_ref, col_ref, *, tile):
    head = pl.program_id(0)
    heads = pl.num_programs(0)
    keys = k_ref.shape[1]
    q = jnp.transpose(q_ref[0])
    rows_ref[0] = q
    rows = q.shape[0]
    pos = jnp.broadcast_to(pos_ref[...], (rows, LANES))
    ids = lax.broadcasted_iota(jnp.int32, (rows, LANES), 1)
    highs, sums = [], []
    for start in range(0, keys, tile):
        scores = dot(q, k_ref[:, start : start + tile], NN)
        lines = [
            jnp.where(
                ids + (start + at) <= pos, scores[:, at : at + LANES] * attn_scale, masked_fill
            )
            for at in range(0, tile, LANES)
        ]
        high = functools.reduce(jnp.maximum, lines)
        highs.append(high)
        sums.append(sum(jnp.exp2(line - high) for line in lines))
    high = functools.reduce(jnp.maximum, highs)
    total = sum(s * jnp.exp2(h - high) for h, s in zip(highs, sums))
    most = jnp.max(high, axis=1, keepdims=True)
    total = jnp.sum(total * jnp.exp2(high - most), axis=1, keepdims=True)
    line = most + jnp.log2(total)
    col_ref[...] = jnp.where(ids == head, line, col_ref[...])

    @pl.when(head == heads - 1)
    def _():
        for at in range(0, rows, LANES):
            out_ref[at // LANES] = jnp.transpose(col_ref[at : at + LANES, :])[: out_ref.shape[1], :]


def score_stats(rel_pos, q, k):
    heads, width, rows = q.shape
    keys = k.shape[1]
    return pl.pallas_call(
        functools.partial(score_stats_kernel, tile=512),
        grid=(heads,),
        in_specs=[
            pl.BlockSpec((rows, 1), lambda h: (0, 0)),
            pl.BlockSpec((1, width, rows), lambda h: (h, 0, 0)),
            pl.BlockSpec((width, keys), lambda h: (0, 0)),
        ],
        out_specs=(
            pl.BlockSpec((rows // LANES, heads, LANES), lambda h: (0, 0, 0)),
            pl.BlockSpec((1, rows, width), lambda h: (h, 0, 0)),
        ),
        out_shape=(
            jax.ShapeDtypeStruct((rows // LANES, heads, LANES), jnp.float32),
            jax.ShapeDtypeStruct((heads, rows, width), q.dtype),
        ),
        scratch_shapes=[pltpu.VMEM((rows, LANES), jnp.float32)],
        compiler_params=params(),
        cost_estimate=pl.CostEstimate(
            flops=2 * heads * rows * keys * width, transcendentals=heads * rows * keys, bytes_accessed=6 << 20
        ),
        name="score_stats",
    )(rel_pos.reshape(rows, 1), q, k)


def combined(stats):
    high = jnp.max(stats, axis=0)
    return high + jnp.log2(jnp.sum(jnp.exp2(stats - high[None]), axis=0))


def head_share_kernel(half_ref, stats_ref, pos_ref, q_ref, k_ref, out_ref, col_ref):
    heads, rows, _ = q_ref.shape
    tile = k_ref.shape[1]
    step = pl.program_id(0)

    @pl.when(step == 0)
    def _():
        line = combined(stats_ref[...]) + math.log2(HEADS)
        lines = [line[:, head * rows : (head + 1) * rows] for head in range(heads)]
        col_ref[:, :heads] = jnp.transpose(jnp.concatenate(lines, axis=0))

    k = k_ref[...]
    total = None
    for head in range(heads):
        scores = dot(q_ref[head], k, NN)
        part = jnp.exp2(scores * attn_scale - col_ref[:, head : head + 1])
        total = part if total is None else total + part
    start = (half_ref[1] * pl.num_programs(0) + step) * tile
    ids = lax.broadcasted_iota(jnp.int32, total.shape, 1) + start
    out_ref[...] = jnp.where(ids <= pos_ref[...], total, 0.0)


def head_share(half, stats, rel_pos, q, k):
    heads, rows, width = q.shape
    rows //= 2
    keys = k.shape[1] // 2
    tile = 256
    steps = keys // tile
    return pl.pallas_call(
        head_share_kernel,
        grid_spec=pltpu.PrefetchScalarGridSpec(
            num_scalar_prefetch=1,
            grid=(steps,),
            in_specs=[
                pl.BlockSpec((stats.shape[0], 1, heads * rows), lambda t, half: (0, 0, half[0])),
                pl.BlockSpec((rows, 1), lambda t, half: (half[0], 0)),
                pl.BlockSpec((heads, rows, width), lambda t, half: (0, half[0], 0)),
                pl.BlockSpec((width, tile), lambda t, half: (0, half[1] * steps + t)),
            ],
            out_specs=pl.BlockSpec((rows, tile), lambda t, half: (0, t)),
            scratch_shapes=[pltpu.VMEM((rows, LANES), jnp.float32)],
        ),
        out_shape=jax.ShapeDtypeStruct((rows, keys), jnp.float32),
        compiler_params=params(),
        cost_estimate=pl.CostEstimate(
            flops=2 * heads * rows * keys * width, transcendentals=heads * rows * keys, bytes_accessed=3 << 20
        ),
        name="head_share",
    )(half, stats, rel_pos.reshape(2 * rows, 1), q, k)


def diagonal(rows):
    shape = (rows, LANES)
    return lax.broadcasted_iota(jnp.int32, shape, 0) == lax.broadcasted_iota(jnp.int32, shape, 1)


def index_logits_kernel(pos_ref, q_ref, w_ref, k_ref, own_ref, logit_ref, stat_ref):
    rows = pos_ref.shape[0]
    iheads = q_ref.shape[0] // rows
    keys = k_ref.shape[0]
    tile = 512
    w = jnp.transpose(w_ref[...])
    for start in range(0, keys, tile):
        k = k_ref[start : start + tile, :]
        lines = []
        for row in range(rows):
            own = slice(row * iheads, (row + 1) * iheads)
            dots = dot(q_ref[own, :], k, NT)
            lines.append(
                jnp.sum(jnp.maximum(dots, 0.0) * w[:, row : row + 1], axis=0, keepdims=True)
            )
        logits = jnp.concatenate(lines, axis=0) * (index_scale * LOG2E)
        ids = lax.broadcasted_iota(jnp.int32, logits.shape, 1) + start
        logit_ref[:, start : start + tile] = jnp.where(ids <= pos_ref[...], logits, masked_fill)
    logits = logit_ref[...]
    high = jnp.max(logits, axis=1, keepdims=True)
    total = jnp.sum(jnp.exp2(logits - high), axis=1, keepdims=True)
    line = jnp.where(diagonal(rows), high + jnp.log2(total), 0.0)
    line = jnp.sum(line, axis=0, keepdims=True)
    groups, heads, _ = own_ref.shape
    copies = stat_ref.shape[0]
    lines = [own_ref[group, head : head + 1, :] for group in range(groups) for head in range(heads)]
    for at, part in enumerate(lines + [line]):
        stat_ref[:, :, at * LANES : (at + 1) * LANES] = jnp.broadcast_to(
            part[None], (copies, 1, LANES)
        )


def index_logits(row_pos, q, w, k, own, copies):
    rows, iheads, width = q.shape
    keys = k.shape[0]
    return pl.pallas_call(
        index_logits_kernel,
        out_shape=(
            jax.ShapeDtypeStruct((rows, keys), jnp.float32),
            jax.ShapeDtypeStruct((copies, 1, own.size + LANES), jnp.float32),
        ),
        compiler_params=pltpu.CompilerParams(vmem_limit_bytes=48 * 1024 * 1024),
        cost_estimate=pl.CostEstimate(
            flops=2 * rows * iheads * keys * width, transcendentals=rows * keys, bytes_accessed=1 << 20
        ),
        name="index_logits",
    )(row_pos.reshape(rows, 1), q.reshape(rows * iheads, width), w, k, own)


def gradients_kernel(
    half_ref, parts_ref, logit_ref, stat_ref, q_ref, w_ref, k_ref, before_ref, rows_ref, keys_ref, total_ref, w_col_ref, *, count
):
    step = pl.program_id(0)
    rows = logit_ref.shape[0]
    iheads = q_ref.shape[0] // rows

    @pl.when(step == 0)
    def _():
        line = combined(stat_ref[...])
        total_ref[...] = jnp.sum(jnp.where(diagonal(rows), line, 0.0), axis=1, keepdims=True)
        w_col_ref[...] = jnp.transpose(w_ref[...])

    target = jnp.sum(parts_ref[...], axis=0)
    probs = jnp.exp2(logit_ref[...] - total_ref[...])
    slope = (probs - target) * count
    k = k_ref[...]
    w = w_col_ref[...]
    coefs = []
    for row in range(rows):
        own = slice(row * iheads, (row + 1) * iheads)
        dots = dot(q_ref[own, :], k, NT)
        coef = jnp.where(dots > 0, slope[row : row + 1, :] * w[:, row : row + 1] * index_scale, 0.0)
        coefs.append(coef.astype(jnp.bfloat16))
    coef = jnp.concatenate(coefs, axis=0)
    grad_keys = dot(coef, q_ref[...], TN)
    near, far, share, _ = keys_ref.shape
    for other in range(far):
        for side in range(near):
            at = (other * near + side) * share
            keys_ref[side, other] = grad_keys[at : at + share, :]
    part = dot(coef, k, NN)

    @pl.when(step == 0)
    def _():
        rows_ref[...] = part if before_ref is None else before_ref[...] + part

    @pl.when(step > 0)
    def _():
        rows_ref[...] += part


def gradients(half, parts, logits, stats, q, w, k, before, count, sizes):
    rows, iheads, width = q.shape
    keys = parts.shape[2]
    flat = rows * iheads
    _, nf, nz = sizes
    share = keys // (nf * nz)
    far = nf // 2
    tile = far * nz * share
    last = stats.shape[2] // LANES - 1
    body = gradients_kernel
    operands = [parts, logits, stats, q.reshape(flat, width), w, k]
    in_specs = [
        pl.BlockSpec((parts.shape[0], rows, tile), lambda t, half: (0, 0, t)),
        pl.BlockSpec((rows, tile), lambda t, half: (0, half[0] * 2 + t)),
        pl.BlockSpec((stats.shape[0], 1, LANES), lambda t, half: (0, 0, last)),
        pl.BlockSpec((flat, width), lambda t, half: (0, 0)),
        pl.BlockSpec((rows, iheads), lambda t, half: (0, 0)),
        pl.BlockSpec((tile, width), lambda t, half: (half[0] * 2 + t, 0)),
    ]
    if before is None:
        body = lambda *refs, count: gradients_kernel(*refs[:7], None, *refs[7:], count=count)
    else:
        operands.append(before)
        in_specs.append(pl.BlockSpec((flat, width), lambda t, half: (0, 0)))
    return pl.pallas_call(
        functools.partial(body, count=float(count)),
        grid_spec=pltpu.PrefetchScalarGridSpec(
            num_scalar_prefetch=1,
            grid=(keys // tile,),
            in_specs=in_specs,
            out_specs=(
                pl.BlockSpec((flat, width), lambda t, half: (0, 0)),
                pl.BlockSpec((nz, far, share, width), lambda t, half: (0, t, 0, 0)),
            ),
            scratch_shapes=[pltpu.VMEM((rows, 1), jnp.float32), pltpu.VMEM((iheads, rows), jnp.float32)],
        ),
        out_shape=(
            jax.ShapeDtypeStruct((flat, width), jnp.float32),
            jax.ShapeDtypeStruct((nz, nf, share, width), jnp.float32),
        ),
        compiler_params=params(),
        cost_estimate=pl.CostEstimate(
            flops=6 * flat * keys * width, transcendentals=rows * keys, bytes_accessed=2 << 20
        ),
        name="gradients",
    )(half, *operands)


def exchanged(parts, axis):
    return lax.all_to_all(parts, axis, split_axis=0, concat_axis=0, tiled=True)


def spread(shard, axis):
    size = lax.axis_size(axis)
    return exchanged(jnp.broadcast_to(shard[None], (size, *shard.shape)), axis)


def summed(shard, axis):
    size = lax.axis_size(axis)
    parts = exchanged(shard.reshape(size, -1, shard.shape[-1]), axis)
    return parts.sum(axis=0)


def at_owner(parts, axis):
    size = lax.axis_size(axis)
    own = lax.axis_index(axis)
    total = lax.dynamic_index_in_dim(parts, own, 0, keepdims=False)
    got = []
    for hop in range(1, size):
        part = lax.dynamic_index_in_dim(parts, own ^ hop, 0, keepdims=False)
        got.append(lax.ppermute(part, axis, [(i, i ^ hop) for i in range(size)]))
    return sum(got, total)


def shards(query_pos, mla_query, latent_keys, index_query, index_keys, index_weights):
    keys = latent_keys.shape[0]
    rows = index_query.shape[0]
    rel_pos = query_pos - lax.axis_index(KEY) * keys
    row_pos = lax.dynamic_slice_in_dim(rel_pos, lax.axis_index(HEAD) * rows, rows, 0)
    q = jnp.swapaxes(mla_query, 1, 2)
    k = jnp.swapaxes(latent_keys, 0, 1)
    sizes = [lax.axis_size(axis) for axis in HEAD]
    own_stats, q_rows = score_stats(rel_pos, q, k)
    logits, own_stats = index_logits(
        row_pos, index_query, index_weights, index_keys, own_stats, lax.axis_size(KEY)
    )
    stats = exchanged(own_stats, KEY)
    mine = lax.axis_index("yl")
    other = 1 - mine
    swap = [(0, 1), (1, 0)]

    def pick(*halves):
        return jnp.stack(halves).astype(jnp.int32)

    grad_rows, grad_keys = None, []
    shares = {}
    for name, rows_half, halves in (("sent", other, (mine, other)), ("kept", mine, (other, mine))):
        for turn, half in enumerate(halves):
            shares[name, turn] = head_share(pick(rows_half, half), stats, rel_pos, q_rows, k)
    for turn, half in enumerate((other, mine)):
        near = lax.ppermute(shares["sent", turn], "yl", swap)
        near = (near + shares["kept", turn]).reshape(-1, rows, keys // 2)
        parts = exchanged(near, RING)
        grad_rows, part = gradients(
            pick(half), parts, logits, stats, index_query, index_weights, index_keys, grad_rows,
            lax.axis_size(KEY) * keys, sizes,
        )
        grad_keys.append(part)
    near = lax.ppermute(grad_keys[0], "yl", swap)
    near = near + grad_keys[1]
    near = at_owner(near, "zl")
    key_grads = at_owner(near, "zh")
    total = summed(grad_rows, SIDE)
    total = spread(total, "yh").sum(axis=0)
    query_grads = spread(total, SIDE).reshape(index_query.shape)
    return (query_grads, key_grads)


def solution(mesh):
    finer = Mesh(mesh.devices.reshape(2, 4, 2, 4, 4, 2), HEAD + KEY)
    return jax.shard_map(
        shards,
        mesh=finer,
        in_specs=(
            P(),
            P(HEAD, None, None),
            P(KEY, None),
            P(HEAD, None, None),
            P(KEY, None),
            P(HEAD, None),
        ),
        out_specs=(P(HEAD, None, None), P(KEY + HEAD, None)),
        check_vma=False,
    )
```

time: 214 us -> 181 us (0.85)
  the two profiles are of different devices: /device:TPU:72 before, /device:TPU:1 now
where the time goes in v2:
time: 181 us; the launch traced here: 180 us
  starting transfers between devices  57.9 us (32%)
  waiting for transfers between devices  47.8 us (26%)
  Pallas kernels  37.7 us (21%)
  blocking collectives  17.5 us (10%)
  local copies, waits for them, and re-layouts  13.8 us (8%)
  other arithmetic  3.93 us (2%)
    all_to_all x5, starting transfers between devices, exchanged(): return lax.all_to_all(parts, axis, split_axis=0, concat_axis=0, tiled=True)  37.2 us
    all_to_all x5, waiting for transfers between devices, exchanged(): return lax.all_to_all(parts, axis, split_axis=0, concat_axis=0, tiled=True)  27 us
    all_to_all x1, blocking collectives, exchanged(): return lax.all_to_all(parts, axis, split_axis=0, concat_axis=0, tiled=True)  17.5 us
    ppermute x2, waiting for transfers between devices, shards(): near = lax.ppermute(shares['sent', turn], 'yl', swap)  16.3 us
    pallas_call x4, Pallas kernels, head_share(): pl.pallas_call(head_share_kernel, grid_spec=pltpu.PrefetchScalarGridSpec(...  15 us
    ppermute x4, starting transfers between devices, at_owner(): got.append(lax.ppermute(part, axis, [(i, i ^ hop) for i in range(size)]))  13.6 us
    unnamed x39, local copies, waits for them, and re-layouts  11.9 us
    pallas_call x1, Pallas kernels, score_stats(): pl.pallas_call(functools.partial(score_stats_kernel, tile=512), grid=(hea...  11.8 us
  transfers between devices with their start and end apart: 12, of which 6 were waited for; matrix products, arithmetic and copies ran while one was open for 2% of the time, Pallas kernels for 10%

profile of v2, /device:TPU:1, one launch (start us, length us, event | category | flops | bytes accessed | tf_op | source)
XLA Modules:
  0.0 179.6 jit_solution(954713017255822472)
XLA Ops:
  5.0 11.8 %score_stats.1 = (f32[2,8,128]{2,1,0:T(8,128)S(1)}, bf16[8,256,576]{2,1,0:T(8,128)(2,1)}) custom-call(s32[256,1]{1,0:T(8,128)S(1)} %copy.15.pos_ref, bf16[8,576,256]{2,1,0:T(8,128)(2,1)S(1)} %bitcast.34, bf16[576,2048]{1,0:T(8,128)(2,1)S(1)} %bitcast.28), custom_call_target="tpu_custom_call" | custom-call | flops 4831838208 | bytes 6291456 | tf_op jit(solution)/shard_map/score_stats/pallas_call | solution.py:74
  16.8 4.0 %index_logits.1 = (f32[16,2048]{1,0:T(8,128)S(1)}, f32[32,1,2176]{2,1,0:T(1,128)}) custom-call(s32[16,1]{1,0:T(8,128)S(1)} %copy.16.pos_ref, bf16[1024,128]{1,0:T(8,128)(2,1)S(1)} %bitcast.35, f32[16,64]{1,0:T(8,128)S(1)} %copy-done.12, bf16[2048,128]{1,0:T(8,128)(2,1)S(1)} %copy-done.7, f32[2,8,128]{2,1,0:T(8,128)S(1)} %get-tuple-element.10.own_ref), custom_call_target="tpu_custom_call" | custom-call | flops 536870912 | bytes 1048576 | tf_op jit(solution)/shard_map/index_logits/pallas_call | solution.py:195
  21.4 11.2 %all-to-all-start = ((f32[32,1,2176]{2,1,0:T(1,128)}), f32[32,1,2176]{2,1,0:T(1,128)S(1)}, u32[]{:S(2)}, u32[]{:S(2)}) async-start(f32[32,1,2176]{2,1,0:T(1,128)} %get-tuple-element.11), calls=%async_computation | async-start | bytes 557056 | tf_op jit(solution)/shard_map/all_to_all | solution.py:300
  32.7 13.4 %all-to-all-done.stats_ref.refs_3_.stat_ref = f32[32,1,2176]{2,1,0:T(1,128)S(1)} async-done(((f32[32,1,2176]{2,1,0:T(1,128)}), f32[32,1,2176]{2,1,0:T(1,128)S(1)}, u32[]{:S(2)}, u32[]{:S(2)}) %all-to-all-start) | async-done | bytes 278560 | tf_op jit(solution)/shard_map/all_to_all | solution.py:300
  47.8 3.7 %head_share.6 = f32[128,1024]{1,0:T(8,128)S(1)} custom-call(s32[2]{0:T(128)S(1)} %pad_add_fusion.2.half_ref, f32[32,1,2176]{2,1,0:T(1,128)S(1)} %all-to-all-done.stats_ref.refs_3_.stat_ref, s32[256,1]{1,0:T(8,128)S(1)} %copy.15.pos_ref, bf16[8,256,576]{2,1,0:T(8,128)(2,1)S(1)} %copy-done, bf16[576,2048]{1,0:T(8,128)(2,1)S(1)} %bitcast.29), custom_call_target="tpu_custom_call" | custom-call | flops 1207959552 | bytes 3145728 | tf_op jit(solution)/shard_map/head_share/pallas_call | solution.py:132
  54.2 3.7 %head_share.7 = f32[128,1024]{1,0:T(8,128)S(1)} custom-call(s32[2]{0:T(128)S(1)} %get-tuple-element.21.half_ref, f32[32,1,2176]{2,1,0:T(1,128)S(1)} %all-to-all-done.stats_ref.refs_3_.stat_ref, s32[256,1]{1,0:T(8,128)S(1)} %copy.15.pos_ref, bf16[8,256,576]{2,1,0:T(8,128)(2,1)S(1)} %copy-done, bf16[576,2048]{1,0:T(8,128)(2,1)S(1)} %bitcast.30), custom_call_target="tpu_custom_call" | custom-call | flops 1207959552 | bytes 3145728 | tf_op jit(solution)/shard_map/head_share/pallas_call | solution.py:132
  57.9 8.6 %collective-permute-done.1 = f32[128,1024]{1,0:T(8,128)S(1)} collective-permute-done((f32[128,1024]{1,0:T(8,128)S(1)}, f32[128,1024]{1,0:T(8,128)S(1)}, u32[]{:S(2)}, u32[]{:S(2)}) %collective-permute-start.1) | collective-permute-done | bytes 524320 | tf_op jit(solution)/shard_map/ppermute | solution.py:351
  67.3 10.1 %all-to-all-start.2 = ((f32[8,16,1024]{2,1,0:T(8,128)}), f32[8,16,1024]{2,1,0:T(8,128)S(1)}, u32[]{:S(2)}, u32[]{:S(2)}) async-start(f32[8,16,1024]{2,1,0:T(8,128)} %bitcast.38), calls=%async_computation.2 | async-start | bytes 1048576 | tf_op jit(solution)/shard_map/all_to_all | solution.py:300
  79.1 3.7 %head_share.4 = f32[128,1024]{1,0:T(8,128)S(1)} custom-call(s32[2]{0:T(128)S(1)} %pad_add_fusion.1.half_ref, f32[32,1,2176]{2,1,0:T(1,128)S(1)} %all-to-all-done.stats_ref.refs_3_.stat_ref, s32[256,1]{1,0:T(8,128)S(1)} %copy.15.pos_ref, bf16[8,256,576]{2,1,0:T(8,128)(2,1)S(1)} %copy-done.1, bf16[576,2048]{1,0:T(8,128)(2,1)S(1)} %bitcast.31), custom_call_target="tpu_custom_call" | custom-call | flops 1207959552 | bytes 3145728 | tf_op jit(solution)/shard_map/head_share/pallas_call | solution.py:132
  82.9 2.3 %collective-permute-start = (f32[128,1024]{1,0:T(8,128)S(1)}, f32[128,1024]{1,0:T(8,128)S(1)}, u32[]{:S(2)}, u32[]{:S(2)}) collective-permute-start(f32[128,1024]{1,0:T(8,128)S(1)} %head_share.4), channel_id=1, source_target_pairs={{0,256},{256,0},{1,257},{257,1},{2,258},{258,2},{3,259},{259,3},{4... | collective-permute-start | bytes 1572872 | tf_op jit(solution)/shard_map/ppermute | solution.py:351
  85.2 3.7 %head_share.5 = f32[128,1024]{1,0:T(8,128)S(1)} custom-call(s32[2]{0:T(128)S(1)} %copy-done.5, f32[32,1,2176]{2,1,0:T(1,128)S(1)} %all-to-all-done.stats_ref.refs_3_.stat_ref, s32[256,1]{1,0:T(8,128)S(1)} %copy.15.pos_ref, bf16[8,256,576]{2,1,0:T(8,128)(2,1)S(1)} %copy-done.1, bf16[576,2048]{1,0:T(8,128)(2,1)S(1)} %bitcast.32), custom_call_target="tpu_custom_call" | custom-call | flops 1207959552 | bytes 3145728 | tf_op jit(solution)/shard_map/head_share/pallas_call | solution.py:132
  89.0 7.7 %collective-permute-done = f32[128,1024]{1,0:T(8,128)S(1)} collective-permute-done((f32[128,1024]{1,0:T(8,128)S(1)}, f32[128,1024]{1,0:T(8,128)S(1)}, u32[]{:S(2)}, u32[]{:S(2)}) %collective-permute-start) | collective-permute-done | bytes 524320 | tf_op jit(solution)/shard_map/ppermute | solution.py:351
  97.6 6.4 %all-to-all-start.1 = ((f32[8,16,1024]{2,1,0:T(8,128)}), f32[8,16,1024]{2,1,0:T(8,128)S(1)}, u32[]{:S(2)}, u32[]{:S(2)}) async-start(f32[8,16,1024]{2,1,0:T(8,128)} %bitcast.7), calls=%async_computation.1 | async-start | bytes 1048576 | tf_op jit(solution)/shard_map/all_to_all | solution.py:300
  104.0 3.5 %gradients.2 = (f32[1024,128]{1,0:T(8,128)S(1)}, f32[2,4,128,128]{3,2,1,0:T(8,128)S(1)}) custom-call(s32[1]{0:T(128)} %bitcast.1.refs_0_, f32[8,16,1024]{2,1,0:T(8,128)S(1)} %all-to-all-done.2.refs_1_, f32[16,2048]{1,0:T(8,128)S(1)} %copy-done.17, f32[32,1,2176]{2,1,0:T(1,128)S(1)} %all-to-all-done.stats_ref.refs_3_.stat_ref, ...), custom_call_target="tpu_custom_call" | custom-call | flops 805306368 | bytes 2097152 | tf_op jit(solution)/shard_map/gradients/pallas_call | solution.py:275
  108.3 2.8 %collective-permute-start.2 = (f32[2,4,128,128]{3,2,1,0:T(8,128)S(1)}, f32[2,4,128,128]{3,2,1,0:T(8,128)S(1)}, u32[]{:S(2)}, u32[]{:S(2)}) collective-permute-start(f32[2,4,128,128]{3,2,1,0:T(8,128)S(1)} %get-tuple-element.16), channel_id=1, source_target_pairs={{0,256},{256,0},{1,257},{257,1},{2,258},{258,2},{3,259},{259,3},{4... | collective-permute-start | bytes 1572872 | tf_op jit(solution)/shard_map/ppermute | solution.py:359
  111.1 7.4 %all-to-all-done.1.parts_ref = f32[8,16,1024]{2,1,0:T(8,128)S(1)} async-done(((f32[8,16,1024]{2,1,0:T(8,128)}), f32[8,16,1024]{2,1,0:T(8,128)S(1)}, u32[]{:S(2)}, u32[]{:S(2)}) %all-to-all-start.1) | async-done | bytes 524320 | tf_op jit(solution)/shard_map/all_to_all | solution.py:300
  121.4 3.5 %gradients.3 = (f32[1024,128]{1,0:T(8,128)S(1)}, f32[2,4,128,128]{3,2,1,0:T(8,128)S(1)}) custom-call(s32[1]{0:T(128)} %bitcast.half_ref, f32[8,16,1024]{2,1,0:T(8,128)S(1)} %all-to-all-done.1.parts_ref, f32[16,2048]{1,0:T(8,128)S(1)} %copy-done.18, f32[32,1,2176]{2,1,0:T(1,128)S(1)} %all-to-all-done.stats_ref.refs_3_.stat_ref, ...), custom_call_target="tpu_custom_call" | custom-call | flops 805306368 | bytes 2097152 | tf_op jit(solution)/shard_map/gradients/pallas_call | solution.py:275
  124.9 17.5 %all_to_all.30 = f32[8,128,128]{2,1,0:T(8,128)S(1)} all-to-all(f32[8,128,128]{2,1,0:T(8,128)S(1)} %bitcast.33), channel_id=1, replica_groups=mesh['yl'=2,'zh'=4,'zl'=2,'x'=4,'yh'=4,'core'=2] {'x','core'}, dimensions={0} | all-to-all | bytes 1048576 | tf_op jit(solution)/shard_map/all_to_all | solution.py:300
  143.1 3.4 %all-to-all-start.4 = ((f32[4,128,128]{2,1,0:T(8,128)}), f32[4,128,128]{2,1,0:T(8,128)S(1)}, u32[]{:S(2)}, u32[]{:S(2)}) async-start(f32[4,128,128]{2,1,0:T(8,128)} %broadcast_in_dim.4), calls=%async_computation.4 | async-start | bytes 524288 | tf_op jit(solution)/shard_map/all_to_all | solution.py:300
  148.9 6.2 %all-to-all-done.4 = f32[4,128,128]{2,1,0:T(8,128)S(1)} async-done(((f32[4,128,128]{2,1,0:T(8,128)}), f32[4,128,128]{2,1,0:T(8,128)S(1)}, u32[]{:S(2)}, u32[]{:S(2)}) %all-to-all-start.4) | async-done | bytes 262176 | tf_op jit(solution)/shard_map/all_to_all | solution.py:300
  156.0 6.2 %all-to-all-start.5 = ((f32[8,128,128]{2,1,0:T(8,128)}), f32[8,128,128]{2,1,0:T(8,128)S(1)}, u32[]{:S(2)}, u32[]{:S(2)}) async-start(f32[8,128,128]{2,1,0:T(8,128)} %broadcast_in_dim.5), calls=%async_computation.5 | async-start | bytes 1048576 | tf_op jit(solution)/shard_map/all_to_all | solution.py:300
  164.2 4.6 %collective-permute-start.5 = (f32[128,128]{1,0:T(8,128)S(1)}, f32[128,128]{1,0:T(8,128)S(1)}, u32[]{:S(2)}, u32[]{:S(2)}) collective-permute-start(f32[128,128]{1,0:T(8,128)S(1)} %get-tuple-element.20), channel_id=1, source_target_pairs={{0,128},{64,192},{128,0},{192,64},{1,129},{65,193},{129,1},{193,65... | collective-permute-start | bytes 196616 | tf_op jit(solution)/shard_map/ppermute | solution.py:321
  168.9 4.8 %collective-permute-start.4 = (f32[128,128]{1,0:T(8,128)S(1)}, f32[128,128]{1,0:T(8,128)S(1)}, u32[]{:S(2)}, u32[]{:S(2)}) collective-permute-start(f32[128,128]{1,0:T(8,128)S(1)} %get-tuple-element.18), channel_id=1, source_target_pairs={{0,64},{64,0},{128,192},{192,128},{1,65},{65,1},{129,193},{193,129... | collective-permute-start | bytes 196616 | tf_op jit(solution)/shard_map/ppermute | solution.py:321
  173.6 4.5 %collective-permute-done.4 = f32[128,128]{1,0:T(8,128)S(1)} collective-permute-done((f32[128,128]{1,0:T(8,128)S(1)}, f32[128,128]{1,0:T(8,128)S(1)}, u32[]{:S(2)}, u32[]{:S(2)}) %collective-permute-start.4) | collective-permute-done | bytes 65568 | tf_op jit(solution)/shard_map/ppermute | solution.py:321
  (66 shorter events, 23.9 us)
Async XLA Ops:
  1.6 1.7 copy-start.2
  5.0 11.8 %copy-start.7 = (bf16[2048,128]{1,0:T(8,128)(2,1)S(1)}, bf16[2048,128]{1,0:T(8,128)(2,1)}, u32[]{:S(2)}) copy-start(bf16[2048,128]{1,0:T(8,128)(2,1)} %k_ref.3) | copy-start | bytes 1572868
  5.0 11.8 %copy-start.9 = (bf16[16,64,128]{2,1,0:T(8,128)(2,1)S(1)}, bf16[16,64,128]{2,1,0:T(8,128)(2,1)}, u32[]{:S(2)}) copy-start(bf16[16,64,128]{2,1,0:T(8,128)(2,1)} %param.9) | copy-start | bytes 786436
  5.0 11.8 %copy-start.12 = (f32[16,64]{1,0:T(8,128)S(1)}, f32[16,64]{1,0:T(8,128)}, u32[]{:S(2)}) copy-start(f32[16,64]{1,0:T(8,128)} %w_ref.3) | copy-start | bytes 12292
  16.7 29.3 %copy-start.3 = (bf16[2048,576]{0,1:T(8,128)(2,1)S(1)}, bf16[2048,576]{0,1:T(8,128)(2,1)}, u32[]{:S(2)}) copy-start(bf16[2048,576]{0,1:T(8,128)(2,1)} %param.8) | copy-start | bytes 7077892
  21.4 24.7 %all-to-all-start = ((f32[32,1,2176]{2,1,0:T(1,128)}), f32[32,1,2176]{2,1,0:T(1,128)S(1)}, u32[]{:S(2)}, u32[]{:S(2)}) async-start(f32[32,1,2176]{2,1,0:T(1,128)} %get-tuple-element.11), calls=%async_computation | async-start | bytes 557056 | tf_op jit(solution)/shard_map/all_to_all | solution.py:300
  46.1 1.7 copy-start
  51.5 14.9 %collective-permute-start.1 = (f32[128,1024]{1,0:T(8,128)S(1)}, f32[128,1024]{1,0:T(8,128)S(1)}, u32[]{:S(2)}, u32[]{:S(2)}) collective-permute-start(f32[128,1024]{1,0:T(8,128)S(1)} %head_share.6), channel_id=1, source_target_pairs={{0,256},{256,0},{1,257},{257,1},{2,258},{258,2},{3,259},{259,3},{4... | collective-permute-start | bytes 1572872 | tf_op jit(solution)/shard_map/ppermute | solution.py:351
  57.9 19.6 %copy-start.1 = (bf16[8,256,576]{2,1,0:T(8,128)(2,1)S(1)}, bf16[8,256,576]{2,1,0:T(8,128)(2,1)}, u32[]{:S(2)}) copy-start(bf16[8,256,576]{2,1,0:T(8,128)(2,1)} %get-tuple-element.12.q_ref) | copy-start | bytes 7077892
  67.3 30.2 %all-to-all-start.2 = ((f32[8,16,1024]{2,1,0:T(8,128)}), f32[8,16,1024]{2,1,0:T(8,128)S(1)}, u32[]{:S(2)}, u32[]{:S(2)}) async-start(f32[8,16,1024]{2,1,0:T(8,128)} %bitcast.38), calls=%async_computation.2 | async-start | bytes 1048576 | tf_op jit(solution)/shard_map/all_to_all | solution.py:300
  79.1 6.1 %copy-start.5 = (s32[2]{0:T(128)S(1)}, s32[2]{0:T(128)}, u32[]{:S(2)}) copy-start(s32[2]{0:T(128)} %get-tuple-element.22.half_ref) | copy-start | bytes 28
  82.9 13.8 %collective-permute-start = (f32[128,1024]{1,0:T(8,128)S(1)}, f32[128,1024]{1,0:T(8,128)S(1)}, u32[]{:S(2)}, u32[]{:S(2)}) collective-permute-start(f32[128,1024]{1,0:T(8,128)S(1)} %head_share.4), channel_id=1, source_target_pairs={{0,256},{256,0},{1,257},{257,1},{2,258},{258,2},{3,259},{259,3},{4... | collective-permute-start | bytes 1572872 | tf_op jit(solution)/shard_map/ppermute | solution.py:351
  89.0 15.0 %copy-start.8 = (bf16[2048,128]{1,0:T(8,128)(2,1)S(1)}, bf16[2048,128]{1,0:T(8,128)(2,1)}, u32[]{:S(2)}) copy-start(bf16[2048,128]{1,0:T(8,128)(2,1)} %k_ref.3) | copy-start | bytes 1572868
  89.0 15.0 %copy-start.10 = (bf16[16,64,128]{2,1,0:T(8,128)(2,1)S(1)}, bf16[16,64,128]{2,1,0:T(8,128)(2,1)}, u32[]{:S(2)}) copy-start(bf16[16,64,128]{2,1,0:T(8,128)(2,1)} %param.9) | copy-start | bytes 786436
  89.0 15.0 %copy-start.13 = (f32[16,64]{1,0:T(8,128)S(1)}, f32[16,64]{1,0:T(8,128)}, u32[]{:S(2)}) copy-start(f32[16,64]{1,0:T(8,128)} %w_ref.3) | copy-start | bytes 12292
  89.0 15.0 %copy-start.17 = (f32[16,2048]{1,0:T(8,128)S(1)}, f32[16,2048]{1,0:T(8,128)}, u32[]{:S(2)}) copy-start(f32[16,2048]{1,0:T(8,128)} %copy-done.16) | copy-start | bytes 393220
  97.6 20.9 %all-to-all-start.1 = ((f32[8,16,1024]{2,1,0:T(8,128)}), f32[8,16,1024]{2,1,0:T(8,128)S(1)}, u32[]{:S(2)}, u32[]{:S(2)}) async-start(f32[8,16,1024]{2,1,0:T(8,128)} %bitcast.7), calls=%async_computation.1 | async-start | bytes 1048576 | tf_op jit(solution)/shard_map/all_to_all | solution.py:300
  108.3 38.3 %collective-permute-start.2 = (f32[2,4,128,128]{3,2,1,0:T(8,128)S(1)}, f32[2,4,128,128]{3,2,1,0:T(8,128)S(1)}, u32[]{:S(2)}, u32[]{:S(2)}) collective-permute-start(f32[2,4,128,128]{3,2,1,0:T(8,128)S(1)} %get-tuple-element.16), channel_id=1, source_target_pairs={{0,256},{256,0},{1,257},{257,1},{2,258},{258,2},{3,259},{259,3},{4... | collective-permute-start | bytes 1572872 | tf_op jit(solution)/shard_map/ppermute | solution.py:359
  143.1 12.0 %all-to-all-start.4 = ((f32[4,128,128]{2,1,0:T(8,128)}), f32[4,128,128]{2,1,0:T(8,128)S(1)}, u32[]{:S(2)}, u32[]{:S(2)}) async-start(f32[4,128,128]{2,1,0:T(8,128)} %broadcast_in_dim.4), calls=%async_computation.4 | async-start | bytes 524288 | tf_op jit(solution)/shard_map/all_to_all | solution.py:300
  146.7 15.5 %collective-permute-start.3 = (f32[4,128,128]{2,1,0:T(8,128)S(1)}, f32[4,128,128]{2,1,0:T(8,128)S(1)}, u32[]{:S(2)}, u32[]{:S(2)}) collective-permute-start(f32[4,128,128]{2,1,0:T(8,128)S(1)} %dynamic-slice_bitcast_fusion), channel_id=1, source_target_pairs={{0,32},{32,0},{1,33},{33,1},{2,34},{34,2},{3,35},{35,3},{4,36},{36... | collective-permute-start | bytes 786440 | tf_op jit(solution)/shard_map/ppermute | solution.py:321
  156.0 22.8 %all-to-all-start.5 = ((f32[8,128,128]{2,1,0:T(8,128)}), f32[8,128,128]{2,1,0:T(8,128)S(1)}, u32[]{:S(2)}, u32[]{:S(2)}) async-start(f32[8,128,128]{2,1,0:T(8,128)} %broadcast_in_dim.5), calls=%async_computation.5 | async-start | bytes 1048576 | tf_op jit(solution)/shard_map/all_to_all | solution.py:300
  162.2 11.4 %collective-permute-start.6 = (f32[128,128]{1,0:T(8,128)S(1)}, f32[128,128]{1,0:T(8,128)S(1)}, u32[]{:S(2)}, u32[]{:S(2)}) collective-permute-start(f32[128,128]{1,0:T(8,128)S(1)} %get-tuple-element.19), channel_id=1, source_target_pairs={{0,192},{64,128},{128,64},{192,0},{1,193},{65,129},{129,65},{193,1... | collective-permute-start | bytes 196616 | tf_op jit(solution)/shard_map/ppermute | solution.py:321
  164.2 9.4 %collective-permute-start.5 = (f32[128,128]{1,0:T(8,128)S(1)}, f32[128,128]{1,0:T(8,128)S(1)}, u32[]{:S(2)}, u32[]{:S(2)}) collective-permute-start(f32[128,128]{1,0:T(8,128)S(1)} %get-tuple-element.20), channel_id=1, source_target_pairs={{0,128},{64,192},{128,0},{192,64},{1,129},{65,193},{129,1},{193,65... | collective-permute-start | bytes 196616 | tf_op jit(solution)/shard_map/ppermute | solution.py:321
  168.9 9.3 %collective-permute-start.4 = (f32[128,128]{1,0:T(8,128)S(1)}, f32[128,128]{1,0:T(8,128)S(1)}, u32[]{:S(2)}, u32[]{:S(2)}) collective-permute-start(f32[128,128]{1,0:T(8,128)S(1)} %get-tuple-element.18), channel_id=1, source_target_pairs={{0,64},{64,0},{128,192},{192,128},{1,65},{65,1},{129,193},{193,129... | collective-permute-start | bytes 196616 | tf_op jit(solution)/shard_map/ppermute | solution.py:321
  (7 other events, 7.7 us)

commit v3 on v2

--- a/solution.py
+++ b/solution.py
@@ -22,6 +22,10 @@
 NT = (((1,), (1,)), ((), ()))
 NN = (((1,), (0,)), ((), ()))
 TN = (((0,), (0,)), ((), ()))
+
+
+def in_hbm(x):
+    return pltpu.with_memory_space_constraint(x, pltpu.HBM)
 
 
 def dot(a, b, dims):
@@ -85,7 +89,7 @@
         ),
         out_shape=(
             jax.ShapeDtypeStruct((rows // LANES, heads, LANES), jnp.float32),
-            jax.ShapeDtypeStruct((heads, rows, width), q.dtype),
+            pltpu.HBM((heads, rows, width), q.dtype),
         ),
         scratch_shapes=[pltpu.VMEM((rows, LANES), jnp.float32)],
         compiler_params=params(),
@@ -93,7 +97,7 @@
             flops=2 * heads * rows * keys * width, transcendentals=heads * rows * keys, bytes_accessed=6 << 20
         ),
         name="score_stats",
-    )(rel_pos.reshape(rows, 1), q, k)
+    )(rel_pos.reshape(rows, 1), in_hbm(q), k)
 
 
 def combined(stats):
@@ -149,7 +153,7 @@
             flops=2 * heads * rows * keys * width, transcendentals=heads * rows * keys, bytes_accessed=3 << 20
         ),
         name="head_share",
-    )(half, stats, rel_pos.reshape(2 * rows, 1), q, k)
+    )(half, stats, rel_pos.reshape(2 * rows, 1), in_hbm(q), k)
 
 
 def diagonal(rows):
@@ -166,12 +170,10 @@
     for start in range(0, keys, tile):
         k = k_ref[start : start + tile, :]
         lines = []
+        dots = jnp.maximum(dot(q_ref[...], k, NT), 0.0)
         for row in range(rows):
-            own = slice(row * iheads, (row + 1) * iheads)
-            dots = dot(q_ref[own, :], k, NT)
-            lines.append(
-                jnp.sum(jnp.maximum(dots, 0.0) * w[:, row : row + 1], axis=0, keepdims=True)
-            )
+            own = dots[row * iheads : (row + 1) * iheads, :]
+            lines.append(jnp.sum(own * w[:, row : row + 1], axis=0, keepdims=True))
         logits = jnp.concatenate(lines, axis=0) * (index_scale * LOG2E)
         ids = lax.broadcasted_iota(jnp.int32, logits.shape, 1) + start
         logit_ref[:, start : start + tile] = jnp.where(ids <= pos_ref[...], logits, masked_fill)
@@ -195,8 +197,8 @@
     return pl.pallas_call(
         index_logits_kernel,
         out_shape=(
-            jax.ShapeDtypeStruct((rows, keys), jnp.float32),
-            jax.ShapeDtypeStruct((copies, 1, own.size + LANES), jnp.float32),
+            pltpu.HBM((rows, keys), jnp.float32),
+            pltpu.HBM((copies, 1, own.size + LANES), jnp.float32),
         ),
         compiler_params=pltpu.CompilerParams(vmem_limit_bytes=48 * 1024 * 1024),
         cost_estimate=pl.CostEstimate(
@@ -206,9 +208,12 @@
     )(row_pos.reshape(rows, 1), q.reshape(rows * iheads, width), w, k, own)
 
 
-def gradients_kernel(
-    half_ref, parts_ref, logit_ref, stat_ref, q_ref, w_ref, k_ref, before_ref, rows_ref, keys_ref, total_ref, w_col_ref, *, count
-):
+def gradients_kernel(half_ref, parts_ref, logit_ref, stat_ref, q_ref, w_ref, k_ref, *refs, count, before, row_part, key_part):
+    refs = list(refs)
+    before_ref = refs.pop(0) if before else None
+    rows_ref = refs.pop(0) if row_part else None
+    keys_ref = refs.pop(0) if key_part else None
+    total_ref, w_col_ref = refs
     step = pl.program_id(0)
     rows = logit_ref.shape[0]
     iheads = q_ref.shape[0] // rows
@@ -224,31 +229,33 @@
     slope = (probs - target) * count
     k = k_ref[...]
     w = w_col_ref[...]
+    dots = dot(q_ref[...], k, NT)
     coefs = []
     for row in range(rows):
-        own = slice(row * iheads, (row + 1) * iheads)
-        dots = dot(q_ref[own, :], k, NT)
-        coef = jnp.where(dots > 0, slope[row : row + 1, :] * w[:, row : row + 1] * index_scale, 0.0)
+        own = dots[row * iheads : (row + 1) * iheads, :]
+        coef = jnp.where(own > 0, slope[row : row + 1, :] * w[:, row : row + 1] * index_scale, 0.0)
         coefs.append(coef.astype(jnp.bfloat16))
     coef = jnp.concatenate(coefs, axis=0)
-    grad_keys = dot(coef, q_ref[...], TN)
-    near, far, share, _ = keys_ref.shape
-    for other in range(far):
-        for side in range(near):
-            at = (other * near + side) * share
-            keys_ref[side, other] = grad_keys[at : at + share, :]
-    part = dot(coef, k, NN)
-
-    @pl.when(step == 0)
-    def _():
-        rows_ref[...] = part if before_ref is None else before_ref[...] + part
-
-    @pl.when(step > 0)
-    def _():
-        rows_ref[...] += part
-
-
-def gradients(half, parts, logits, stats, q, w, k, before, count, sizes):
+    if key_part:
+        grad_keys = dot(coef, q_ref[...], TN)
+        near, far, share, _ = keys_ref.shape
+        for other in range(far):
+            for side in range(near):
+                at = (other * near + side) * share
+                keys_ref[side, other] = grad_keys[at : at + share, :]
+    if row_part:
+        part = dot(coef, k, NN)
+
+        @pl.when(step == 0)
+        def _():
+            rows_ref[...] = before_ref[...] + part if before else part
+
+        @pl.when(step > 0)
+        def _():
+            rows_ref[...] += part
+
+
+def gradients(half, parts, logits, stats, q, w, k, before, count, sizes, row_part, key_part):
     rows, iheads, width = q.shape
     keys = parts.shape[2]
     flat = rows * iheads
@@ -257,7 +264,6 @@
     far = nf // 2
     tile = far * nz * share
     last = stats.shape[2] // LANES - 1
-    body = gradients_kernel
     operands = [parts, logits, stats, q.reshape(flat, width), w, k]
     in_specs = [
         pl.BlockSpec((parts.shape[0], rows, tile), lambda t, half: (0, 0, t)),
@@ -267,48 +273,55 @@
         pl.BlockSpec((rows, iheads), lambda t, half: (0, 0)),
         pl.BlockSpec((tile, width), lambda t, half: (half[0] * 2 + t, 0)),
     ]
-    if before is None:
-        body = lambda *refs, count: gradients_kernel(*refs[:7], None, *refs[7:], count=count)
-    else:
+    row_spec = pl.BlockSpec((flat, width), lambda t, half: (0, 0))
+    if before is not None:
         operands.append(before)
-        in_specs.append(pl.BlockSpec((flat, width), lambda t, half: (0, 0)))
+        in_specs.append(row_spec)
+    out_specs, out_shape = [], []
+    if row_part:
+        out_specs.append(row_spec)
+        out_shape.append(jax.ShapeDtypeStruct((flat, width), jnp.float32))
+    if key_part:
+        out_specs.append(pl.BlockSpec((nz, far, share, width), lambda t, half: (0, t, 0, 0)))
+        out_shape.append(jax.ShapeDtypeStruct((nz, nf, share, width), jnp.float32))
     return pl.pallas_call(
-        functools.partial(body, count=float(count)),
+        functools.partial(
+            gradients_kernel, count=float(count), before=before is not None, row_part=row_part, key_part=key_part
+        ),
         grid_spec=pltpu.PrefetchScalarGridSpec(
             num_scalar_prefetch=1,
             grid=(keys // tile,),
             in_specs=in_specs,
-            out_specs=(
-                pl.BlockSpec((flat, width), lambda t, half: (0, 0)),
-                pl.BlockSpec((nz, far, share, width), lambda t, half: (0, t, 0, 0)),
-            ),
+            out_specs=out_specs,
             scratch_shapes=[pltpu.VMEM((rows, 1), jnp.float32), pltpu.VMEM((iheads, rows), jnp.float32)],
         ),
-        out_shape=(
-            jax.ShapeDtypeStruct((flat, width), jnp.float32),
-            jax.ShapeDtypeStruct((nz, nf, share, width), jnp.float32),
-        ),
+        out_shape=out_shape,
         compiler_params=params(),
         cost_estimate=pl.CostEstimate(
-            flops=6 * flat * keys * width, transcendentals=rows * keys, bytes_accessed=2 << 20
+            flops=(2 + 2 * row_part + 2 * key_part) * flat * keys * width,
+            transcendentals=rows * keys,
+            bytes_accessed=2 << 20,
         ),
         name="gradients",
-    )(half, *operands)
+    )(half, parts, in_hbm(logits), *operands[2:])
+
+
+def sum_copies_kernel(parts_ref, out_ref):
+    total = jnp.sum(parts_ref[...], axis=0)
+    out_ref[...] = jnp.broadcast_to(total[None], out_ref.shape)
+
+
+def sum_copies(parts, copies):
+    return pl.pallas_call(
+        sum_copies_kernel,
+        out_shape=jax.ShapeDtypeStruct((copies, *parts.shape[1:]), parts.dtype),
+        compiler_params=pltpu.CompilerParams(vmem_limit_bytes=8 * 1024 * 1024),
+        name="sum_copies",
+    )(parts)
 
 
 def exchanged(parts, axis):
     return lax.all_to_all(parts, axis, split_axis=0, concat_axis=0, tiled=True)
-
-
-def spread(shard, axis):
-    size = lax.axis_size(axis)
-    return exchanged(jnp.broadcast_to(shard[None], (size, *shard.shape)), axis)
-
-
-def summed(shard, axis):
-    size = lax.axis_size(axis)
-    parts = exchanged(shard.reshape(size, -1, shard.shape[-1]), axis)
-    return parts.sum(axis=0)
 
 
 def at_owner(parts, axis):
@@ -351,18 +364,28 @@
         near = lax.ppermute(shares["sent", turn], "yl", swap)
         near = (near + shares["kept", turn]).reshape(-1, rows, keys // 2)
         parts = exchanged(near, RING)
-        grad_rows, part = gradients(
-            pick(half), parts, logits, stats, index_query, index_weights, index_keys, grad_rows,
-            lax.axis_size(KEY) * keys, sizes,
-        )
+
+        def grads(rows_before, row_part, key_part):
+            return gradients(
+                pick(half), parts, logits, stats, index_query, index_weights, index_keys, rows_before,
+                lax.axis_size(KEY) * keys, sizes, row_part, key_part,
+            )
+
+        if turn == 0:
+            grad_rows, part = grads(None, True, True)
+        else:
+            (grad_rows,) = grads(grad_rows, True, False)
+        if turn == 1:
+            (part,) = grads(None, False, True)
         grad_keys.append(part)
     near = lax.ppermute(grad_keys[0], "yl", swap)
     near = near + grad_keys[1]
     near = at_owner(near, "zl")
     key_grads = at_owner(near, "zh")
-    total = summed(grad_rows, SIDE)
-    total = spread(total, "yh").sum(axis=0)
-    query_grads = spread(total, SIDE).reshape(index_query.shape)
+    side = lax.axis_size(SIDE)
+    total = exchanged(grad_rows.reshape(side, -1, grad_rows.shape[1]), SIDE)
+    total = exchanged(sum_copies(total, lax.axis_size("yh")), "yh")
+    query_grads = exchanged(sum_copies(total, side), SIDE).reshape(index_query.shape)
     return (query_grads, key_grads)
 
 

time: 181 us -> 175 us (0.967)
  blocking collectives: 17.5 us -> 0 us
  local copies, waits for them, and re-layouts: 13.8 us -> 3.4 us
  Pallas kernels: 37.7 us -> 46.8 us
  starting transfers between devices: 57.9 us -> 66.1 us
  waiting for transfers between devices: 47.8 us -> 51.8 us
    all_to_all x1 -> x0, blocking collectives: 17.5 us -> none  [exchanged(): return lax.all_to_all(parts, axis, split_axis=0, concat_axis=0, tiled=True)]
    unnamed x39 -> x17, local copies, waits for them, and re-layouts: 11.9 us -> 3.05 us
    all_to_all x5 -> x6, starting transfers between devices: 37.2 us -> 45.5 us  [exchanged(): return lax.all_to_all(parts, axis, split_axis=0, concat_axis=0, tiled=True)]
    all_to_all x5 -> x6, waiting for transfers between devices: 27 us -> 33.3 us  [exchanged(): return lax.all_to_all(parts, axis, split_axis=0, concat_axis=0, tiled=True)]
    pallas_call x4, Pallas kernels: 15 us -> 19.6 us  [head_share(): pl.pallas_call(head_share_kernel, grid_spec=pltpu.PrefetchScalarGridSpec(...]
    pallas_call x3 -> x6, Pallas kernels: 11 us -> 14.4 us  [the longest x3 10.6 us: gradients(): pl.pallas_call(functools.partial(gradients_kernel, count=float(count), be...]
    ppermute x2, waiting for transfers between devices: 16.3 us -> 14 us  [shards(): near = lax.ppermute(shares['sent', turn], 'yl', swap)]
  transfers between devices with their start and end apart: 12 -> 13, of which waited for: 6 -> 7; matrix products, arithmetic and copies ran while one was open for 2% -> 2% of each run, Pallas kernels for 10% -> 16%
where the time goes in v3:
time: 175 us; the launch traced here: 173 us
  starting transfers between devices  66.1 us (38%)
  waiting for transfers between devices  51.8 us (30%)
  Pallas kernels  46.8 us (27%)
  other arithmetic  4.39 us (3%)
  local copies, waits for them, and re-layouts  3.4 us (2%)
    all_to_all x6, starting transfers between devices, exchanged(): return lax.all_to_all(parts, axis, split_axis=0, concat_axis=0, tiled=True)  45.5 us
    all_to_all x6, waiting for transfers between devices, exchanged(): return lax.all_to_all(parts, axis, split_axis=0, concat_axis=0, tiled=True)  33.3 us
    pallas_call x4, Pallas kernels, head_share(): pl.pallas_call(head_share_kernel, grid_spec=pltpu.PrefetchScalarGridSpec(...  19.6 us
    ppermute x2, waiting for transfers between devices, shards(): near = lax.ppermute(shares['sent', turn], 'yl', swap)  14 us
    ppermute x4, starting transfers between devices, at_owner(): got.append(lax.ppermute(part, axis, [(i, i ^ hop) for i in range(size)]))  13.6 us
    pallas_call x1, Pallas kernels, score_stats(): pl.pallas_call(functools.partial(score_stats_kernel, tile=512), grid=(hea...  12.8 us
    pallas_call x3, Pallas kernels, gradients(): pl.pallas_call(functools.partial(gradients_kernel, count=float(count), be...  10.6 us
    ppermute x4, waiting for transfers between devices, at_owner(): got.append(lax.ppermute(part, axis, [(i, i ^ hop) for i in range(size)]))  4.56 us
  transfers between devices with their start and end apart: 13, of which 7 were waited for; matrix products, arithmetic and copies ran while one was open for 2% of the time, Pallas kernels for 16%

profile of v3, /device:TPU:1, one launch (start us, length us, event | category | flops | bytes accessed | tf_op | source)
XLA Modules:
  0.0 173.4 jit_solution(272765236013050975)
XLA Ops:
  3.3 12.8 %score_stats.1 = (f32[2,8,128]{2,1,0:T(8,128)S(1)}, bf16[8,256,576]{2,1,0:T(8,128)(2,1)}) custom-call(s32[256,1]{1,0:T(8,128)S(1)} %copy.9.pos_ref, bf16[8,576,256]{2,1,0:T(8,128)(2,1)} %bitcast.40, bf16[576,2048]{1,0:T(8,128)(2,1)S(1)} %bitcast.28), custom_call_target="tpu_custom_call" | custom-call | flops 4831838208 | bytes 6291456 | tf_op jit(solution)/shard_map/score_stats/pallas_call | solution.py:78
  18.3 11.2 %all-to-all-start = ((f32[32,1,2176]{2,1,0:T(1,128)}), f32[32,1,2176]{2,1,0:T(1,128)S(1)}, u32[]{:S(2)}, u32[]{:S(2)}) async-start(f32[32,1,2176]{2,1,0:T(1,128)} %get-tuple-element.9), calls=%async_computation | async-start | bytes 557056 | tf_op jit(solution)/shard_map/all_to_all | solution.py:324
  30.1 12.9 %all-to-all-done.stats_ref.stat_ref = f32[32,1,2176]{2,1,0:T(1,128)S(1)} async-done(((f32[32,1,2176]{2,1,0:T(1,128)}), f32[32,1,2176]{2,1,0:T(1,128)S(1)}, u32[]{:S(2)}, u32[]{:S(2)}) %all-to-all-start) | async-done | bytes 278560 | tf_op jit(solution)/shard_map/all_to_all | solution.py:324
  43.6 4.9 %head_share.6 = f32[128,1024]{1,0:T(8,128)S(1)} custom-call(s32[2]{0:T(128)S(1)} %copy-done.7, f32[32,1,2176]{2,1,0:T(1,128)S(1)} %all-to-all-done.stats_ref.stat_ref, s32[256,1]{1,0:T(8,128)S(1)} %copy.9.pos_ref, bf16[8,256,576]{2,1,0:T(8,128)(2,1)} %get-tuple-element.10.q_ref, bf16[576,2048]{1,0:T(8,128)(2,1)S(1)} %bitcast.29), custom_call_target="tpu_custom_call" | custom-call | flops 1207959552 | bytes 3145728 | tf_op jit(solution)/shard_map/head_share/pallas_call | solution.py:136
  51.1 4.9 %head_share.7 = f32[128,1024]{1,0:T(8,128)S(1)} custom-call(s32[2]{0:T(128)S(1)} %get-tuple-element.17.half_ref, f32[32,1,2176]{2,1,0:T(1,128)S(1)} %all-to-all-done.stats_ref.stat_ref, s32[256,1]{1,0:T(8,128)S(1)} %copy.9.pos_ref, bf16[8,256,576]{2,1,0:T(8,128)(2,1)} %get-tuple-element.10.q_ref, bf16[576,2048]{1,0:T(8,128)(2,1)S(1)} %bitcast.30), custom_call_target="tpu_custom_call" | custom-call | flops 1207959552 | bytes 3145728 | tf_op jit(solution)/shard_map/head_share/pallas_call | solution.py:136
  56.0 7.4 %collective-permute-done.1 = f32[128,1024]{1,0:T(8,128)S(1)} collective-permute-done((f32[128,1024]{1,0:T(8,128)S(1)}, f32[128,1024]{1,0:T(8,128)S(1)}, u32[]{:S(2)}, u32[]{:S(2)}) %collective-permute-start.1) | collective-permute-done | bytes 524320 | tf_op jit(solution)/shard_map/ppermute | solution.py:364
  64.3 10.0 %all-to-all-start.2 = ((f32[8,16,1024]{2,1,0:T(8,128)}), f32[8,16,1024]{2,1,0:T(8,128)}, u32[]{:S(2)}, u32[]{:S(2)}) async-start(f32[8,16,1024]{2,1,0:T(8,128)} %bitcast.37), calls=%async_computation.2 | async-start | bytes 1048576 | tf_op jit(solution)/shard_map/all_to_all | solution.py:324
  74.5 4.9 %head_share.4 = f32[128,1024]{1,0:T(8,128)S(1)} custom-call(s32[2]{0:T(128)S(1)} %pad_add_fusion.1.half_ref, f32[32,1,2176]{2,1,0:T(1,128)S(1)} %all-to-all-done.stats_ref.stat_ref, s32[256,1]{1,0:T(8,128)S(1)} %copy.9.pos_ref, bf16[8,256,576]{2,1,0:T(8,128)(2,1)} %get-tuple-element.10.q_ref, bf16[576,2048]{1,0:T(8,128)(2,1)S(1)} %bitcast.31), custom_call_target="tpu_custom_call" | custom-call | flops 1207959552 | bytes 3145728 | tf_op jit(solution)/shard_map/head_share/pallas_call | solution.py:136
  81.7 4.9 %head_share.5 = f32[128,1024]{1,0:T(8,128)S(1)} custom-call(s32[2]{0:T(128)S(1)} %copy-done.6, f32[32,1,2176]{2,1,0:T(1,128)S(1)} %all-to-all-done.stats_ref.stat_ref, s32[256,1]{1,0:T(8,128)S(1)} %copy.9.pos_ref, bf16[8,256,576]{2,1,0:T(8,128)(2,1)} %get-tuple-element.10.q_ref, bf16[576,2048]{1,0:T(8,128)(2,1)S(1)} %bitcast.32), custom_call_target="tpu_custom_call" | custom-call | flops 1207959552 | bytes 3145728 | tf_op jit(solution)/shard_map/head_share/pallas_call | solution.py:136
  86.6 6.5 %collective-permute-done = f32[128,1024]{1,0:T(8,128)S(1)} collective-permute-done((f32[128,1024]{1,0:T(8,128)S(1)}, f32[128,1024]{1,0:T(8,128)S(1)}, u32[]{:S(2)}, u32[]{:S(2)}) %collective-permute-start) | collective-permute-done | bytes 524320 | tf_op jit(solution)/shard_map/ppermute | solution.py:364
  94.0 6.4 %all-to-all-start.1 = ((f32[8,16,1024]{2,1,0:T(8,128)}), f32[8,16,1024]{2,1,0:T(8,128)S(1)}, u32[]{:S(2)}, u32[]{:S(2)}) async-start(f32[8,16,1024]{2,1,0:T(8,128)} %bitcast.7), calls=%async_computation.1 | async-start | bytes 1048576 | tf_op jit(solution)/shard_map/all_to_all | solution.py:324
  100.4 3.6 %gradients.3 = (f32[1024,128]{1,0:T(8,128)S(1)}, f32[2,4,128,128]{3,2,1,0:T(8,128)S(1)}) custom-call(s32[1]{0:T(128)} %bitcast.1.half_ref, f32[8,16,1024]{2,1,0:T(8,128)} %all-to-all-done.2.parts_ref, f32[16,2048]{1,0:T(8,128)} %get-tuple-element.11.logit_ref, f32[32,1,2176]{2,1,0:T(1,128)S(1)} %all-to-all-done.stats_ref.stat_ref, ...), custom_call_target="tpu_custom_call" | custom-call | flops 805306368 | bytes 2097152 | tf_op jit(solution)/shard_map/gradients/pallas_call | solution.py:287
  104.0 2.7 %collective-permute-start.2 = (f32[2,4,128,128]{3,2,1,0:T(8,128)S(1)}, f32[2,4,128,128]{3,2,1,0:T(8,128)S(1)}, u32[]{:S(2)}, u32[]{:S(2)}) collective-permute-start(f32[2,4,128,128]{3,2,1,0:T(8,128)S(1)} %get-tuple-element.13), channel_id=1, source_target_pairs={{0,256},{256,0},{1,257},{257,1},{2,258},{258,2},{3,259},{259,3},{4... | collective-permute-start | bytes 1572872 | tf_op jit(solution)/shard_map/ppermute | solution.py:381
  106.7 8.2 %all-to-all-done.1.parts_ref = f32[8,16,1024]{2,1,0:T(8,128)S(1)} async-done(((f32[8,16,1024]{2,1,0:T(8,128)}), f32[8,16,1024]{2,1,0:T(8,128)S(1)}, u32[]{:S(2)}, u32[]{:S(2)}) %all-to-all-start.1) | async-done | bytes 524320 | tf_op jit(solution)/shard_map/all_to_all | solution.py:324
  114.9 3.6 %gradients.4 = f32[1024,128]{1,0:T(8,128)} custom-call(s32[1]{0:T(128)} %bitcast.half_ref, f32[8,16,1024]{2,1,0:T(8,128)S(1)} %all-to-all-done.1.parts_ref, f32[16,2048]{1,0:T(8,128)} %get-tuple-element.11.logit_ref, f32[32,1,2176]{2,1,0:T(1,128)S(1)} %all-to-all-done.stats_ref.stat_ref, bf16[1024,128]{1,0:T(8,128)(2,1)S(1)} %bitcast.35, ...), custom_call_target="tpu_custom_call" | custom-call | flops 536870912 | bytes 2097152 | tf_op jit(solution)/shard_map/gradients/pallas_call | solution.py:287
  118.5 8.4 %all-to-all-start.3 = ((f32[8,128,128]{2,1,0:T(8,128)}), f32[8,128,128]{2,1,0:T(8,128)S(1)}, u32[]{:S(2)}, u32[]{:S(2)}) async-start(f32[8,128,128]{2,1,0:T(8,128)} %bitcast.9), calls=%async_computation.3 | async-start | bytes 1048576 | tf_op jit(solution)/shard_map/all_to_all | solution.py:324
  126.9 9.3 %all-to-all-done.3.parts_ref = f32[8,128,128]{2,1,0:T(8,128)S(1)} async-done(((f32[8,128,128]{2,1,0:T(8,128)}), f32[8,128,128]{2,1,0:T(8,128)S(1)}, u32[]{:S(2)}, u32[]{:S(2)}) %all-to-all-start.3) | async-done | bytes 524320 | tf_op jit(solution)/shard_map/all_to_all | solution.py:324
  137.0 3.4 %all-to-all-start.4 = ((f32[4,128,128]{2,1,0:T(8,128)}), f32[4,128,128]{2,1,0:T(8,128)S(1)}, u32[]{:S(2)}, u32[]{:S(2)}) async-start(f32[4,128,128]{2,1,0:T(8,128)} %sum_copies.2), calls=%async_computation.4 | async-start | bytes 524288 | tf_op jit(solution)/shard_map/all_to_all | solution.py:324
  140.4 3.5 %gradients.5 = f32[2,4,128,128]{3,2,1,0:T(8,128)S(1)} custom-call(s32[1]{0:T(128)} %bitcast.half_ref, f32[8,16,1024]{2,1,0:T(8,128)S(1)} %all-to-all-done.1.parts_ref, f32[16,2048]{1,0:T(8,128)} %get-tuple-element.11.logit_ref, f32[32,1,2176]{2,1,0:T(1,128)S(1)} %all-to-all-done.stats_ref.stat_ref, bf16[1024,128]{1,0:T(8,128)(2,1)S(1)} %bitcast.36, ...), custom_call_target="tpu_custom_call" | custom-call | flops 536870912 | bytes 2097152 | tf_op jit(solution)/shard_map/gradients/pallas_call | solution.py:287
  146.2 2.8 %all-to-all-done.4.parts_ref = f32[4,128,128]{2,1,0:T(8,128)S(1)} async-done(((f32[4,128,128]{2,1,0:T(8,128)}), f32[4,128,128]{2,1,0:T(8,128)S(1)}, u32[]{:S(2)}, u32[]{:S(2)}) %all-to-all-start.4) | async-done | bytes 262176 | tf_op jit(solution)/shard_map/all_to_all | solution.py:324
  149.8 6.1 %all-to-all-start.5 = ((f32[8,128,128]{2,1,0:T(8,128)}), f32[8,128,128]{2,1,0:T(8,128)S(1)}, u32[]{:S(2)}, u32[]{:S(2)}) async-start(f32[8,128,128]{2,1,0:T(8,128)} %sum_copies.3), calls=%async_computation.5 | async-start | bytes 1048576 | tf_op jit(solution)/shard_map/all_to_all | solution.py:324
  158.0 4.6 %collective-permute-start.5 = (f32[128,128]{1,0:T(8,128)S(1)}, f32[128,128]{1,0:T(8,128)S(1)}, u32[]{:S(2)}, u32[]{:S(2)}) collective-permute-start(f32[128,128]{1,0:T(8,128)S(1)} %get-tuple-element.16), channel_id=1, source_target_pairs={{0,128},{64,192},{128,0},{192,64},{1,129},{65,193},{129,1},{193,65... | collective-permute-start | bytes 196616 | tf_op jit(solution)/shard_map/ppermute | solution.py:334
  162.6 4.7 %collective-permute-start.4 = (f32[128,128]{1,0:T(8,128)S(1)}, f32[128,128]{1,0:T(8,128)S(1)}, u32[]{:S(2)}, u32[]{:S(2)}) collective-permute-start(f32[128,128]{1,0:T(8,128)S(1)} %get-tuple-element.14), channel_id=1, source_target_pairs={{0,64},{64,0},{128,192},{192,128},{1,65},{65,1},{129,193},{193,129... | collective-permute-start | bytes 196616 | tf_op jit(solution)/shard_map/ppermute | solution.py:334
  167.4 4.5 %collective-permute-done.4 = f32[128,128]{1,0:T(8,128)S(1)} collective-permute-done((f32[128,128]{1,0:T(8,128)S(1)}, f32[128,128]{1,0:T(8,128)S(1)}, u32[]{:S(2)}, u32[]{:S(2)}) %collective-permute-start.4) | collective-permute-done | bytes 65568 | tf_op jit(solution)/shard_map/ppermute | solution.py:334
  (44 shorter events, 20.1 us)
Async XLA Ops:
  1.6 1.7 copy-start
  3.3 12.8 %copy-start.2 = (bf16[2048,128]{1,0:T(8,128)(2,1)S(1)}, bf16[2048,128]{1,0:T(8,128)(2,1)}, u32[]{:S(2)}) copy-start(bf16[2048,128]{1,0:T(8,128)(2,1)} %k_ref.7) | copy-start | bytes 1572868
  3.3 12.8 %copy-start.3 = (bf16[16,64,128]{2,1,0:T(8,128)(2,1)S(1)}, bf16[16,64,128]{2,1,0:T(8,128)(2,1)}, u32[]{:S(2)}) copy-start(bf16[16,64,128]{2,1,0:T(8,128)(2,1)} %param.9) | copy-start | bytes 786436
  3.3 12.8 %copy-start.4 = (f32[16,64]{1,0:T(8,128)S(1)}, f32[16,64]{1,0:T(8,128)}, u32[]{:S(2)}) copy-start(f32[16,64]{1,0:T(8,128)} %w_ref.7) | copy-start | bytes 12292
  16.1 26.9 %copy-start.1 = (bf16[2048,576]{0,1:T(8,128)(2,1)S(1)}, bf16[2048,576]{0,1:T(8,128)(2,1)}, u32[]{:S(2)}) copy-start(bf16[2048,576]{0,1:T(8,128)(2,1)} %param.8) | copy-start | bytes 7077892
  18.3 24.7 %all-to-all-start = ((f32[32,1,2176]{2,1,0:T(1,128)}), f32[32,1,2176]{2,1,0:T(1,128)S(1)}, u32[]{:S(2)}, u32[]{:S(2)}) async-start(f32[32,1,2176]{2,1,0:T(1,128)} %get-tuple-element.9), calls=%async_computation | async-start | bytes 557056 | tf_op jit(solution)/shard_map/all_to_all | solution.py:324
  43.0 0.6 copy-start.7
  48.5 14.9 %collective-permute-start.1 = (f32[128,1024]{1,0:T(8,128)S(1)}, f32[128,1024]{1,0:T(8,128)S(1)}, u32[]{:S(2)}, u32[]{:S(2)}) collective-permute-start(f32[128,1024]{1,0:T(8,128)S(1)} %head_share.6), channel_id=1, source_target_pairs={{0,256},{256,0},{1,257},{257,1},{2,258},{258,2},{3,259},{259,3},{4... | collective-permute-start | bytes 1572872 | tf_op jit(solution)/shard_map/ppermute | solution.py:364
  64.3 29.7 %all-to-all-start.2 = ((f32[8,16,1024]{2,1,0:T(8,128)}), f32[8,16,1024]{2,1,0:T(8,128)}, u32[]{:S(2)}, u32[]{:S(2)}) async-start(f32[8,16,1024]{2,1,0:T(8,128)} %bitcast.37), calls=%async_computation.2 | async-start | bytes 1048576 | tf_op jit(solution)/shard_map/all_to_all | solution.py:324
  74.4 7.2 %copy-start.6 = (s32[2]{0:T(128)S(1)}, s32[2]{0:T(128)}, u32[]{:S(2)}) copy-start(s32[2]{0:T(128)} %get-tuple-element.18.half_ref) | copy-start | bytes 28
  79.4 13.8 %collective-permute-start = (f32[128,1024]{1,0:T(8,128)S(1)}, f32[128,1024]{1,0:T(8,128)S(1)}, u32[]{:S(2)}, u32[]{:S(2)}) collective-permute-start(f32[128,1024]{1,0:T(8,128)S(1)} %head_share.4), channel_id=1, source_target_pairs={{0,256},{256,0},{1,257},{257,1},{2,258},{258,2},{3,259},{259,3},{4... | collective-permute-start | bytes 1572872 | tf_op jit(solution)/shard_map/ppermute | solution.py:364
  86.6 13.8 %copy-start.5 = (f32[16,64]{1,0:T(8,128)S(1)}, f32[16,64]{1,0:T(8,128)}, u32[]{:S(2)}) copy-start(f32[16,64]{1,0:T(8,128)} %w_ref.7) | copy-start | bytes 12292
  94.0 20.9 %all-to-all-start.1 = ((f32[8,16,1024]{2,1,0:T(8,128)}), f32[8,16,1024]{2,1,0:T(8,128)S(1)}, u32[]{:S(2)}, u32[]{:S(2)}) async-start(f32[8,16,1024]{2,1,0:T(8,128)} %bitcast.7), calls=%async_computation.1 | async-start | bytes 1048576 | tf_op jit(solution)/shard_map/all_to_all | solution.py:324
  104.0 39.8 %collective-permute-start.2 = (f32[2,4,128,128]{3,2,1,0:T(8,128)S(1)}, f32[2,4,128,128]{3,2,1,0:T(8,128)S(1)}, u32[]{:S(2)}, u32[]{:S(2)}) collective-permute-start(f32[2,4,128,128]{3,2,1,0:T(8,128)S(1)} %get-tuple-element.13), channel_id=1, source_target_pairs={{0,256},{256,0},{1,257},{257,1},{2,258},{258,2},{3,259},{259,3},{4... | collective-permute-start | bytes 1572872 | tf_op jit(solution)/shard_map/ppermute | solution.py:381
  118.5 17.7 %all-to-all-start.3 = ((f32[8,128,128]{2,1,0:T(8,128)}), f32[8,128,128]{2,1,0:T(8,128)S(1)}, u32[]{:S(2)}, u32[]{:S(2)}) async-start(f32[8,128,128]{2,1,0:T(8,128)} %bitcast.9), calls=%async_computation.3 | async-start | bytes 1048576 | tf_op jit(solution)/shard_map/all_to_all | solution.py:324
  137.0 12.0 %all-to-all-start.4 = ((f32[4,128,128]{2,1,0:T(8,128)}), f32[4,128,128]{2,1,0:T(8,128)S(1)}, u32[]{:S(2)}, u32[]{:S(2)}) async-start(f32[4,128,128]{2,1,0:T(8,128)} %sum_copies.2), calls=%async_computation.4 | async-start | bytes 524288 | tf_op jit(solution)/shard_map/all_to_all | solution.py:324
  144.0 12.0 %collective-permute-start.3 = (f32[4,128,128]{2,1,0:T(8,128)S(1)}, f32[4,128,128]{2,1,0:T(8,128)S(1)}, u32[]{:S(2)}, u32[]{:S(2)}) collective-permute-start(f32[4,128,128]{2,1,0:T(8,128)S(1)} %dynamic-slice_bitcast_fusion), channel_id=1, source_target_pairs={{0,32},{32,0},{1,33},{33,1},{2,34},{34,2},{3,35},{35,3},{4,36},{36... | collective-permute-start | bytes 786440 | tf_op jit(solution)/shard_map/ppermute | solution.py:334
  149.8 22.8 %all-to-all-start.5 = ((f32[8,128,128]{2,1,0:T(8,128)}), f32[8,128,128]{2,1,0:T(8,128)S(1)}, u32[]{:S(2)}, u32[]{:S(2)}) async-start(f32[8,128,128]{2,1,0:T(8,128)} %sum_copies.3), calls=%async_computation.5 | async-start | bytes 1048576 | tf_op jit(solution)/shard_map/all_to_all | solution.py:324
  156.0 11.4 %collective-permute-start.6 = (f32[128,128]{1,0:T(8,128)S(1)}, f32[128,128]{1,0:T(8,128)S(1)}, u32[]{:S(2)}, u32[]{:S(2)}) collective-permute-start(f32[128,128]{1,0:T(8,128)S(1)} %get-tuple-element.15), channel_id=1, source_target_pairs={{0,192},{64,128},{128,64},{192,0},{1,193},{65,129},{129,65},{193,1... | collective-permute-start | bytes 196616 | tf_op jit(solution)/shard_map/ppermute | solution.py:334
  158.0 9.4 %collective-permute-start.5 = (f32[128,128]{1,0:T(8,128)S(1)}, f32[128,128]{1,0:T(8,128)S(1)}, u32[]{:S(2)}, u32[]{:S(2)}) collective-permute-start(f32[128,128]{1,0:T(8,128)S(1)} %get-tuple-element.16), channel_id=1, source_target_pairs={{0,128},{64,192},{128,0},{192,64},{1,129},{65,193},{129,1},{193,65... | collective-permute-start | bytes 196616 | tf_op jit(solution)/shard_map/ppermute | solution.py:334
  162.6 9.3 %collective-permute-start.4 = (f32[128,128]{1,0:T(8,128)S(1)}, f32[128,128]{1,0:T(8,128)S(1)}, u32[]{:S(2)}, u32[]{:S(2)}) collective-permute-start(f32[128,128]{1,0:T(8,128)S(1)} %get-tuple-element.14), channel_id=1, source_target_pairs={{0,64},{64,0},{128,192},{192,128},{1,65},{65,1},{129,193},{193,129... | collective-permute-start | bytes 196616 | tf_op jit(solution)/shard_map/ppermute | solution.py:334

commit v4 on v3

--- a/solution.py
+++ b/solution.py
@@ -11,6 +11,8 @@
 
 HEADS = 128
 LANES = 128
+PIECE = 144
+TILE = 512
 KEY = ("x", "yh", "core")
 HEAD = ("yl", "zh", "zl")
 RING = ("zh", "zl")
@@ -28,20 +30,38 @@
     return pltpu.with_memory_space_constraint(x, pltpu.HBM)
 
 
+def in_vmem(x):
+    return pltpu.with_memory_space_constraint(x, pltpu.VMEM)
+
+
 def dot(a, b, dims):
     return lax.dot_general(a, b, dims, preferred_element_type=jnp.float32)
 
 
-def params(semantics=("arbitrary",)):
+def params(mebibytes=24):
     return pltpu.CompilerParams(
-        dimension_semantics=semantics, vmem_limit_bytes=48 * 1024 * 1024
+        dimension_semantics=("arbitrary",), vmem_limit_bytes=mebibytes * 1024 * 1024
     )
 
 
-def score_stats_kernel(pos_ref, q_ref, k_ref, out_ref, rows_ref, col_ref, *, tile):
+def score_stats_kernel(pos_ref, q_ref, source_ref, out_ref, rows_ref, k_ref, col_ref, sems, *, tile):
     head = pl.program_id(0)
     heads = pl.num_programs(0)
     keys = k_ref.shape[1]
+    copies = [
+        pltpu.make_async_copy(
+            source_ref.at[pl.ds(at * PIECE, PIECE), :], k_ref.at[pl.ds(at * PIECE, PIECE), :], sems.at[at]
+        )
+        for at in range(k_ref.shape[0] // PIECE)
+    ]
+
+    @pl.when(head == 0)
+    def _():
+        for copy in copies:
+            copy.start()
+        for copy in copies:
+            copy.wait()
+
     q = jnp.transpose(q_ref[0])
     rows_ref[0] = q
     rows = q.shape[0]
@@ -81,23 +101,28 @@
         in_specs=[
             pl.BlockSpec((rows, 1), lambda h: (0, 0)),
             pl.BlockSpec((1, width, rows), lambda h: (h, 0, 0)),
-            pl.BlockSpec((width, keys), lambda h: (0, 0)),
+            pl.BlockSpec(memory_space=pl.ANY),
         ],
         out_specs=(
             pl.BlockSpec((rows // LANES, heads, LANES), lambda h: (0, 0, 0)),
             pl.BlockSpec((1, rows, width), lambda h: (h, 0, 0)),
+            pl.BlockSpec(memory_space=pltpu.VMEM),
         ),
         out_shape=(
             jax.ShapeDtypeStruct((rows // LANES, heads, LANES), jnp.float32),
             pltpu.HBM((heads, rows, width), q.dtype),
-        ),
-        scratch_shapes=[pltpu.VMEM((rows, LANES), jnp.float32)],
+            pltpu.VMEM((width, keys), k.dtype),
+        ),
+        scratch_shapes=[
+            pltpu.VMEM((rows, LANES), jnp.float32),
+            pltpu.SemaphoreType.DMA((width // PIECE,)),
+        ],
         compiler_params=params(),
         cost_estimate=pl.CostEstimate(
             flops=2 * heads * rows * keys * width, transcendentals=heads * rows * keys, bytes_accessed=6 << 20
         ),
         name="score_stats",
-    )(rel_pos.reshape(rows, 1), in_hbm(q), k)
+    )(rel_pos.reshape(rows, 1), in_hbm(q), in_hbm(k))
 
 
 def combined(stats):
@@ -105,55 +130,66 @@
     return high + jnp.log2(jnp.sum(jnp.exp2(stats - high[None]), axis=0))
 
 
-def head_share_kernel(half_ref, stats_ref, pos_ref, q_ref, k_ref, out_ref, col_ref):
-    heads, rows, _ = q_ref.shape
-    tile = k_ref.shape[1]
-    step = pl.program_id(0)
-
-    @pl.when(step == 0)
+def head_share_kernel(mine_ref, stats_ref, pos_ref, q_ref, k_ref, out_ref, col_ref, *, other_keys):
+    head = pl.program_id(0)
+    heads = pl.num_programs(0)
+    rows, keys = out_ref.shape
+
+    @pl.when(head == 0)
     def _():
         line = combined(stats_ref[...]) + math.log2(HEADS)
-        lines = [line[:, head * rows : (head + 1) * rows] for head in range(heads)]
-        col_ref[:, :heads] = jnp.transpose(jnp.concatenate(lines, axis=0))
-
-    k = k_ref[...]
-    total = None
-    for head in range(heads):
-        scores = dot(q_ref[head], k, NN)
-        part = jnp.exp2(scores * attn_scale - col_ref[:, head : head + 1])
-        total = part if total is None else total + part
-    start = (half_ref[1] * pl.num_programs(0) + step) * tile
-    ids = lax.broadcasted_iota(jnp.int32, total.shape, 1) + start
-    out_ref[...] = jnp.where(ids <= pos_ref[...], total, 0.0)
-
-
-def head_share(half, stats, rel_pos, q, k):
+        lines = [line[:, at * rows : (at + 1) * rows] for at in range(col_ref.shape[0])]
+        cols = jnp.transpose(jnp.concatenate(lines, axis=0))
+        for at in range(col_ref.shape[0]):
+            col_ref[at] = jnp.broadcast_to(cols[:, at : at + 1], col_ref.shape[1:])
+        out_ref[...] = jnp.zeros(out_ref.shape, jnp.float32)
+
+    half = 1 - mine_ref[0] if other_keys else mine_ref[0]
+    start = pl.multiple_of(half * keys, keys)
+    q = q_ref[0]
+    line = col_ref[head]
+    for at in range(0, keys, TILE):
+        scores = dot(q, k_ref[:, pl.ds(start + at, TILE)], NN) * attn_scale
+        for lane in range(0, TILE, LANES):
+            out_ref[:, at + lane : at + lane + LANES] += jnp.exp2(
+                scores[:, lane : lane + LANES] - line
+            )
+
+    @pl.when(head == heads - 1)
+    def _():
+        ids = lax.broadcasted_iota(jnp.int32, out_ref.shape, 1) + start
+        out_ref[...] = jnp.where(ids <= pos_ref[...], out_ref[...], 0.0)
+
+
+def head_share(mine, other_rows, other_keys, stats, rel_pos, q, k):
     heads, rows, width = q.shape
     rows //= 2
     keys = k.shape[1] // 2
-    tile = 256
-    steps = keys // tile
+
+    def part(mine):
+        return 1 - mine[0] if other_rows else mine[0]
+
     return pl.pallas_call(
-        head_share_kernel,
+        functools.partial(head_share_kernel, other_keys=other_keys),
         grid_spec=pltpu.PrefetchScalarGridSpec(
             num_scalar_prefetch=1,
-            grid=(steps,),
+            grid=(heads,),
             in_specs=[
-                pl.BlockSpec((stats.shape[0], 1, heads * rows), lambda t, half: (0, 0, half[0])),
-                pl.BlockSpec((rows, 1), lambda t, half: (half[0], 0)),
-                pl.BlockSpec((heads, rows, width), lambda t, half: (0, half[0], 0)),
-                pl.BlockSpec((width, tile), lambda t, half: (0, half[1] * steps + t)),
+                pl.BlockSpec((stats.shape[0], 1, heads * rows), lambda h, mine: (0, 0, part(mine))),
+                pl.BlockSpec((rows, 1), lambda h, mine: (part(mine), 0)),
+                pl.BlockSpec((1, rows, width), lambda h, mine: (h, part(mine), 0)),
+                pl.BlockSpec(memory_space=pltpu.VMEM),
             ],
-            out_specs=pl.BlockSpec((rows, tile), lambda t, half: (0, t)),
-            scratch_shapes=[pltpu.VMEM((rows, LANES), jnp.float32)],
+            out_specs=pl.BlockSpec((rows, keys), lambda h, mine: (0, 0)),
+            scratch_shapes=[pltpu.VMEM((heads, rows, LANES), jnp.float32)],
         ),
         out_shape=jax.ShapeDtypeStruct((rows, keys), jnp.float32),
-        compiler_params=params(),
+        compiler_params=params(12),
         cost_estimate=pl.CostEstimate(
             flops=2 * heads * rows * keys * width, transcendentals=heads * rows * keys, bytes_accessed=3 << 20
         ),
         name="head_share",
-    )(half, stats, rel_pos.reshape(2 * rows, 1), in_hbm(q), k)
+    )(mine, stats, rel_pos.reshape(2 * rows, 1), in_hbm(q), in_vmem(k))
 
 
 def diagonal(rows):
@@ -200,7 +236,7 @@
             pltpu.HBM((rows, keys), jnp.float32),
             pltpu.HBM((copies, 1, own.size + LANES), jnp.float32),
         ),
-        compiler_params=pltpu.CompilerParams(vmem_limit_bytes=48 * 1024 * 1024),
+        compiler_params=pltpu.CompilerParams(vmem_limit_bytes=16 * 1024 * 1024),
         cost_estimate=pl.CostEstimate(
             flops=2 * rows * iheads * keys * width, transcendentals=rows * keys, bytes_accessed=1 << 20
         ),
@@ -255,7 +291,7 @@
             rows_ref[...] += part
 
 
-def gradients(half, parts, logits, stats, q, w, k, before, count, sizes, row_part, key_part):
+def gradients(mine, other_keys, parts, logits, stats, q, w, k, before, count, sizes, row_part, key_part):
     rows, iheads, width = q.shape
     keys = parts.shape[2]
     flat = rows * iheads
@@ -264,14 +300,18 @@
     far = nf // 2
     tile = far * nz * share
     last = stats.shape[2] // LANES - 1
+
+    def part(mine):
+        return 1 - mine[0] if other_keys else mine[0]
+
     operands = [parts, logits, stats, q.reshape(flat, width), w, k]
     in_specs = [
         pl.BlockSpec((parts.shape[0], rows, tile), lambda t, half: (0, 0, t)),
-        pl.BlockSpec((rows, tile), lambda t, half: (0, half[0] * 2 + t)),
+        pl.BlockSpec((rows, tile), lambda t, mine: (0, part(mine) * 2 + t)),
         pl.BlockSpec((stats.shape[0], 1, LANES), lambda t, half: (0, 0, last)),
         pl.BlockSpec((flat, width), lambda t, half: (0, 0)),
         pl.BlockSpec((rows, iheads), lambda t, half: (0, 0)),
-        pl.BlockSpec((tile, width), lambda t, half: (half[0] * 2 + t, 0)),
+        pl.BlockSpec((tile, width), lambda t, mine: (part(mine) * 2 + t, 0)),
     ]
     row_spec = pl.BlockSpec((flat, width), lambda t, half: (0, 0))
     if before is not None:
@@ -303,7 +343,7 @@
             bytes_accessed=2 << 20,
         ),
         name="gradients",
-    )(half, parts, in_hbm(logits), *operands[2:])
+    )(mine, parts, in_hbm(logits), *operands[2:])
 
 
 def sum_copies_kernel(parts_ref, out_ref):
@@ -340,34 +380,30 @@
     rows = index_query.shape[0]
     rel_pos = query_pos - lax.axis_index(KEY) * keys
     row_pos = lax.dynamic_slice_in_dim(rel_pos, lax.axis_index(HEAD) * rows, rows, 0)
+    mine = in_hbm(lax.axis_index("yl").astype(jnp.int32).reshape(1))
     q = jnp.swapaxes(mla_query, 1, 2)
     k = jnp.swapaxes(latent_keys, 0, 1)
     sizes = [lax.axis_size(axis) for axis in HEAD]
-    own_stats, q_rows = score_stats(rel_pos, q, k)
+    own_stats, q_rows, k_held = score_stats(rel_pos, q, k)
     logits, own_stats = index_logits(
         row_pos, index_query, index_weights, index_keys, own_stats, lax.axis_size(KEY)
     )
     stats = exchanged(own_stats, KEY)
-    mine = lax.axis_index("yl")
-    other = 1 - mine
     swap = [(0, 1), (1, 0)]
-
-    def pick(*halves):
-        return jnp.stack(halves).astype(jnp.int32)
 
     grad_rows, grad_keys = None, []
     shares = {}
-    for name, rows_half, halves in (("sent", other, (mine, other)), ("kept", mine, (other, mine))):
-        for turn, half in enumerate(halves):
-            shares[name, turn] = head_share(pick(rows_half, half), stats, rel_pos, q_rows, k)
-    for turn, half in enumerate((other, mine)):
+    for name, first in (("sent", False), ("kept", True)):
+        for turn in range(2):
+            shares[name, turn] = head_share(mine, name == "sent", first == (turn == 0), stats, rel_pos, q_rows, k_held)
+    for turn in range(2):
         near = lax.ppermute(shares["sent", turn], "yl", swap)
         near = (near + shares["kept", turn]).reshape(-1, rows, keys // 2)
         parts = exchanged(near, RING)
 
         def grads(rows_before, row_part, key_part):
             return gradients(
-                pick(half), parts, logits, stats, index_query, index_weights, index_keys, rows_before,
+                mine, turn == 0, parts, logits, stats, index_query, index_weights, index_keys, rows_before,
                 lax.axis_size(KEY) * keys, sizes, row_part, key_part,
             )
 

time: 175 us -> 177 us (1.011)
  blocking collectives: 0 us -> 24.7 us
  waiting for transfers between devices: 51.8 us -> 36.6 us
  starting transfers between devices: 66.1 us -> 54.9 us
  Pallas kernels: 46.8 us -> 54.3 us
  local copies, waits for them, and re-layouts: 3.4 us -> 1.16 us
    all_to_all x0 -> x1, blocking collectives: none -> 24.7 us  [exchanged(): return lax.all_to_all(parts, axis, split_axis=0, concat_axis=0, tiled=True)]
    all_to_all x6 -> x5, waiting for transfers between devices: 33.3 us -> 20.4 us  [exchanged(): return lax.all_to_all(parts, axis, split_axis=0, concat_axis=0, tiled=True)]
    all_to_all x6 -> x5, starting transfers between devices: 45.5 us -> 34.3 us  [exchanged(): return lax.all_to_all(parts, axis, split_axis=0, concat_axis=0, tiled=True)]
    pallas_call x4, Pallas kernels: 19.6 us -> 25.4 us  [head_share(): pl.pallas_call(functools.partial(head_share_kernel, other_keys=other_keys...]
    ppermute x2, waiting for transfers between devices: 14 us -> 11.7 us  [shards(): near = lax.ppermute(shares['sent', turn], 'yl', swap)]
    unnamed x17 -> x9, local copies, waits for them, and re-layouts: 3.05 us -> 0.82 us
  transfers between devices with their start and end apart: 13 -> 12, of which waited for: 7 -> 6; matrix products, arithmetic and copies ran while one was open for 2% -> 1% of each run, Pallas kernels for 16% -> 18%
where the time goes in v4:
time: 177 us; the launch traced here: 176 us
  starting transfers between devices  54.9 us (31%)
  Pallas kernels  54.3 us (31%)
  waiting for transfers between devices  36.6 us (21%)
  blocking collectives  24.7 us (14%)
  other arithmetic  3.16 us (2%)
    all_to_all x5, starting transfers between devices, exchanged(): return lax.all_to_all(parts, axis, split_axis=0, concat_axis=0, tiled=True)  34.3 us
    pallas_call x4, Pallas kernels, head_share(): pl.pallas_call(functools.partial(head_share_kernel, other_keys=other_keys...  25.4 us
    all_to_all x1, blocking collectives, exchanged(): return lax.all_to_all(parts, axis, split_axis=0, concat_axis=0, tiled=True)  24.7 us
    all_to_all x5, waiting for transfers between devices, exchanged(): return lax.all_to_all(parts, axis, split_axis=0, concat_axis=0, tiled=True)  20.4 us
    pallas_call x1, Pallas kernels, score_stats(): pl.pallas_call(functools.partial(score_stats_kernel, tile=512), grid=(hea...  14.5 us
    ppermute x4, starting transfers between devices, at_owner(): got.append(lax.ppermute(part, axis, [(i, i ^ hop) for i in range(size)]))  13.6 us
    ppermute x2, waiting for transfers between devices, shards(): near = lax.ppermute(shares['sent', turn], 'yl', swap)  11.7 us
    pallas_call x3, Pallas kernels, gradients(): pl.pallas_call(functools.partial(gradients_kernel, count=float(count), be...  10.6 us
  transfers between devices with their start and end apart: 12, of which 6 were waited for; matrix products, arithmetic and copies ran while one was open for 1% of the time, Pallas kernels for 18%

profile of v4, /device:TPU:1, one launch (start us, length us, event | category | flops | bytes accessed | tf_op | source)
XLA Modules:
  0.0 175.7 jit_solution(10655863782033958387)
XLA Ops:
  1.7 14.5 %score_stats.1 = (f32[2,8,128]{2,1,0:T(8,128)S(1)}, bf16[8,256,576]{2,1,0:T(8,128)(2,1)}, bf16[576,2048]{1,0:T(8,128)(2,1)S(1)}) custom-call(s32[256,1]{1,0:T(8,128)S(1)} %copy.9.pos_ref, bf16[8,576,256]{2,1,0:T(8,128)(2,1)} %bitcast.34, bf16[576,2048]{1,0:T(8,128)(2,1)} %bitcast.35), custom_call_target="tpu_custom_call" | custom-call | flops 4831838208 | bytes 6291456 | tf_op jit(solution)/shard_map/score_stats/pallas_call | solution.py:98
  18.4 24.7 %all_to_all.30.stats_ref.stat_ref = f32[32,1,2176]{2,1,0:T(1,128)S(1)} all-to-all(f32[32,1,2176]{2,1,0:T(1,128)} %get-tuple-element.10), channel_id=1, replica_groups=mesh['yl'=2,'zh'=4,'zl'=2,'x'=4,'yh'=4,'core'=2] {'x','yh','core'}, dimensions={0} | all-to-all | bytes 557056 | tf_op jit(solution)/shard_map/all_to_all | solution.py:364
  43.1 6.3 %head_share.6 = f32[128,1024]{1,0:T(8,128)S(1)} custom-call(s32[1]{0:T(128)} %bitcast.mine_ref.half_ref, f32[32,1,2176]{2,1,0:T(1,128)S(1)} %all_to_all.30.stats_ref.stat_ref, s32[256,1]{1,0:T(8,128)S(1)} %copy.9.pos_ref, bf16[8,256,576]{2,1,0:T(8,128)(2,1)} %get-tuple-element.11.q_ref, bf16[576,2048]{1,0:T(8,128)(2,1)S(1)} %get-tuple-element.12.k_ref), custom_call_target="tpu_custom_call" | custom-call | flops 1207959552 | bytes 3145728 | tf_op jit(solution)/shard_map/head_share/pallas_call | solution.py:172
  51.5 6.4 %head_share.7 = f32[128,1024]{1,0:T(8,128)S(1)} custom-call(s32[1]{0:T(128)} %bitcast.mine_ref.half_ref, f32[32,1,2176]{2,1,0:T(1,128)S(1)} %all_to_all.30.stats_ref.stat_ref, s32[256,1]{1,0:T(8,128)S(1)} %copy.9.pos_ref, bf16[8,256,576]{2,1,0:T(8,128)(2,1)} %get-tuple-element.11.q_ref, bf16[576,2048]{1,0:T(8,128)(2,1)S(1)} %get-tuple-element.12.k_ref), custom_call_target="tpu_custom_call" | custom-call | flops 1207959552 | bytes 3145728 | tf_op jit(solution)/shard_map/head_share/pallas_call | solution.py:172
  57.8 6.6 %collective-permute-done.1 = f32[128,1024]{1,0:T(8,128)S(1)} collective-permute-done((f32[128,1024]{1,0:T(8,128)S(1)}, f32[128,1024]{1,0:T(8,128)S(1)}, u32[]{:S(2)}, u32[]{:S(2)}) %collective-permute-start.1) | collective-permute-done | bytes 524320 | tf_op jit(solution)/shard_map/ppermute | solution.py:400
  65.3 10.0 %all-to-all-start.2 = ((f32[8,16,1024]{2,1,0:T(8,128)}), f32[8,16,1024]{2,1,0:T(8,128)}, u32[]{:S(2)}, u32[]{:S(2)}) async-start(f32[8,16,1024]{2,1,0:T(8,128)} %bitcast.31), calls=%async_computation.2 | async-start | bytes 1048576 | tf_op jit(solution)/shard_map/all_to_all | solution.py:364
  75.3 6.3 %head_share.4 = f32[128,1024]{1,0:T(8,128)S(1)} custom-call(s32[1]{0:T(128)} %bitcast.mine_ref.half_ref, f32[32,1,2176]{2,1,0:T(1,128)S(1)} %all_to_all.30.stats_ref.stat_ref, s32[256,1]{1,0:T(8,128)S(1)} %copy.9.pos_ref, bf16[8,256,576]{2,1,0:T(8,128)(2,1)} %get-tuple-element.11.q_ref, bf16[576,2048]{1,0:T(8,128)(2,1)S(1)} %get-tuple-element.12.k_ref), custom_call_target="tpu_custom_call" | custom-call | flops 1207959552 | bytes 3145728 | tf_op jit(solution)/shard_map/head_share/pallas_call | solution.py:172
  81.7 2.3 %collective-permute-start = (f32[128,1024]{1,0:T(8,128)S(1)}, f32[128,1024]{1,0:T(8,128)S(1)}, u32[]{:S(2)}, u32[]{:S(2)}) collective-permute-start(f32[128,1024]{1,0:T(8,128)S(1)} %head_share.4), channel_id=1, source_target_pairs={{0,256},{256,0},{1,257},{257,1},{2,258},{258,2},{3,259},{259,3},{4... | collective-permute-start | bytes 1572872 | tf_op jit(solution)/shard_map/ppermute | solution.py:400
  84.0 6.4 %head_share.5 = f32[128,1024]{1,0:T(8,128)S(1)} custom-call(s32[1]{0:T(128)} %bitcast.mine_ref.half_ref, f32[32,1,2176]{2,1,0:T(1,128)S(1)} %all_to_all.30.stats_ref.stat_ref, s32[256,1]{1,0:T(8,128)S(1)} %copy.9.pos_ref, bf16[8,256,576]{2,1,0:T(8,128)(2,1)} %get-tuple-element.11.q_ref, bf16[576,2048]{1,0:T(8,128)(2,1)S(1)} %get-tuple-element.12.k_ref), custom_call_target="tpu_custom_call" | custom-call | flops 1207959552 | bytes 3145728 | tf_op jit(solution)/shard_map/head_share/pallas_call | solution.py:172
  90.4 5.1 %collective-permute-done = f32[128,1024]{1,0:T(8,128)S(1)} collective-permute-done((f32[128,1024]{1,0:T(8,128)S(1)}, f32[128,1024]{1,0:T(8,128)S(1)}, u32[]{:S(2)}, u32[]{:S(2)}) %collective-permute-start) | collective-permute-done | bytes 524320 | tf_op jit(solution)/shard_map/ppermute | solution.py:400
  96.3 6.3 %all-to-all-start.1 = ((f32[8,16,1024]{2,1,0:T(8,128)}), f32[8,16,1024]{2,1,0:T(8,128)S(1)}, u32[]{:S(2)}, u32[]{:S(2)}) async-start(f32[8,16,1024]{2,1,0:T(8,128)} %bitcast.6), calls=%async_computation.1 | async-start | bytes 1048576 | tf_op jit(solution)/shard_map/all_to_all | solution.py:364
  102.7 3.6 %gradients.3 = (f32[1024,128]{1,0:T(8,128)S(1)}, f32[2,4,128,128]{3,2,1,0:T(8,128)S(1)}) custom-call(s32[1]{0:T(128)} %bitcast.mine_ref.half_ref, f32[8,16,1024]{2,1,0:T(8,128)} %all-to-all-done.2.parts_ref, f32[16,2048]{1,0:T(8,128)} %get-tuple-element.13.logit_ref, f32[32,1,2176]{2,1,0:T(1,128)S(1)} %all_to_all.30.stats_ref.stat_ref, ...), custom_call_target="tpu_custom_call" | custom-call | flops 805306368 | bytes 2097152 | tf_op jit(solution)/shard_map/gradients/pallas_call | solution.py:327
  106.3 2.7 %collective-permute-start.2 = (f32[2,4,128,128]{3,2,1,0:T(8,128)S(1)}, f32[2,4,128,128]{3,2,1,0:T(8,128)S(1)}, u32[]{:S(2)}, u32[]{:S(2)}) collective-permute-start(f32[2,4,128,128]{3,2,1,0:T(8,128)S(1)} %get-tuple-element.15), channel_id=1, source_target_pairs={{0,256},{256,0},{1,257},{257,1},{2,258},{258,2},{3,259},{259,3},{4... | collective-permute-start | bytes 1572872 | tf_op jit(solution)/shard_map/ppermute | solution.py:417
  109.0 8.2 %all-to-all-done.1.parts_ref = f32[8,16,1024]{2,1,0:T(8,128)S(1)} async-done(((f32[8,16,1024]{2,1,0:T(8,128)}), f32[8,16,1024]{2,1,0:T(8,128)S(1)}, u32[]{:S(2)}, u32[]{:S(2)}) %all-to-all-start.1) | async-done | bytes 524320 | tf_op jit(solution)/shard_map/all_to_all | solution.py:364
  117.2 3.6 %gradients.4 = f32[1024,128]{1,0:T(8,128)} custom-call(s32[1]{0:T(128)} %bitcast.mine_ref.half_ref, f32[8,16,1024]{2,1,0:T(8,128)S(1)} %all-to-all-done.1.parts_ref, f32[16,2048]{1,0:T(8,128)} %get-tuple-element.13.logit_ref, f32[32,1,2176]{2,1,0:T(1,128)S(1)} %all_to_all.30.stats_ref.stat_ref, bf16[1024,128]{1,0:T(8,128)(2,1)S(1)} %bitcast.29, ...), custom_call_target="tpu_custom_call" | custom-call | flops 536870912 | bytes 2097152 | tf_op jit(solution)/shard_map/gradients/pallas_call | solution.py:327
  120.8 8.4 %all-to-all-start.3 = ((f32[8,128,128]{2,1,0:T(8,128)}), f32[8,128,128]{2,1,0:T(8,128)S(1)}, u32[]{:S(2)}, u32[]{:S(2)}) async-start(f32[8,128,128]{2,1,0:T(8,128)} %bitcast.8), calls=%async_computation.3 | async-start | bytes 1048576 | tf_op jit(solution)/shard_map/all_to_all | solution.py:364
  129.2 9.3 %all-to-all-done.3.parts_ref = f32[8,128,128]{2,1,0:T(8,128)S(1)} async-done(((f32[8,128,128]{2,1,0:T(8,128)}), f32[8,128,128]{2,1,0:T(8,128)S(1)}, u32[]{:S(2)}, u32[]{:S(2)}) %all-to-all-start.3) | async-done | bytes 524320 | tf_op jit(solution)/shard_map/all_to_all | solution.py:364
  139.3 3.4 %all-to-all-start.4 = ((f32[4,128,128]{2,1,0:T(8,128)}), f32[4,128,128]{2,1,0:T(8,128)S(1)}, u32[]{:S(2)}, u32[]{:S(2)}) async-start(f32[4,128,128]{2,1,0:T(8,128)} %sum_copies.2), calls=%async_computation.4 | async-start | bytes 524288 | tf_op jit(solution)/shard_map/all_to_all | solution.py:364
  142.7 3.5 %gradients.5 = f32[2,4,128,128]{3,2,1,0:T(8,128)S(1)} custom-call(s32[1]{0:T(128)} %bitcast.mine_ref.half_ref, f32[8,16,1024]{2,1,0:T(8,128)S(1)} %all-to-all-done.1.parts_ref, f32[16,2048]{1,0:T(8,128)} %get-tuple-element.13.logit_ref, f32[32,1,2176]{2,1,0:T(1,128)S(1)} %all_to_all.30.stats_ref.stat_ref, bf16[1024,128]{1,0:T(8,128)(2,1)S(1)} %bitcast.30, ...), custom_call_target="tpu_custom_call" | custom-call | flops 536870912 | bytes 2097152 | tf_op jit(solution)/shard_map/gradients/pallas_call | solution.py:327
  148.5 2.8 %all-to-all-done.4.parts_ref = f32[4,128,128]{2,1,0:T(8,128)S(1)} async-done(((f32[4,128,128]{2,1,0:T(8,128)}), f32[4,128,128]{2,1,0:T(8,128)S(1)}, u32[]{:S(2)}, u32[]{:S(2)}) %all-to-all-start.4) | async-done | bytes 262176 | tf_op jit(solution)/shard_map/all_to_all | solution.py:364
  152.1 6.1 %all-to-all-start.5 = ((f32[8,128,128]{2,1,0:T(8,128)}), f32[8,128,128]{2,1,0:T(8,128)S(1)}, u32[]{:S(2)}, u32[]{:S(2)}) async-start(f32[8,128,128]{2,1,0:T(8,128)} %sum_copies.3), calls=%async_computation.5 | async-start | bytes 1048576 | tf_op jit(solution)/shard_map/all_to_all | solution.py:364
  160.2 4.7 %collective-permute-start.5 = (f32[128,128]{1,0:T(8,128)S(1)}, f32[128,128]{1,0:T(8,128)S(1)}, u32[]{:S(2)}, u32[]{:S(2)}) collective-permute-start(f32[128,128]{1,0:T(8,128)S(1)} %get-tuple-element.18), channel_id=1, source_target_pairs={{0,128},{64,192},{128,0},{192,64},{1,129},{65,193},{129,1},{193,65... | collective-permute-start | bytes 196616 | tf_op jit(solution)/shard_map/ppermute | solution.py:374
  165.0 4.7 %collective-permute-start.4 = (f32[128,128]{1,0:T(8,128)S(1)}, f32[128,128]{1,0:T(8,128)S(1)}, u32[]{:S(2)}, u32[]{:S(2)}) collective-permute-start(f32[128,128]{1,0:T(8,128)S(1)} %get-tuple-element.16), channel_id=1, source_target_pairs={{0,64},{64,0},{128,192},{192,128},{1,65},{65,1},{129,193},{193,129... | collective-permute-start | bytes 196616 | tf_op jit(solution)/shard_map/ppermute | solution.py:374
  169.7 4.5 %collective-permute-done.4 = f32[128,128]{1,0:T(8,128)S(1)} collective-permute-done((f32[128,128]{1,0:T(8,128)S(1)}, f32[128,128]{1,0:T(8,128)S(1)}, u32[]{:S(2)}, u32[]{:S(2)}) %collective-permute-start.4) | collective-permute-done | bytes 65568 | tf_op jit(solution)/shard_map/ppermute | solution.py:374
  (32 shorter events, 14.2 us)
Async XLA Ops:
  1.6 14.6 %copy-start = (bf16[2048,128]{1,0:T(8,128)(2,1)S(1)}, bf16[2048,128]{1,0:T(8,128)(2,1)}, u32[]{:S(2)}) copy-start(bf16[2048,128]{1,0:T(8,128)(2,1)} %k_ref.7) | copy-start | bytes 1572868
  1.6 14.6 %copy-start.1 = (bf16[16,64,128]{2,1,0:T(8,128)(2,1)S(1)}, bf16[16,64,128]{2,1,0:T(8,128)(2,1)}, u32[]{:S(2)}) copy-start(bf16[16,64,128]{2,1,0:T(8,128)(2,1)} %param.9) | copy-start | bytes 786436
  1.7 14.6 %copy-start.2 = (f32[16,64]{1,0:T(8,128)S(1)}, f32[16,64]{1,0:T(8,128)}, u32[]{:S(2)}) copy-start(f32[16,64]{1,0:T(8,128)} %w_ref.7) | copy-start | bytes 12292
  49.4 14.9 %collective-permute-start.1 = (f32[128,1024]{1,0:T(8,128)S(1)}, f32[128,1024]{1,0:T(8,128)S(1)}, u32[]{:S(2)}, u32[]{:S(2)}) collective-permute-start(f32[128,1024]{1,0:T(8,128)S(1)} %head_share.6), channel_id=1, source_target_pairs={{0,256},{256,0},{1,257},{257,1},{2,258},{258,2},{3,259},{259,3},{4... | collective-permute-start | bytes 1572872 | tf_op jit(solution)/shard_map/ppermute | solution.py:400
  65.3 31.1 %all-to-all-start.2 = ((f32[8,16,1024]{2,1,0:T(8,128)}), f32[8,16,1024]{2,1,0:T(8,128)}, u32[]{:S(2)}, u32[]{:S(2)}) async-start(f32[8,16,1024]{2,1,0:T(8,128)} %bitcast.31), calls=%async_computation.2 | async-start | bytes 1048576 | tf_op jit(solution)/shard_map/all_to_all | solution.py:364
  81.7 13.8 %collective-permute-start = (f32[128,1024]{1,0:T(8,128)S(1)}, f32[128,1024]{1,0:T(8,128)S(1)}, u32[]{:S(2)}, u32[]{:S(2)}) collective-permute-start(f32[128,1024]{1,0:T(8,128)S(1)} %head_share.4), channel_id=1, source_target_pairs={{0,256},{256,0},{1,257},{257,1},{2,258},{258,2},{3,259},{259,3},{4... | collective-permute-start | bytes 1572872 | tf_op jit(solution)/shard_map/ppermute | solution.py:400
  90.4 12.3 %copy-start.3 = (f32[16,64]{1,0:T(8,128)S(1)}, f32[16,64]{1,0:T(8,128)}, u32[]{:S(2)}) copy-start(f32[16,64]{1,0:T(8,128)} %w_ref.7) | copy-start | bytes 12292
  96.3 20.9 %all-to-all-start.1 = ((f32[8,16,1024]{2,1,0:T(8,128)}), f32[8,16,1024]{2,1,0:T(8,128)S(1)}, u32[]{:S(2)}, u32[]{:S(2)}) async-start(f32[8,16,1024]{2,1,0:T(8,128)} %bitcast.6), calls=%async_computation.1 | async-start | bytes 1048576 | tf_op jit(solution)/shard_map/all_to_all | solution.py:364
  106.3 39.8 %collective-permute-start.2 = (f32[2,4,128,128]{3,2,1,0:T(8,128)S(1)}, f32[2,4,128,128]{3,2,1,0:T(8,128)S(1)}, u32[]{:S(2)}, u32[]{:S(2)}) collective-permute-start(f32[2,4,128,128]{3,2,1,0:T(8,128)S(1)} %get-tuple-element.15), channel_id=1, source_target_pairs={{0,256},{256,0},{1,257},{257,1},{2,258},{258,2},{3,259},{259,3},{4... | collective-permute-start | bytes 1572872 | tf_op jit(solution)/shard_map/ppermute | solution.py:417
  120.8 17.8 %all-to-all-start.3 = ((f32[8,128,128]{2,1,0:T(8,128)}), f32[8,128,128]{2,1,0:T(8,128)S(1)}, u32[]{:S(2)}, u32[]{:S(2)}) async-start(f32[8,128,128]{2,1,0:T(8,128)} %bitcast.8), calls=%async_computation.3 | async-start | bytes 1048576 | tf_op jit(solution)/shard_map/all_to_all | solution.py:364
  139.3 12.0 %all-to-all-start.4 = ((f32[4,128,128]{2,1,0:T(8,128)}), f32[4,128,128]{2,1,0:T(8,128)S(1)}, u32[]{:S(2)}, u32[]{:S(2)}) async-start(f32[4,128,128]{2,1,0:T(8,128)} %sum_copies.2), calls=%async_computation.4 | async-start | bytes 524288 | tf_op jit(solution)/shard_map/all_to_all | solution.py:364
  146.3 11.9 %collective-permute-start.3 = (f32[4,128,128]{2,1,0:T(8,128)S(1)}, f32[4,128,128]{2,1,0:T(8,128)S(1)}, u32[]{:S(2)}, u32[]{:S(2)}) collective-permute-start(f32[4,128,128]{2,1,0:T(8,128)S(1)} %dynamic-slice_bitcast_fusion), channel_id=1, source_target_pairs={{0,32},{32,0},{1,33},{33,1},{2,34},{34,2},{3,35},{35,3},{4,36},{36... | collective-permute-start | bytes 786440 | tf_op jit(solution)/shard_map/ppermute | solution.py:374
  152.1 22.8 %all-to-all-start.5 = ((f32[8,128,128]{2,1,0:T(8,128)}), f32[8,128,128]{2,1,0:T(8,128)S(1)}, u32[]{:S(2)}, u32[]{:S(2)}) async-start(f32[8,128,128]{2,1,0:T(8,128)} %sum_copies.3), calls=%async_computation.5 | async-start | bytes 1048576 | tf_op jit(solution)/shard_map/all_to_all | solution.py:364
  158.3 11.4 %collective-permute-start.6 = (f32[128,128]{1,0:T(8,128)S(1)}, f32[128,128]{1,0:T(8,128)S(1)}, u32[]{:S(2)}, u32[]{:S(2)}) collective-permute-start(f32[128,128]{1,0:T(8,128)S(1)} %get-tuple-element.17), channel_id=1, source_target_pairs={{0,192},{64,128},{128,64},{192,0},{1,193},{65,129},{129,65},{193,1... | collective-permute-start | bytes 196616 | tf_op jit(solution)/shard_map/ppermute | solution.py:374
  160.2 9.5 %collective-permute-start.5 = (f32[128,128]{1,0:T(8,128)S(1)}, f32[128,128]{1,0:T(8,128)S(1)}, u32[]{:S(2)}, u32[]{:S(2)}) collective-permute-start(f32[128,128]{1,0:T(8,128)S(1)} %get-tuple-element.18), channel_id=1, source_target_pairs={{0,128},{64,192},{128,0},{192,64},{1,129},{65,193},{129,1},{193,65... | collective-permute-start | bytes 196616 | tf_op jit(solution)/shard_map/ppermute | solution.py:374
  165.0 9.3 %collective-permute-start.4 = (f32[128,128]{1,0:T(8,128)S(1)}, f32[128,128]{1,0:T(8,128)S(1)}, u32[]{:S(2)}, u32[]{:S(2)}) collective-permute-start(f32[128,128]{1,0:T(8,128)S(1)} %get-tuple-element.16), channel_id=1, source_target_pairs={{0,64},{64,0},{128,192},{192,128},{1,65},{65,1},{129,193},{193,129... | collective-permute-start | bytes 196616 | tf_op jit(solution)/shard_map/ppermute | solution.py:374

commit v5 on v3

--- a/solution.py
+++ b/solution.py
@@ -11,6 +11,7 @@
 
 HEADS = 128
 LANES = 128
+TILE = 512
 KEY = ("x", "yh", "core")
 HEAD = ("yl", "zh", "zl")
 RING = ("zh", "zl")
@@ -28,13 +29,17 @@
     return pltpu.with_memory_space_constraint(x, pltpu.HBM)
 
 
+def in_vmem(x):
+    return pltpu.with_memory_space_constraint(x, pltpu.VMEM)
+
+
 def dot(a, b, dims):
     return lax.dot_general(a, b, dims, preferred_element_type=jnp.float32)
 
 
-def params(semantics=("arbitrary",)):
+def params(mebibytes=24):
     return pltpu.CompilerParams(
-        dimension_semantics=semantics, vmem_limit_bytes=48 * 1024 * 1024
+        dimension_semantics=("arbitrary",), vmem_limit_bytes=mebibytes * 1024 * 1024
     )
 
 
@@ -43,7 +48,7 @@
     heads = pl.num_programs(0)
     keys = k_ref.shape[1]
     q = jnp.transpose(q_ref[0])
-    rows_ref[0] = q
+    rows_ref[head] = q
     rows = q.shape[0]
     pos = jnp.broadcast_to(pos_ref[...], (rows, LANES))
     ids = lax.broadcasted_iota(jnp.int32, (rows, LANES), 1)
@@ -85,11 +90,11 @@
         ],
         out_specs=(
             pl.BlockSpec((rows // LANES, heads, LANES), lambda h: (0, 0, 0)),
-            pl.BlockSpec((1, rows, width), lambda h: (h, 0, 0)),
+            pl.BlockSpec(memory_space=pltpu.VMEM),
         ),
         out_shape=(
             jax.ShapeDtypeStruct((rows // LANES, heads, LANES), jnp.float32),
-            pltpu.HBM((heads, rows, width), q.dtype),
+            pltpu.VMEM((heads, rows, width), q.dtype),
         ),
         scratch_shapes=[pltpu.VMEM((rows, LANES), jnp.float32)],
         compiler_params=params(),
@@ -97,7 +102,7 @@
             flops=2 * heads * rows * keys * width, transcendentals=heads * rows * keys, bytes_accessed=6 << 20
         ),
         name="score_stats",
-    )(rel_pos.reshape(rows, 1), in_hbm(q), k)
+    )(rel_pos.reshape(rows, 1), in_hbm(q), in_hbm(k))
 
 
 def combined(stats):
@@ -105,10 +110,11 @@
     return high + jnp.log2(jnp.sum(jnp.exp2(stats - high[None]), axis=0))
 
 
-def head_share_kernel(half_ref, stats_ref, pos_ref, q_ref, k_ref, out_ref, col_ref):
-    heads, rows, _ = q_ref.shape
-    tile = k_ref.shape[1]
+def head_share_kernel(mine_ref, stats_ref, pos_ref, q_ref, k_ref, out_ref, col_ref, *, other_rows, other_keys):
     step = pl.program_id(0)
+    heads = q_ref.shape[0]
+    rows, tile = out_ref.shape
+    mine = mine_ref[0]
 
     @pl.when(step == 0)
     def _():
@@ -116,44 +122,51 @@
         lines = [line[:, head * rows : (head + 1) * rows] for head in range(heads)]
         col_ref[:, :heads] = jnp.transpose(jnp.concatenate(lines, axis=0))
 
+    own = pl.ds(pl.multiple_of((1 - mine if other_rows else mine) * rows, rows), rows)
     k = k_ref[...]
     total = None
     for head in range(heads):
-        scores = dot(q_ref[head], k, NN)
+        scores = dot(q_ref[head, own, :], k, NN)
         part = jnp.exp2(scores * attn_scale - col_ref[:, head : head + 1])
         total = part if total is None else total + part
-    start = (half_ref[1] * pl.num_programs(0) + step) * tile
-    ids = lax.broadcasted_iota(jnp.int32, total.shape, 1) + start
+    half = 1 - mine if other_keys else mine
+    ids = lax.broadcasted_iota(jnp.int32, total.shape, 1) + (half * pl.num_programs(0) + step) * tile
     out_ref[...] = jnp.where(ids <= pos_ref[...], total, 0.0)
 
 
-def head_share(half, stats, rel_pos, q, k):
+def head_share(mine, other_rows, other_keys, stats, rel_pos, q, k):
     heads, rows, width = q.shape
     rows //= 2
     keys = k.shape[1] // 2
-    tile = 256
-    steps = keys // tile
+    steps = keys // TILE
+
+    def rows_half(mine):
+        return 1 - mine[0] if other_rows else mine[0]
+
+    def keys_half(mine):
+        return 1 - mine[0] if other_keys else mine[0]
+
     return pl.pallas_call(
-        head_share_kernel,
+        functools.partial(head_share_kernel, other_rows=other_rows, other_keys=other_keys),
         grid_spec=pltpu.PrefetchScalarGridSpec(
             num_scalar_prefetch=1,
             grid=(steps,),
             in_specs=[
-                pl.BlockSpec((stats.shape[0], 1, heads * rows), lambda t, half: (0, 0, half[0])),
-                pl.BlockSpec((rows, 1), lambda t, half: (half[0], 0)),
-                pl.BlockSpec((heads, rows, width), lambda t, half: (0, half[0], 0)),
-                pl.BlockSpec((width, tile), lambda t, half: (0, half[1] * steps + t)),
+                pl.BlockSpec((stats.shape[0], 1, heads * rows), lambda t, mine: (0, 0, rows_half(mine))),
+                pl.BlockSpec((rows, 1), lambda t, mine: (rows_half(mine), 0)),
+                pl.BlockSpec(memory_space=pltpu.VMEM),
+                pl.BlockSpec((width, TILE), lambda t, mine: (0, keys_half(mine) * steps + t)),
             ],
-            out_specs=pl.BlockSpec((rows, tile), lambda t, half: (0, t)),
+            out_specs=pl.BlockSpec((rows, TILE), lambda t, mine: (0, t)),
             scratch_shapes=[pltpu.VMEM((rows, LANES), jnp.float32)],
         ),
         out_shape=jax.ShapeDtypeStruct((rows, keys), jnp.float32),
-        compiler_params=params(),
+        compiler_params=params(12),
         cost_estimate=pl.CostEstimate(
             flops=2 * heads * rows * keys * width, transcendentals=heads * rows * keys, bytes_accessed=3 << 20
         ),
         name="head_share",
-    )(half, stats, rel_pos.reshape(2 * rows, 1), in_hbm(q), k)
+    )(mine, stats, rel_pos.reshape(2 * rows, 1), in_vmem(q), in_hbm(k))
 
 
 def diagonal(rows):
@@ -200,7 +213,7 @@
             pltpu.HBM((rows, keys), jnp.float32),
             pltpu.HBM((copies, 1, own.size + LANES), jnp.float32),
         ),
-        compiler_params=pltpu.CompilerParams(vmem_limit_bytes=48 * 1024 * 1024),
+        compiler_params=pltpu.CompilerParams(vmem_limit_bytes=16 * 1024 * 1024),
         cost_estimate=pl.CostEstimate(
             flops=2 * rows * iheads * keys * width, transcendentals=rows * keys, bytes_accessed=1 << 20
         ),
@@ -255,7 +268,7 @@
             rows_ref[...] += part
 
 
-def gradients(half, parts, logits, stats, q, w, k, before, count, sizes, row_part, key_part):
+def gradients(mine, other_keys, parts, logits, stats, q, w, k, before, count, sizes, row_part, key_part):
     rows, iheads, width = q.shape
     keys = parts.shape[2]
     flat = rows * iheads
@@ -264,14 +277,18 @@
     far = nf // 2
     tile = far * nz * share
     last = stats.shape[2] // LANES - 1
+
+    def part(mine):
+        return 1 - mine[0] if other_keys else mine[0]
+
     operands = [parts, logits, stats, q.reshape(flat, width), w, k]
     in_specs = [
         pl.BlockSpec((parts.shape[0], rows, tile), lambda t, half: (0, 0, t)),
-        pl.BlockSpec((rows, tile), lambda t, half: (0, half[0] * 2 + t)),
+        pl.BlockSpec((rows, tile), lambda t, mine: (0, part(mine) * 2 + t)),
         pl.BlockSpec((stats.shape[0], 1, LANES), lambda t, half: (0, 0, last)),
         pl.BlockSpec((flat, width), lambda t, half: (0, 0)),
         pl.BlockSpec((rows, iheads), lambda t, half: (0, 0)),
-        pl.BlockSpec((tile, width), lambda t, half: (half[0] * 2 + t, 0)),
+        pl.BlockSpec((tile, width), lambda t, mine: (part(mine) * 2 + t, 0)),
     ]
     row_spec = pl.BlockSpec((flat, width), lambda t, half: (0, 0))
     if before is not None:
@@ -303,7 +320,7 @@
             bytes_accessed=2 << 20,
         ),
         name="gradients",
-    )(half, parts, in_hbm(logits), *operands[2:])
+    )(mine, parts, in_hbm(logits), *operands[2:])
 
 
 def sum_copies_kernel(parts_ref, out_ref):
@@ -340,6 +357,7 @@
     rows = index_query.shape[0]
     rel_pos = query_pos - lax.axis_index(KEY) * keys
     row_pos = lax.dynamic_slice_in_dim(rel_pos, lax.axis_index(HEAD) * rows, rows, 0)
+    mine = in_hbm(lax.axis_index("yl").astype(jnp.int32).reshape(1))
     q = jnp.swapaxes(mla_query, 1, 2)
     k = jnp.swapaxes(latent_keys, 0, 1)
     sizes = [lax.axis_size(axis) for axis in HEAD]
@@ -348,26 +366,23 @@
         row_pos, index_query, index_weights, index_keys, own_stats, lax.axis_size(KEY)
     )
     stats = exchanged(own_stats, KEY)
-    mine = lax.axis_index("yl")
-    other = 1 - mine
     swap = [(0, 1), (1, 0)]
-
-    def pick(*halves):
-        return jnp.stack(halves).astype(jnp.int32)
 
     grad_rows, grad_keys = None, []
     shares = {}
-    for name, rows_half, halves in (("sent", other, (mine, other)), ("kept", mine, (other, mine))):
-        for turn, half in enumerate(halves):
-            shares[name, turn] = head_share(pick(rows_half, half), stats, rel_pos, q_rows, k)
-    for turn, half in enumerate((other, mine)):
+    for name, first in (("sent", False), ("kept", True)):
+        for turn in range(2):
+            shares[name, turn] = head_share(
+                mine, name == "sent", first == (turn == 0), stats, rel_pos, q_rows, k
+            )
+    for turn in range(2):
         near = lax.ppermute(shares["sent", turn], "yl", swap)
         near = (near + shares["kept", turn]).reshape(-1, rows, keys // 2)
         parts = exchanged(near, RING)
 
         def grads(rows_before, row_part, key_part):
             return gradients(
-                pick(half), parts, logits, stats, index_query, index_weights, index_keys, rows_before,
+                mine, turn == 0, parts, logits, stats, index_query, index_weights, index_keys, rows_before,
                 lax.axis_size(KEY) * keys, sizes, row_part, key_part,
             )
 
@@ -385,7 +400,7 @@
     side = lax.axis_size(SIDE)
     total = exchanged(grad_rows.reshape(side, -1, grad_rows.shape[1]), SIDE)
     total = exchanged(sum_copies(total, lax.axis_size("yh")), "yh")
-    query_grads = exchanged(sum_copies(total, side), SIDE).reshape(index_query.shape)
+    query_grads = exchanged(sum_copies(total, side).reshape(index_query.shape), SIDE)
     return (query_grads, key_grads)
 
 

time: 175 us -> 169 us (0.966)
  blocking collectives: 0 us -> 24.7 us
  starting transfers between devices: 66.1 us -> 54.6 us
  waiting for transfers between devices: 51.8 us -> 42.5 us
  Pallas kernels: 46.8 us -> 41.1 us
  local copies, waits for them, and re-layouts: 3.4 us -> 1.18 us
    all_to_all x0 -> x1, blocking collectives: none -> 24.7 us  [exchanged(): return lax.all_to_all(parts, axis, split_axis=0, concat_axis=0, tiled=True)]
    all_to_all x6 -> x5, waiting for transfers between devices: 33.3 us -> 20.4 us  [exchanged(): return lax.all_to_all(parts, axis, split_axis=0, concat_axis=0, tiled=True)]
    all_to_all x6 -> x5, starting transfers between devices: 45.5 us -> 34.1 us  [exchanged(): return lax.all_to_all(parts, axis, split_axis=0, concat_axis=0, tiled=True)]
    pallas_call x4, Pallas kernels: 19.6 us -> 13.9 us  [head_share(): pl.pallas_call(functools.partial(head_share_kernel, other_rows=other_rows...]
    ppermute x2, waiting for transfers between devices: 14 us -> 17.6 us  [shards(): near = lax.ppermute(shares['sent', turn], 'yl', swap)]
    unnamed x17 -> x11, local copies, waits for them, and re-layouts: 3.05 us -> 0.83 us
  transfers between devices with their start and end apart: 13 -> 12, of which waited for: 7 -> 6; matrix products, arithmetic and copies ran while one was open for 2% -> 1% of each run, Pallas kernels for 16% -> 13%
where the time goes in v5:
time: 169 us; the launch traced here: 168 us
  starting transfers between devices  54.6 us (32%)
  waiting for transfers between devices  42.5 us (25%)
  Pallas kernels  41.1 us (24%)
  blocking collectives  24.7 us (15%)
  other arithmetic  3.16 us (2%)
    all_to_all x5, starting transfers between devices, exchanged(): return lax.all_to_all(parts, axis, split_axis=0, concat_axis=0, tiled=True)  34.1 us
    all_to_all x1, blocking collectives, exchanged(): return lax.all_to_all(parts, axis, split_axis=0, concat_axis=0, tiled=True)  24.7 us
    all_to_all x5, waiting for transfers between devices, exchanged(): return lax.all_to_all(parts, axis, split_axis=0, concat_axis=0, tiled=True)  20.4 us
    ppermute x2, waiting for transfers between devices, shards(): near = lax.ppermute(shares['sent', turn], 'yl', swap)  17.6 us
    pallas_call x4, Pallas kernels, head_share(): pl.pallas_call(functools.partial(head_share_kernel, other_rows=other_rows...  13.9 us
    ppermute x4, starting transfers between devices, at_owner(): got.append(lax.ppermute(part, axis, [(i, i ^ hop) for i in range(size)]))  13.6 us
    pallas_call x1, Pallas kernels, score_stats(): pl.pallas_call(functools.partial(score_stats_kernel, tile=512), grid=(hea...  12.8 us
    pallas_call x3, Pallas kernels, gradients(): pl.pallas_call(functools.partial(gradients_kernel, count=float(count), be...  10.6 us
  transfers between devices with their start and end apart: 12, of which 6 were waited for; matrix products, arithmetic and copies ran while one was open for 1% of the time, Pallas kernels for 13%

profile of v5, /device:TPU:1, one launch (start us, length us, event | category | flops | bytes accessed | tf_op | source)
XLA Modules:
  0.0 168.1 jit_solution(1982647949968257933)
XLA Ops:
  1.7 12.8 %score_stats.1 = (f32[2,8,128]{2,1,0:T(8,128)S(1)}, bf16[8,256,576]{2,1,0:T(8,128)(2,1)S(1)}) custom-call(s32[256,1]{1,0:T(8,128)S(1)} %copy.9.pos_ref, bf16[8,576,256]{2,1,0:T(8,128)(2,1)} %bitcast.38, bf16[576,2048]{1,0:T(8,128)(2,1)} %bitcast.31), custom_call_target="tpu_custom_call" | custom-call | flops 4831838208 | bytes 6291456 | tf_op jit(solution)/shard_map/score_stats/pallas_call | solution.py:83
  16.7 24.7 %all_to_all.30.stats_ref.stat_ref = f32[32,1,2176]{2,1,0:T(1,128)S(1)} all-to-all(f32[32,1,2176]{2,1,0:T(1,128)} %get-tuple-element.9), channel_id=1, replica_groups=mesh['yl'=2,'zh'=4,'zl'=2,'x'=4,'yh'=4,'core'=2] {'x','yh','core'}, dimensions={0} | all-to-all | bytes 557056 | tf_op jit(solution)/shard_map/all_to_all | solution.py:341
  41.4 3.4 %head_share.6 = f32[128,1024]{1,0:T(8,128)S(1)} custom-call(s32[1]{0:T(128)} %bitcast.mine_ref.half_ref, f32[32,1,2176]{2,1,0:T(1,128)S(1)} %all_to_all.30.stats_ref.stat_ref, s32[256,1]{1,0:T(8,128)S(1)} %copy.9.pos_ref, bf16[8,256,576]{2,1,0:T(8,128)(2,1)S(1)} %get-tuple-element.10.q_ref, bf16[576,2048]{1,0:T(8,128)(2,1)} %bitcast.32), custom_call_target="tpu_custom_call" | custom-call | flops 1207959552 | bytes 3145728 | tf_op jit(solution)/shard_map/head_share/pallas_call | solution.py:149
  46.8 3.5 %head_share.7 = f32[128,1024]{1,0:T(8,128)S(1)} custom-call(s32[1]{0:T(128)} %bitcast.mine_ref.half_ref, f32[32,1,2176]{2,1,0:T(1,128)S(1)} %all_to_all.30.stats_ref.stat_ref, s32[256,1]{1,0:T(8,128)S(1)} %copy.9.pos_ref, bf16[8,256,576]{2,1,0:T(8,128)(2,1)S(1)} %get-tuple-element.10.q_ref, bf16[576,2048]{1,0:T(8,128)(2,1)} %bitcast.33), custom_call_target="tpu_custom_call" | custom-call | flops 1207959552 | bytes 3145728 | tf_op jit(solution)/shard_map/head_share/pallas_call | solution.py:149
  50.3 9.5 %collective-permute-done.1 = f32[128,1024]{1,0:T(8,128)S(1)} collective-permute-done((f32[128,1024]{1,0:T(8,128)S(1)}, f32[128,1024]{1,0:T(8,128)S(1)}, u32[]{:S(2)}, u32[]{:S(2)}) %collective-permute-start.1) | collective-permute-done | bytes 524320 | tf_op jit(solution)/shard_map/ppermute | solution.py:379
  60.7 10.0 %all-to-all-start.2 = ((f32[8,16,1024]{2,1,0:T(8,128)}), f32[8,16,1024]{2,1,0:T(8,128)}, u32[]{:S(2)}, u32[]{:S(2)}) async-start(f32[8,16,1024]{2,1,0:T(8,128)} %bitcast.36), calls=%async_computation.2 | async-start | bytes 1048576 | tf_op jit(solution)/shard_map/all_to_all | solution.py:341
  70.7 3.5 %head_share.4 = f32[128,1024]{1,0:T(8,128)S(1)} custom-call(s32[1]{0:T(128)} %bitcast.mine_ref.half_ref, f32[32,1,2176]{2,1,0:T(1,128)S(1)} %all_to_all.30.stats_ref.stat_ref, s32[256,1]{1,0:T(8,128)S(1)} %copy.9.pos_ref, bf16[8,256,576]{2,1,0:T(8,128)(2,1)S(1)} %get-tuple-element.10.q_ref, bf16[576,2048]{1,0:T(8,128)(2,1)} %bitcast.34), custom_call_target="tpu_custom_call" | custom-call | flops 1207959552 | bytes 3145728 | tf_op jit(solution)/shard_map/head_share/pallas_call | solution.py:149
  74.2 2.3 %collective-permute-start = (f32[128,1024]{1,0:T(8,128)S(1)}, f32[128,1024]{1,0:T(8,128)S(1)}, u32[]{:S(2)}, u32[]{:S(2)}) collective-permute-start(f32[128,1024]{1,0:T(8,128)S(1)} %head_share.4), channel_id=1, source_target_pairs={{0,256},{256,0},{1,257},{257,1},{2,258},{258,2},{3,259},{259,3},{4... | collective-permute-start | bytes 1572872 | tf_op jit(solution)/shard_map/ppermute | solution.py:379
  76.5 3.5 %head_share.5 = f32[128,1024]{1,0:T(8,128)S(1)} custom-call(s32[1]{0:T(128)} %bitcast.mine_ref.half_ref, f32[32,1,2176]{2,1,0:T(1,128)S(1)} %all_to_all.30.stats_ref.stat_ref, s32[256,1]{1,0:T(8,128)S(1)} %copy.9.pos_ref, bf16[8,256,576]{2,1,0:T(8,128)(2,1)S(1)} %get-tuple-element.10.q_ref, bf16[576,2048]{1,0:T(8,128)(2,1)} %bitcast.35), custom_call_target="tpu_custom_call" | custom-call | flops 1207959552 | bytes 3145728 | tf_op jit(solution)/shard_map/head_share/pallas_call | solution.py:149
  80.0 8.1 %collective-permute-done = f32[128,1024]{1,0:T(8,128)S(1)} collective-permute-done((f32[128,1024]{1,0:T(8,128)S(1)}, f32[128,1024]{1,0:T(8,128)S(1)}, u32[]{:S(2)}, u32[]{:S(2)}) %collective-permute-start) | collective-permute-done | bytes 524320 | tf_op jit(solution)/shard_map/ppermute | solution.py:379
  88.9 6.2 %all-to-all-start.1 = ((f32[8,16,1024]{2,1,0:T(8,128)}), f32[8,16,1024]{2,1,0:T(8,128)S(1)}, u32[]{:S(2)}, u32[]{:S(2)}) async-start(f32[8,16,1024]{2,1,0:T(8,128)} %bitcast.6), calls=%async_computation.1 | async-start | bytes 1048576 | tf_op jit(solution)/shard_map/all_to_all | solution.py:341
  95.2 3.6 %gradients.3 = (f32[1024,128]{1,0:T(8,128)S(1)}, f32[2,4,128,128]{3,2,1,0:T(8,128)S(1)}) custom-call(s32[1]{0:T(128)} %bitcast.mine_ref.half_ref, f32[8,16,1024]{2,1,0:T(8,128)} %all-to-all-done.2.parts_ref, f32[16,2048]{1,0:T(8,128)} %get-tuple-element.11.logit_ref, f32[32,1,2176]{2,1,0:T(1,128)S(1)} %all_to_all.30.stats_ref.stat_ref, ...), custom_call_target="tpu_custom_call" | custom-call | flops 805306368 | bytes 2097152 | tf_op jit(solution)/shard_map/gradients/pallas_call | solution.py:304
  98.8 2.6 %collective-permute-start.2 = (f32[2,4,128,128]{3,2,1,0:T(8,128)S(1)}, f32[2,4,128,128]{3,2,1,0:T(8,128)S(1)}, u32[]{:S(2)}, u32[]{:S(2)}) collective-permute-start(f32[2,4,128,128]{3,2,1,0:T(8,128)S(1)} %get-tuple-element.13), channel_id=1, source_target_pairs={{0,256},{256,0},{1,257},{257,1},{2,258},{258,2},{3,259},{259,3},{4... | collective-permute-start | bytes 1572872 | tf_op jit(solution)/shard_map/ppermute | solution.py:396
  101.5 8.3 %all-to-all-done.1.parts_ref = f32[8,16,1024]{2,1,0:T(8,128)S(1)} async-done(((f32[8,16,1024]{2,1,0:T(8,128)}), f32[8,16,1024]{2,1,0:T(8,128)S(1)}, u32[]{:S(2)}, u32[]{:S(2)}) %all-to-all-start.1) | async-done | bytes 524320 | tf_op jit(solution)/shard_map/all_to_all | solution.py:341
  109.7 3.6 %gradients.4 = f32[1024,128]{1,0:T(8,128)} custom-call(s32[1]{0:T(128)} %bitcast.mine_ref.half_ref, f32[8,16,1024]{2,1,0:T(8,128)S(1)} %all-to-all-done.1.parts_ref, f32[16,2048]{1,0:T(8,128)} %get-tuple-element.11.logit_ref, f32[32,1,2176]{2,1,0:T(1,128)S(1)} %all_to_all.30.stats_ref.stat_ref, bf16[1024,128]{1,0:T(8,128)(2,1)S(1)} %bitcast.29, ...), custom_call_target="tpu_custom_call" | custom-call | flops 536870912 | bytes 2097152 | tf_op jit(solution)/shard_map/gradients/pallas_call | solution.py:304
  113.3 8.3 %all-to-all-start.3 = ((f32[8,128,128]{2,1,0:T(8,128)}), f32[8,128,128]{2,1,0:T(8,128)S(1)}, u32[]{:S(2)}, u32[]{:S(2)}) async-start(f32[8,128,128]{2,1,0:T(8,128)} %bitcast.8), calls=%async_computation.3 | async-start | bytes 1048576 | tf_op jit(solution)/shard_map/all_to_all | solution.py:341
  121.6 9.3 %all-to-all-done.3.parts_ref = f32[8,128,128]{2,1,0:T(8,128)S(1)} async-done(((f32[8,128,128]{2,1,0:T(8,128)}), f32[8,128,128]{2,1,0:T(8,128)S(1)}, u32[]{:S(2)}, u32[]{:S(2)}) %all-to-all-start.3) | async-done | bytes 524320 | tf_op jit(solution)/shard_map/all_to_all | solution.py:341
  131.7 3.4 %all-to-all-start.4 = ((f32[4,128,128]{2,1,0:T(8,128)}), f32[4,128,128]{2,1,0:T(8,128)S(1)}, u32[]{:S(2)}, u32[]{:S(2)}) async-start(f32[4,128,128]{2,1,0:T(8,128)} %sum_copies.2), calls=%async_computation.4 | async-start | bytes 524288 | tf_op jit(solution)/shard_map/all_to_all | solution.py:341
  135.1 3.5 %gradients.5 = f32[2,4,128,128]{3,2,1,0:T(8,128)S(1)} custom-call(s32[1]{0:T(128)} %bitcast.mine_ref.half_ref, f32[8,16,1024]{2,1,0:T(8,128)S(1)} %all-to-all-done.1.parts_ref, f32[16,2048]{1,0:T(8,128)} %get-tuple-element.11.logit_ref, f32[32,1,2176]{2,1,0:T(1,128)S(1)} %all_to_all.30.stats_ref.stat_ref, bf16[1024,128]{1,0:T(8,128)(2,1)S(1)} %bitcast.30, ...), custom_call_target="tpu_custom_call" | custom-call | flops 536870912 | bytes 2097152 | tf_op jit(solution)/shard_map/gradients/pallas_call | solution.py:304
  140.9 2.8 %all-to-all-done.4.parts_ref = f32[4,128,128]{2,1,0:T(8,128)S(1)} async-done(((f32[4,128,128]{2,1,0:T(8,128)}), f32[4,128,128]{2,1,0:T(8,128)S(1)}, u32[]{:S(2)}, u32[]{:S(2)}) %all-to-all-start.4) | async-done | bytes 262176 | tf_op jit(solution)/shard_map/all_to_all | solution.py:341
  144.5 6.1 %all-to-all-start.5 = ((f32[16,64,128]{2,1,0:T(8,128)}), f32[16,64,128]{2,1,0:T(8,128)S(1)}, u32[]{:S(2)}, u32[]{:S(2)}) async-start(f32[16,64,128]{2,1,0:T(8,128)} %bitcast.9), calls=%async_computation.5 | async-start | bytes 1048576 | tf_op jit(solution)/shard_map/all_to_all | solution.py:341
  152.8 4.6 %collective-permute-start.5 = (f32[128,128]{1,0:T(8,128)S(1)}, f32[128,128]{1,0:T(8,128)S(1)}, u32[]{:S(2)}, u32[]{:S(2)}) collective-permute-start(f32[128,128]{1,0:T(8,128)S(1)} %get-tuple-element.16), channel_id=1, source_target_pairs={{0,128},{64,192},{128,0},{192,64},{1,129},{65,193},{129,1},{193,65... | collective-permute-start | bytes 196616 | tf_op jit(solution)/shard_map/ppermute | solution.py:351
  157.4 4.7 %collective-permute-start.4 = (f32[128,128]{1,0:T(8,128)S(1)}, f32[128,128]{1,0:T(8,128)S(1)}, u32[]{:S(2)}, u32[]{:S(2)}) collective-permute-start(f32[128,128]{1,0:T(8,128)S(1)} %get-tuple-element.14), channel_id=1, source_target_pairs={{0,64},{64,0},{128,192},{192,128},{1,65},{65,1},{129,193},{193,129... | collective-permute-start | bytes 196616 | tf_op jit(solution)/shard_map/ppermute | solution.py:351
  162.2 4.5 %collective-permute-done.4 = f32[128,128]{1,0:T(8,128)S(1)} collective-permute-done((f32[128,128]{1,0:T(8,128)S(1)}, f32[128,128]{1,0:T(8,128)S(1)}, u32[]{:S(2)}, u32[]{:S(2)}) %collective-permute-start.4) | collective-permute-done | bytes 65568 | tf_op jit(solution)/shard_map/ppermute | solution.py:351
  (34 shorter events, 14.3 us)
Async XLA Ops:
  1.6 12.8 %copy-start = (bf16[2048,128]{1,0:T(8,128)(2,1)S(1)}, bf16[2048,128]{1,0:T(8,128)(2,1)}, u32[]{:S(2)}) copy-start(bf16[2048,128]{1,0:T(8,128)(2,1)} %k_ref.7) | copy-start | bytes 1572868
  1.6 12.8 %copy-start.1 = (bf16[16,64,128]{2,1,0:T(8,128)(2,1)S(1)}, bf16[16,64,128]{2,1,0:T(8,128)(2,1)}, u32[]{:S(2)}) copy-start(bf16[16,64,128]{2,1,0:T(8,128)(2,1)} %param.9) | copy-start | bytes 786436
  1.7 12.8 %copy-start.3 = (f32[16,64]{1,0:T(8,128)S(1)}, f32[16,64]{1,0:T(8,128)}, u32[]{:S(2)}) copy-start(f32[16,64]{1,0:T(8,128)} %w_ref.7) | copy-start | bytes 12292
  44.8 15.0 %collective-permute-start.1 = (f32[128,1024]{1,0:T(8,128)S(1)}, f32[128,1024]{1,0:T(8,128)S(1)}, u32[]{:S(2)}, u32[]{:S(2)}) collective-permute-start(f32[128,1024]{1,0:T(8,128)S(1)} %head_share.6), channel_id=1, source_target_pairs={{0,256},{256,0},{1,257},{257,1},{2,258},{258,2},{3,259},{259,3},{4... | collective-permute-start | bytes 1572872 | tf_op jit(solution)/shard_map/ppermute | solution.py:379
  60.7 28.3 %all-to-all-start.2 = ((f32[8,16,1024]{2,1,0:T(8,128)}), f32[8,16,1024]{2,1,0:T(8,128)}, u32[]{:S(2)}, u32[]{:S(2)}) async-start(f32[8,16,1024]{2,1,0:T(8,128)} %bitcast.36), calls=%async_computation.2 | async-start | bytes 1048576 | tf_op jit(solution)/shard_map/all_to_all | solution.py:341
  74.2 13.9 %collective-permute-start = (f32[128,1024]{1,0:T(8,128)S(1)}, f32[128,1024]{1,0:T(8,128)S(1)}, u32[]{:S(2)}, u32[]{:S(2)}) collective-permute-start(f32[128,1024]{1,0:T(8,128)S(1)} %head_share.4), channel_id=1, source_target_pairs={{0,256},{256,0},{1,257},{257,1},{2,258},{258,2},{3,259},{259,3},{4... | collective-permute-start | bytes 1572872 | tf_op jit(solution)/shard_map/ppermute | solution.py:379
  80.0 15.2 %copy-start.2 = (bf16[16,64,128]{2,1,0:T(8,128)(2,1)S(1)}, bf16[16,64,128]{2,1,0:T(8,128)(2,1)}, u32[]{:S(2)}) copy-start(bf16[16,64,128]{2,1,0:T(8,128)(2,1)} %param.9) | copy-start | bytes 786436
  80.0 15.2 %copy-start.4 = (f32[16,64]{1,0:T(8,128)S(1)}, f32[16,64]{1,0:T(8,128)}, u32[]{:S(2)}) copy-start(f32[16,64]{1,0:T(8,128)} %w_ref.7) | copy-start | bytes 12292
  88.9 20.8 %all-to-all-start.1 = ((f32[8,16,1024]{2,1,0:T(8,128)}), f32[8,16,1024]{2,1,0:T(8,128)S(1)}, u32[]{:S(2)}, u32[]{:S(2)}) async-start(f32[8,16,1024]{2,1,0:T(8,128)} %bitcast.6), calls=%async_computation.1 | async-start | bytes 1048576 | tf_op jit(solution)/shard_map/all_to_all | solution.py:341
  98.8 39.8 %collective-permute-start.2 = (f32[2,4,128,128]{3,2,1,0:T(8,128)S(1)}, f32[2,4,128,128]{3,2,1,0:T(8,128)S(1)}, u32[]{:S(2)}, u32[]{:S(2)}) collective-permute-start(f32[2,4,128,128]{3,2,1,0:T(8,128)S(1)} %get-tuple-element.13), channel_id=1, source_target_pairs={{0,256},{256,0},{1,257},{257,1},{2,258},{258,2},{3,259},{259,3},{4... | collective-permute-start | bytes 1572872 | tf_op jit(solution)/shard_map/ppermute | solution.py:396
  113.3 17.7 %all-to-all-start.3 = ((f32[8,128,128]{2,1,0:T(8,128)}), f32[8,128,128]{2,1,0:T(8,128)S(1)}, u32[]{:S(2)}, u32[]{:S(2)}) async-start(f32[8,128,128]{2,1,0:T(8,128)} %bitcast.8), calls=%async_computation.3 | async-start | bytes 1048576 | tf_op jit(solution)/shard_map/all_to_all | solution.py:341
  131.7 12.0 %all-to-all-start.4 = ((f32[4,128,128]{2,1,0:T(8,128)}), f32[4,128,128]{2,1,0:T(8,128)S(1)}, u32[]{:S(2)}, u32[]{:S(2)}) async-start(f32[4,128,128]{2,1,0:T(8,128)} %sum_copies.2), calls=%async_computation.4 | async-start | bytes 524288 | tf_op jit(solution)/shard_map/all_to_all | solution.py:341
  138.7 11.9 %collective-permute-start.3 = (f32[4,128,128]{2,1,0:T(8,128)S(1)}, f32[4,128,128]{2,1,0:T(8,128)S(1)}, u32[]{:S(2)}, u32[]{:S(2)}) collective-permute-start(f32[4,128,128]{2,1,0:T(8,128)S(1)} %dynamic-slice_bitcast_fusion), channel_id=1, source_target_pairs={{0,32},{32,0},{1,33},{33,1},{2,34},{34,2},{3,35},{35,3},{4,36},{36... | collective-permute-start | bytes 786440 | tf_op jit(solution)/shard_map/ppermute | solution.py:351
  144.5 22.8 %all-to-all-start.5 = ((f32[16,64,128]{2,1,0:T(8,128)}), f32[16,64,128]{2,1,0:T(8,128)S(1)}, u32[]{:S(2)}, u32[]{:S(2)}) async-start(f32[16,64,128]{2,1,0:T(8,128)} %bitcast.9), calls=%async_computation.5 | async-start | bytes 1048576 | tf_op jit(solution)/shard_map/all_to_all | solution.py:341
  150.7 11.4 %collective-permute-start.6 = (f32[128,128]{1,0:T(8,128)S(1)}, f32[128,128]{1,0:T(8,128)S(1)}, u32[]{:S(2)}, u32[]{:S(2)}) collective-permute-start(f32[128,128]{1,0:T(8,128)S(1)} %get-tuple-element.15), channel_id=1, source_target_pairs={{0,192},{64,128},{128,64},{192,0},{1,193},{65,129},{129,65},{193,1... | collective-permute-start | bytes 196616 | tf_op jit(solution)/shard_map/ppermute | solution.py:351
  152.8 9.4 %collective-permute-start.5 = (f32[128,128]{1,0:T(8,128)S(1)}, f32[128,128]{1,0:T(8,128)S(1)}, u32[]{:S(2)}, u32[]{:S(2)}) collective-permute-start(f32[128,128]{1,0:T(8,128)S(1)} %get-tuple-element.16), channel_id=1, source_target_pairs={{0,128},{64,192},{128,0},{192,64},{1,129},{65,193},{129,1},{193,65... | collective-permute-start | bytes 196616 | tf_op jit(solution)/shard_map/ppermute | solution.py:351
  157.4 9.3 %collective-permute-start.4 = (f32[128,128]{1,0:T(8,128)S(1)}, f32[128,128]{1,0:T(8,128)S(1)}, u32[]{:S(2)}, u32[]{:S(2)}) collective-permute-start(f32[128,128]{1,0:T(8,128)S(1)} %get-tuple-element.14), channel_id=1, source_target_pairs={{0,64},{64,0},{128,192},{192,128},{1,65},{65,1},{129,193},{193,129... | collective-permute-start | bytes 196616 | tf_op jit(solution)/shard_map/ppermute | solution.py:351

commit v6 on v5

--- a/solution.py
+++ b/solution.py
@@ -43,60 +43,78 @@
     )
 
 
-def score_stats_kernel(pos_ref, q_ref, k_ref, out_ref, rows_ref, col_ref, *, tile):
-    head = pl.program_id(0)
-    heads = pl.num_programs(0)
-    keys = k_ref.shape[1]
-    q = jnp.transpose(q_ref[0])
-    rows_ref[head] = q
-    rows = q.shape[0]
-    pos = jnp.broadcast_to(pos_ref[...], (rows, LANES))
+def score_stats_kernel(pos_ref, q_ref, k_ref, out_ref, rows_ref, high_ref, sum_ref):
+    step = pl.program_id(0)
+    heads, rows, _ = rows_ref.shape
+    tile = k_ref.shape[1]
     ids = lax.broadcasted_iota(jnp.int32, (rows, LANES), 1)
-    highs, sums = [], []
-    for start in range(0, keys, tile):
-        scores = dot(q, k_ref[:, start : start + tile], NN)
-        lines = [
-            jnp.where(
-                ids + (start + at) <= pos, scores[:, at : at + LANES] * attn_scale, masked_fill
-            )
-            for at in range(0, tile, LANES)
-        ]
-        high = functools.reduce(jnp.maximum, lines)
-        highs.append(high)
-        sums.append(sum(jnp.exp2(line - high) for line in lines))
-    high = functools.reduce(jnp.maximum, highs)
-    total = sum(s * jnp.exp2(h - high) for h, s in zip(highs, sums))
-    most = jnp.max(high, axis=1, keepdims=True)
-    total = jnp.sum(total * jnp.exp2(high - most), axis=1, keepdims=True)
-    line = most + jnp.log2(total)
-    col_ref[...] = jnp.where(ids == head, line, col_ref[...])
-
-    @pl.when(head == heads - 1)
+    past = ids + step * tile - jnp.broadcast_to(pos_ref[...], (rows, LANES))
+    k = k_ref[...]
+
+    def over_heads(first):
+        for head in range(heads):
+            if first:
+                q = jnp.transpose(q_ref[head])
+                rows_ref[head] = q
+            else:
+                q = rows_ref[head]
+            scores = dot(q, k, NN)
+            lines = [
+                jnp.where(past <= -at, scores[:, at : at + LANES] * attn_scale, masked_fill)
+                for at in range(0, tile, LANES)
+            ]
+            if first:
+                high = functools.reduce(jnp.maximum, lines)
+                total = sum(jnp.exp2(line - high) for line in lines)
+            else:
+                before = high_ref[head]
+                high = functools.reduce(jnp.maximum, lines, before)
+                total = sum_ref[head] * jnp.exp2(before - high) + sum(
+                    jnp.exp2(line - high) for line in lines
+                )
+            high_ref[head] = high
+            sum_ref[head] = total
+
+    @pl.when(step == 0)
     def _():
+        over_heads(True)
+
+    @pl.when(step > 0)
+    def _():
+        over_heads(False)
+
+    @pl.when(step == pl.num_programs(0) - 1)
+    def _():
+        cols = jnp.zeros((rows, LANES), jnp.float32)
+        for head in range(heads):
+            high = high_ref[head]
+            most = jnp.max(high, axis=1, keepdims=True)
+            total = jnp.sum(sum_ref[head] * jnp.exp2(high - most), axis=1, keepdims=True)
+            cols = jnp.where(ids == head, most + jnp.log2(total), cols)
         for at in range(0, rows, LANES):
-            out_ref[at // LANES] = jnp.transpose(col_ref[at : at + LANES, :])[: out_ref.shape[1], :]
+            out_ref[at // LANES] = jnp.transpose(cols[at : at + LANES, :])[:heads, :]
 
 
 def score_stats(rel_pos, q, k):
     heads, width, rows = q.shape
     keys = k.shape[1]
     return pl.pallas_call(
-        functools.partial(score_stats_kernel, tile=512),
-        grid=(heads,),
+        score_stats_kernel,
+        grid=(keys // TILE,),
         in_specs=[
-            pl.BlockSpec((rows, 1), lambda h: (0, 0)),
-            pl.BlockSpec((1, width, rows), lambda h: (h, 0, 0)),
-            pl.BlockSpec((width, keys), lambda h: (0, 0)),
+            pl.BlockSpec((rows, 1), lambda t: (0, 0)),
+            pl.BlockSpec((heads, width, rows), lambda t: (0, 0, 0), pipeline_mode=pl.Buffered(1)),
+            pl.BlockSpec((width, TILE), lambda t: (0, t)),
         ],
         out_specs=(
-            pl.BlockSpec((rows // LANES, heads, LANES), lambda h: (0, 0, 0)),
+            pl.BlockSpec((rows // LANES, heads, LANES), lambda t: (0, 0, 0)),
             pl.BlockSpec(memory_space=pltpu.VMEM),
         ),
         out_shape=(
             jax.ShapeDtypeStruct((rows // LANES, heads, LANES), jnp.float32),
             pltpu.VMEM((heads, rows, width), q.dtype),
         ),
-        scratch_shapes=[pltpu.VMEM((rows, LANES), jnp.float32)],
+        scratch_shapes=[pltpu.VMEM((heads, rows, LANES), jnp.float32)] * 2,
         compiler_params=params(),
         cost_estimate=pl.CostEstimate(
             flops=2 * heads * rows * keys * width, transcendentals=heads * rows * keys, bytes_accessed=6 << 20
@@ -235,7 +253,7 @@
     def _():
         line = combined(stat_ref[...])
         total_ref[...] = jnp.sum(jnp.where(diagonal(rows), line, 0.0), axis=1, keepdims=True)
-        w_col_ref[...] = jnp.transpose(w_ref[...])
+        w_col_ref[...] = jnp.transpose(w_ref[...]) * index_scale
 
     target = jnp.sum(parts_ref[...], axis=0)
     probs = jnp.exp2(logit_ref[...] - total_ref[...])
@@ -246,7 +264,7 @@
     coefs = []
     for row in range(rows):
         own = dots[row * iheads : (row + 1) * iheads, :]
-        coef = jnp.where(own > 0, slope[row : row + 1, :] * w[:, row : row + 1] * index_scale, 0.0)
+        coef = jnp.where(own > 0, slope[row : row + 1, :] * w[:, row : row + 1], 0.0)
         coefs.append(coef.astype(jnp.bfloat16))
     coef = jnp.concatenate(coefs, axis=0)
     if key_part:
@@ -275,7 +293,8 @@
     _, nf, nz = sizes
     share = keys // (nf * nz)
     far = nf // 2
-    tile = far * nz * share
+    tile = far * nz * share if key_part else keys
+    steps = keys // tile
     last = stats.shape[2] // LANES - 1
 
     def part(mine):
@@ -284,11 +303,11 @@
     operands = [parts, logits, stats, q.reshape(flat, width), w, k]
     in_specs = [
         pl.BlockSpec((parts.shape[0], rows, tile), lambda t, half: (0, 0, t)),
-        pl.BlockSpec((rows, tile), lambda t, mine: (0, part(mine) * 2 + t)),
+        pl.BlockSpec((rows, tile), lambda t, mine: (0, part(mine) * steps + t)),
         pl.BlockSpec((stats.shape[0], 1, LANES), lambda t, half: (0, 0, last)),
         pl.BlockSpec((flat, width), lambda t, half: (0, 0)),
         pl.BlockSpec((rows, iheads), lambda t, half: (0, 0)),
-        pl.BlockSpec((tile, width), lambda t, mine: (part(mine) * 2 + t, 0)),
+        pl.BlockSpec((tile, width), lambda t, mine: (part(mine) * steps + t, 0)),
     ]
     row_spec = pl.BlockSpec((flat, width), lambda t, half: (0, 0))
     if before is not None:
@@ -307,7 +326,7 @@
         ),
         grid_spec=pltpu.PrefetchScalarGridSpec(
             num_scalar_prefetch=1,
-            grid=(keys // tile,),
+            grid=(steps,),
             in_specs=in_specs,
             out_specs=out_specs,
             scratch_shapes=[pltpu.VMEM((rows, 1), jnp.float32), pltpu.VMEM((iheads, rows), jnp.float32)],

time: 169 us -> 167 us (0.988)
  Pallas kernels: 41.1 us -> 38.8 us
where the time goes in v6:
time: 167 us; the launch traced here: 166 us
  starting transfers between devices  54.8 us (33%)
  waiting for transfers between devices  42.7 us (26%)
  Pallas kernels  38.8 us (23%)
  blocking collectives  24.7 us (15%)
  other arithmetic  3.16 us (2%)
    all_to_all x5, starting transfers between devices, exchanged(): return lax.all_to_all(parts, axis, split_axis=0, concat_axis=0, tiled=True)  34.3 us
    all_to_all x1, blocking collectives, exchanged(): return lax.all_to_all(parts, axis, split_axis=0, concat_axis=0, tiled=True)  24.7 us
    all_to_all x5, waiting for transfers between devices, exchanged(): return lax.all_to_all(parts, axis, split_axis=0, concat_axis=0, tiled=True)  20.6 us
    ppermute x2, waiting for transfers between devices, shards(): near = lax.ppermute(shares['sent', turn], 'yl', swap)  17.6 us
    pallas_call x4, Pallas kernels, head_share(): pl.pallas_call(functools.partial(head_share_kernel, other_rows=other_rows...  13.9 us
    ppermute x4, starting transfers between devices, at_owner(): got.append(lax.ppermute(part, axis, [(i, i ^ hop) for i in range(size)]))  13.6 us
    pallas_call x1, Pallas kernels, score_stats(): pl.pallas_call(score_stats_kernel, grid=(keys // TILE,), in_specs=[pl.Blo...  11.4 us
    pallas_call x3, Pallas kernels, gradients(): pl.pallas_call(functools.partial(gradients_kernel, count=float(count), be...  9.81 us
  transfers between devices with their start and end apart: 12, of which 6 were waited for; matrix products, arithmetic and copies ran while one was open for 1% of the time, Pallas kernels for 13%

profile of v6, /device:TPU:1, one launch (start us, length us, event | category | flops | bytes accessed | tf_op | source)
XLA Modules:
  0.0 166.3 jit_solution(10570681161458283621)
XLA Ops:
  1.7 11.4 %score_stats.1 = (f32[2,8,128]{2,1,0:T(8,128)S(1)}, bf16[8,256,576]{2,1,0:T(8,128)(2,1)S(1)}) custom-call(s32[256,1]{1,0:T(8,128)S(1)} %copy.9.pos_ref, bf16[8,576,256]{2,1,0:T(8,128)(2,1)} %bitcast.38, bf16[576,2048]{1,0:T(8,128)(2,1)} %bitcast.31), custom_call_target="tpu_custom_call" | custom-call | flops 4831838208 | bytes 6291456 | tf_op jit(solution)/shard_map/score_stats/pallas_call | solution.py:101
  15.3 24.7 %all_to_all.30.stats_ref.stat_ref = f32[32,1,2176]{2,1,0:T(1,128)S(1)} all-to-all(f32[32,1,2176]{2,1,0:T(1,128)} %get-tuple-element.9), channel_id=1, replica_groups=mesh['yl'=2,'zh'=4,'zl'=2,'x'=4,'yh'=4,'core'=2] {'x','yh','core'}, dimensions={0} | all-to-all | bytes 557056 | tf_op jit(solution)/shard_map/all_to_all | solution.py:360
  40.0 3.4 %head_share.6 = f32[128,1024]{1,0:T(8,128)S(1)} custom-call(s32[1]{0:T(128)} %bitcast.mine_ref.half_ref, f32[32,1,2176]{2,1,0:T(1,128)S(1)} %all_to_all.30.stats_ref.stat_ref, s32[256,1]{1,0:T(8,128)S(1)} %copy.9.pos_ref, bf16[8,256,576]{2,1,0:T(8,128)(2,1)S(1)} %get-tuple-element.10.q_ref, bf16[576,2048]{1,0:T(8,128)(2,1)} %bitcast.32), custom_call_target="tpu_custom_call" | custom-call | flops 1207959552 | bytes 3145728 | tf_op jit(solution)/shard_map/head_share/pallas_call | solution.py:167
  45.4 3.5 %head_share.7 = f32[128,1024]{1,0:T(8,128)S(1)} custom-call(s32[1]{0:T(128)} %bitcast.mine_ref.half_ref, f32[32,1,2176]{2,1,0:T(1,128)S(1)} %all_to_all.30.stats_ref.stat_ref, s32[256,1]{1,0:T(8,128)S(1)} %copy.9.pos_ref, bf16[8,256,576]{2,1,0:T(8,128)(2,1)S(1)} %get-tuple-element.10.q_ref, bf16[576,2048]{1,0:T(8,128)(2,1)} %bitcast.33), custom_call_target="tpu_custom_call" | custom-call | flops 1207959552 | bytes 3145728 | tf_op jit(solution)/shard_map/head_share/pallas_call | solution.py:167
  48.9 9.5 %collective-permute-done.1 = f32[128,1024]{1,0:T(8,128)S(1)} collective-permute-done((f32[128,1024]{1,0:T(8,128)S(1)}, f32[128,1024]{1,0:T(8,128)S(1)}, u32[]{:S(2)}, u32[]{:S(2)}) %collective-permute-start.1) | collective-permute-done | bytes 524320 | tf_op jit(solution)/shard_map/ppermute | solution.py:398
  59.2 10.0 %all-to-all-start.2 = ((f32[8,16,1024]{2,1,0:T(8,128)}), f32[8,16,1024]{2,1,0:T(8,128)}, u32[]{:S(2)}, u32[]{:S(2)}) async-start(f32[8,16,1024]{2,1,0:T(8,128)} %bitcast.36), calls=%async_computation.2 | async-start | bytes 1048576 | tf_op jit(solution)/shard_map/all_to_all | solution.py:360
  69.3 3.5 %head_share.4 = f32[128,1024]{1,0:T(8,128)S(1)} custom-call(s32[1]{0:T(128)} %bitcast.mine_ref.half_ref, f32[32,1,2176]{2,1,0:T(1,128)S(1)} %all_to_all.30.stats_ref.stat_ref, s32[256,1]{1,0:T(8,128)S(1)} %copy.9.pos_ref, bf16[8,256,576]{2,1,0:T(8,128)(2,1)S(1)} %get-tuple-element.10.q_ref, bf16[576,2048]{1,0:T(8,128)(2,1)} %bitcast.34), custom_call_target="tpu_custom_call" | custom-call | flops 1207959552 | bytes 3145728 | tf_op jit(solution)/shard_map/head_share/pallas_call | solution.py:167
  72.7 2.3 %collective-permute-start = (f32[128,1024]{1,0:T(8,128)S(1)}, f32[128,1024]{1,0:T(8,128)S(1)}, u32[]{:S(2)}, u32[]{:S(2)}) collective-permute-start(f32[128,1024]{1,0:T(8,128)S(1)} %head_share.4), channel_id=1, source_target_pairs={{0,256},{256,0},{1,257},{257,1},{2,258},{258,2},{3,259},{259,3},{4... | collective-permute-start | bytes 1572872 | tf_op jit(solution)/shard_map/ppermute | solution.py:398
  75.1 3.5 %head_share.5 = f32[128,1024]{1,0:T(8,128)S(1)} custom-call(s32[1]{0:T(128)} %bitcast.mine_ref.half_ref, f32[32,1,2176]{2,1,0:T(1,128)S(1)} %all_to_all.30.stats_ref.stat_ref, s32[256,1]{1,0:T(8,128)S(1)} %copy.9.pos_ref, bf16[8,256,576]{2,1,0:T(8,128)(2,1)S(1)} %get-tuple-element.10.q_ref, bf16[576,2048]{1,0:T(8,128)(2,1)} %bitcast.35), custom_call_target="tpu_custom_call" | custom-call | flops 1207959552 | bytes 3145728 | tf_op jit(solution)/shard_map/head_share/pallas_call | solution.py:167
  78.6 8.1 %collective-permute-done = f32[128,1024]{1,0:T(8,128)S(1)} collective-permute-done((f32[128,1024]{1,0:T(8,128)S(1)}, f32[128,1024]{1,0:T(8,128)S(1)}, u32[]{:S(2)}, u32[]{:S(2)}) %collective-permute-start) | collective-permute-done | bytes 524320 | tf_op jit(solution)/shard_map/ppermute | solution.py:398
  87.5 6.4 %all-to-all-start.1 = ((f32[8,16,1024]{2,1,0:T(8,128)}), f32[8,16,1024]{2,1,0:T(8,128)S(1)}, u32[]{:S(2)}, u32[]{:S(2)}) async-start(f32[8,16,1024]{2,1,0:T(8,128)} %bitcast.6), calls=%async_computation.1 | async-start | bytes 1048576 | tf_op jit(solution)/shard_map/all_to_all | solution.py:360
  94.0 3.5 %gradients.3 = (f32[1024,128]{1,0:T(8,128)S(1)}, f32[2,4,128,128]{3,2,1,0:T(8,128)S(1)}) custom-call(s32[1]{0:T(128)} %bitcast.mine_ref.half_ref, f32[8,16,1024]{2,1,0:T(8,128)} %all-to-all-done.2.parts_ref, f32[16,2048]{1,0:T(8,128)} %get-tuple-element.11.logit_ref, f32[32,1,2176]{2,1,0:T(1,128)S(1)} %all_to_all.30.stats_ref.stat_ref, ...), custom_call_target="tpu_custom_call" | custom-call | flops 805306368 | bytes 2097152 | tf_op jit(solution)/shard_map/gradients/pallas_call | solution.py:323
  97.4 2.6 %collective-permute-start.2 = (f32[2,4,128,128]{3,2,1,0:T(8,128)S(1)}, f32[2,4,128,128]{3,2,1,0:T(8,128)S(1)}, u32[]{:S(2)}, u32[]{:S(2)}) collective-permute-start(f32[2,4,128,128]{3,2,1,0:T(8,128)S(1)} %get-tuple-element.13), channel_id=1, source_target_pairs={{0,256},{256,0},{1,257},{257,1},{2,258},{258,2},{3,259},{259,3},{4... | collective-permute-start | bytes 1572872 | tf_op jit(solution)/shard_map/ppermute | solution.py:415
  100.1 8.5 %all-to-all-done.1.parts_ref = f32[8,16,1024]{2,1,0:T(8,128)S(1)} async-done(((f32[8,16,1024]{2,1,0:T(8,128)}), f32[8,16,1024]{2,1,0:T(8,128)S(1)}, u32[]{:S(2)}, u32[]{:S(2)}) %all-to-all-start.1) | async-done | bytes 524320 | tf_op jit(solution)/shard_map/all_to_all | solution.py:360
  108.5 2.9 %gradients.4 = f32[1024,128]{1,0:T(8,128)} custom-call(s32[1]{0:T(128)} %bitcast.mine_ref.half_ref, f32[8,16,1024]{2,1,0:T(8,128)S(1)} %all-to-all-done.1.parts_ref, f32[16,2048]{1,0:T(8,128)} %get-tuple-element.11.logit_ref, f32[32,1,2176]{2,1,0:T(1,128)S(1)} %all_to_all.30.stats_ref.stat_ref, bf16[1024,128]{1,0:T(8,128)(2,1)S(1)} %bitcast.29, ...), custom_call_target="tpu_custom_call" | custom-call | flops 536870912 | bytes 2097152 | tf_op jit(solution)/shard_map/gradients/pallas_call | solution.py:323
  111.4 8.3 %all-to-all-start.3 = ((f32[8,128,128]{2,1,0:T(8,128)}), f32[8,128,128]{2,1,0:T(8,128)S(1)}, u32[]{:S(2)}, u32[]{:S(2)}) async-start(f32[8,128,128]{2,1,0:T(8,128)} %bitcast.8), calls=%async_computation.3 | async-start | bytes 1048576 | tf_op jit(solution)/shard_map/all_to_all | solution.py:360
  119.8 9.3 %all-to-all-done.3.parts_ref = f32[8,128,128]{2,1,0:T(8,128)S(1)} async-done(((f32[8,128,128]{2,1,0:T(8,128)}), f32[8,128,128]{2,1,0:T(8,128)S(1)}, u32[]{:S(2)}, u32[]{:S(2)}) %all-to-all-start.3) | async-done | bytes 524320 | tf_op jit(solution)/shard_map/all_to_all | solution.py:360
  129.8 3.4 %all-to-all-start.4 = ((f32[4,128,128]{2,1,0:T(8,128)}), f32[4,128,128]{2,1,0:T(8,128)S(1)}, u32[]{:S(2)}, u32[]{:S(2)}) async-start(f32[4,128,128]{2,1,0:T(8,128)} %sum_copies.2), calls=%async_computation.4 | async-start | bytes 524288 | tf_op jit(solution)/shard_map/all_to_all | solution.py:360
  133.3 3.4 %gradients.5 = f32[2,4,128,128]{3,2,1,0:T(8,128)S(1)} custom-call(s32[1]{0:T(128)} %bitcast.mine_ref.half_ref, f32[8,16,1024]{2,1,0:T(8,128)S(1)} %all-to-all-done.1.parts_ref, f32[16,2048]{1,0:T(8,128)} %get-tuple-element.11.logit_ref, f32[32,1,2176]{2,1,0:T(1,128)S(1)} %all_to_all.30.stats_ref.stat_ref, bf16[1024,128]{1,0:T(8,128)(2,1)S(1)} %bitcast.30, ...), custom_call_target="tpu_custom_call" | custom-call | flops 536870912 | bytes 2097152 | tf_op jit(solution)/shard_map/gradients/pallas_call | solution.py:323
  139.0 2.8 %all-to-all-done.4.parts_ref = f32[4,128,128]{2,1,0:T(8,128)S(1)} async-done(((f32[4,128,128]{2,1,0:T(8,128)}), f32[4,128,128]{2,1,0:T(8,128)S(1)}, u32[]{:S(2)}, u32[]{:S(2)}) %all-to-all-start.4) | async-done | bytes 262176 | tf_op jit(solution)/shard_map/all_to_all | solution.py:360
  142.7 6.1 %all-to-all-start.5 = ((f32[16,64,128]{2,1,0:T(8,128)}), f32[16,64,128]{2,1,0:T(8,128)S(1)}, u32[]{:S(2)}, u32[]{:S(2)}) async-start(f32[16,64,128]{2,1,0:T(8,128)} %bitcast.9), calls=%async_computation.5 | async-start | bytes 1048576 | tf_op jit(solution)/shard_map/all_to_all | solution.py:360
  150.9 4.6 %collective-permute-start.5 = (f32[128,128]{1,0:T(8,128)S(1)}, f32[128,128]{1,0:T(8,128)S(1)}, u32[]{:S(2)}, u32[]{:S(2)}) collective-permute-start(f32[128,128]{1,0:T(8,128)S(1)} %get-tuple-element.16), channel_id=1, source_target_pairs={{0,128},{64,192},{128,0},{192,64},{1,129},{65,193},{129,1},{193,65... | collective-permute-start | bytes 196616 | tf_op jit(solution)/shard_map/ppermute | solution.py:370
  155.5 4.7 %collective-permute-start.4 = (f32[128,128]{1,0:T(8,128)S(1)}, f32[128,128]{1,0:T(8,128)S(1)}, u32[]{:S(2)}, u32[]{:S(2)}) collective-permute-start(f32[128,128]{1,0:T(8,128)S(1)} %get-tuple-element.14), channel_id=1, source_target_pairs={{0,64},{64,0},{128,192},{192,128},{1,65},{65,1},{129,193},{193,129... | collective-permute-start | bytes 196616 | tf_op jit(solution)/shard_map/ppermute | solution.py:370
  160.3 4.5 %collective-permute-done.4 = f32[128,128]{1,0:T(8,128)S(1)} collective-permute-done((f32[128,128]{1,0:T(8,128)S(1)}, f32[128,128]{1,0:T(8,128)S(1)}, u32[]{:S(2)}, u32[]{:S(2)}) %collective-permute-start.4) | collective-permute-done | bytes 65568 | tf_op jit(solution)/shard_map/ppermute | solution.py:370
  (34 shorter events, 14.3 us)
Async XLA Ops:
  1.6 11.4 %copy-start = (bf16[2048,128]{1,0:T(8,128)(2,1)S(1)}, bf16[2048,128]{1,0:T(8,128)(2,1)}, u32[]{:S(2)}) copy-start(bf16[2048,128]{1,0:T(8,128)(2,1)} %k_ref.7) | copy-start | bytes 1572868
  1.6 11.4 %copy-start.1 = (bf16[16,64,128]{2,1,0:T(8,128)(2,1)S(1)}, bf16[16,64,128]{2,1,0:T(8,128)(2,1)}, u32[]{:S(2)}) copy-start(bf16[16,64,128]{2,1,0:T(8,128)(2,1)} %param.9) | copy-start | bytes 786436
  1.7 11.4 %copy-start.3 = (f32[16,64]{1,0:T(8,128)S(1)}, f32[16,64]{1,0:T(8,128)}, u32[]{:S(2)}) copy-start(f32[16,64]{1,0:T(8,128)} %w_ref.7) | copy-start | bytes 12292
  43.4 14.9 %collective-permute-start.1 = (f32[128,1024]{1,0:T(8,128)S(1)}, f32[128,1024]{1,0:T(8,128)S(1)}, u32[]{:S(2)}, u32[]{:S(2)}) collective-permute-start(f32[128,1024]{1,0:T(8,128)S(1)} %head_share.6), channel_id=1, source_target_pairs={{0,256},{256,0},{1,257},{257,1},{2,258},{258,2},{3,259},{259,3},{4... | collective-permute-start | bytes 1572872 | tf_op jit(solution)/shard_map/ppermute | solution.py:398
  59.2 28.3 %all-to-all-start.2 = ((f32[8,16,1024]{2,1,0:T(8,128)}), f32[8,16,1024]{2,1,0:T(8,128)}, u32[]{:S(2)}, u32[]{:S(2)}) async-start(f32[8,16,1024]{2,1,0:T(8,128)} %bitcast.36), calls=%async_computation.2 | async-start | bytes 1048576 | tf_op jit(solution)/shard_map/all_to_all | solution.py:360
  72.7 13.9 %collective-permute-start = (f32[128,1024]{1,0:T(8,128)S(1)}, f32[128,1024]{1,0:T(8,128)S(1)}, u32[]{:S(2)}, u32[]{:S(2)}) collective-permute-start(f32[128,1024]{1,0:T(8,128)S(1)} %head_share.4), channel_id=1, source_target_pairs={{0,256},{256,0},{1,257},{257,1},{2,258},{258,2},{3,259},{259,3},{4... | collective-permute-start | bytes 1572872 | tf_op jit(solution)/shard_map/ppermute | solution.py:398
  78.5 15.4 %copy-start.2 = (bf16[16,64,128]{2,1,0:T(8,128)(2,1)S(1)}, bf16[16,64,128]{2,1,0:T(8,128)(2,1)}, u32[]{:S(2)}) copy-start(bf16[16,64,128]{2,1,0:T(8,128)(2,1)} %param.9) | copy-start | bytes 786436
  78.6 15.4 %copy-start.4 = (f32[16,64]{1,0:T(8,128)S(1)}, f32[16,64]{1,0:T(8,128)}, u32[]{:S(2)}) copy-start(f32[16,64]{1,0:T(8,128)} %w_ref.7) | copy-start | bytes 12292
  87.5 21.0 %all-to-all-start.1 = ((f32[8,16,1024]{2,1,0:T(8,128)}), f32[8,16,1024]{2,1,0:T(8,128)S(1)}, u32[]{:S(2)}, u32[]{:S(2)}) async-start(f32[8,16,1024]{2,1,0:T(8,128)} %bitcast.6), calls=%async_computation.1 | async-start | bytes 1048576 | tf_op jit(solution)/shard_map/all_to_all | solution.py:360
  97.4 39.3 %collective-permute-start.2 = (f32[2,4,128,128]{3,2,1,0:T(8,128)S(1)}, f32[2,4,128,128]{3,2,1,0:T(8,128)S(1)}, u32[]{:S(2)}, u32[]{:S(2)}) collective-permute-start(f32[2,4,128,128]{3,2,1,0:T(8,128)S(1)} %get-tuple-element.13), channel_id=1, source_target_pairs={{0,256},{256,0},{1,257},{257,1},{2,258},{258,2},{3,259},{259,3},{4... | collective-permute-start | bytes 1572872 | tf_op jit(solution)/shard_map/ppermute | solution.py:415
  111.4 17.7 %all-to-all-start.3 = ((f32[8,128,128]{2,1,0:T(8,128)}), f32[8,128,128]{2,1,0:T(8,128)S(1)}, u32[]{:S(2)}, u32[]{:S(2)}) async-start(f32[8,128,128]{2,1,0:T(8,128)} %bitcast.8), calls=%async_computation.3 | async-start | bytes 1048576 | tf_op jit(solution)/shard_map/all_to_all | solution.py:360
  129.8 12.0 %all-to-all-start.4 = ((f32[4,128,128]{2,1,0:T(8,128)}), f32[4,128,128]{2,1,0:T(8,128)S(1)}, u32[]{:S(2)}, u32[]{:S(2)}) async-start(f32[4,128,128]{2,1,0:T(8,128)} %sum_copies.2), calls=%async_computation.4 | async-start | bytes 524288 | tf_op jit(solution)/shard_map/all_to_all | solution.py:360
  136.8 12.0 %collective-permute-start.3 = (f32[4,128,128]{2,1,0:T(8,128)S(1)}, f32[4,128,128]{2,1,0:T(8,128)S(1)}, u32[]{:S(2)}, u32[]{:S(2)}) collective-permute-start(f32[4,128,128]{2,1,0:T(8,128)S(1)} %dynamic-slice_bitcast_fusion), channel_id=1, source_target_pairs={{0,32},{32,0},{1,33},{33,1},{2,34},{34,2},{3,35},{35,3},{4,36},{36... | collective-permute-start | bytes 786440 | tf_op jit(solution)/shard_map/ppermute | solution.py:370
  142.7 22.8 %all-to-all-start.5 = ((f32[16,64,128]{2,1,0:T(8,128)}), f32[16,64,128]{2,1,0:T(8,128)S(1)}, u32[]{:S(2)}, u32[]{:S(2)}) async-start(f32[16,64,128]{2,1,0:T(8,128)} %bitcast.9), calls=%async_computation.5 | async-start | bytes 1048576 | tf_op jit(solution)/shard_map/all_to_all | solution.py:360
  148.9 11.4 %collective-permute-start.6 = (f32[128,128]{1,0:T(8,128)S(1)}, f32[128,128]{1,0:T(8,128)S(1)}, u32[]{:S(2)}, u32[]{:S(2)}) collective-permute-start(f32[128,128]{1,0:T(8,128)S(1)} %get-tuple-element.15), channel_id=1, source_target_pairs={{0,192},{64,128},{128,64},{192,0},{1,193},{65,129},{129,65},{193,1... | collective-permute-start | bytes 196616 | tf_op jit(solution)/shard_map/ppermute | solution.py:370
  150.9 9.4 %collective-permute-start.5 = (f32[128,128]{1,0:T(8,128)S(1)}, f32[128,128]{1,0:T(8,128)S(1)}, u32[]{:S(2)}, u32[]{:S(2)}) collective-permute-start(f32[128,128]{1,0:T(8,128)S(1)} %get-tuple-element.16), channel_id=1, source_target_pairs={{0,128},{64,192},{128,0},{192,64},{1,129},{65,193},{129,1},{193,65... | collective-permute-start | bytes 196616 | tf_op jit(solution)/shard_map/ppermute | solution.py:370
  155.5 9.3 %collective-permute-start.4 = (f32[128,128]{1,0:T(8,128)S(1)}, f32[128,128]{1,0:T(8,128)S(1)}, u32[]{:S(2)}, u32[]{:S(2)}) collective-permute-start(f32[128,128]{1,0:T(8,128)S(1)} %get-tuple-element.14), channel_id=1, source_target_pairs={{0,64},{64,0},{128,192},{192,128},{1,65},{65,1},{129,193},{193,129... | collective-permute-start | bytes 196616 | tf_op jit(solution)/shard_map/ppermute | solution.py:370

commit v7 on v6

--- a/solution.py
+++ b/solution.py
@@ -348,10 +348,15 @@
 
 
 def sum_copies(parts, copies):
+    count, rows, width = parts.shape
+    block = rows // 4
     return pl.pallas_call(
         sum_copies_kernel,
-        out_shape=jax.ShapeDtypeStruct((copies, *parts.shape[1:]), parts.dtype),
-        compiler_params=pltpu.CompilerParams(vmem_limit_bytes=8 * 1024 * 1024),
+        grid=(rows // block,),
+        in_specs=[pl.BlockSpec((count, block, width), lambda r: (0, r, 0))],
+        out_specs=pl.BlockSpec((copies, block, width), lambda r: (0, r, 0)),
+        out_shape=jax.ShapeDtypeStruct((copies, rows, width), parts.dtype),
+        compiler_params=params(8),
         name="sum_copies",
     )(parts)
 

time: 167 us -> 168 us (level)
  transfers between devices with their start and end apart: 12 -> 12, of which waited for: 6 -> 6; matrix products, arithmetic and copies ran while one was open for 1% -> 1% of each run, Pallas kernels for 13% -> 14%
where the time goes in v7:
time: 168 us; the launch traced here: 167 us
  starting transfers between devices  54.8 us (33%)
  waiting for transfers between devices  42.7 us (25%)
  Pallas kernels  40 us (24%)
  blocking collectives  24.7 us (15%)
  other arithmetic  3.16 us (2%)
    all_to_all x5, starting transfers between devices, exchanged(): return lax.all_to_all(parts, axis, split_axis=0, concat_axis=0, tiled=True)  34.3 us
    all_to_all x1, blocking collectives, exchanged(): return lax.all_to_all(parts, axis, split_axis=0, concat_axis=0, tiled=True)  24.7 us
    all_to_all x5, waiting for transfers between devices, exchanged(): return lax.all_to_all(parts, axis, split_axis=0, concat_axis=0, tiled=True)  20.6 us
    ppermute x2, waiting for transfers between devices, shards(): near = lax.ppermute(shares['sent', turn], 'yl', swap)  17.6 us
    pallas_call x4, Pallas kernels, head_share(): pl.pallas_call(functools.partial(head_share_kernel, other_rows=other_rows...  13.9 us
    ppermute x4, starting transfers between devices, at_owner(): got.append(lax.ppermute(part, axis, [(i, i ^ hop) for i in range(size)]))  13.6 us
    pallas_call x1, Pallas kernels, score_stats(): pl.pallas_call(score_stats_kernel, grid=(keys // TILE,), in_specs=[pl.Blo...  11.4 us
    pallas_call x3, Pallas kernels, gradients(): pl.pallas_call(functools.partial(gradients_kernel, count=float(count), be...  9.81 us
  transfers between devices with their start and end apart: 12, of which 6 were waited for; matrix products, arithmetic and copies ran while one was open for 1% of the time, Pallas kernels for 14%

profile of v7, /device:TPU:1, one launch (start us, length us, event | category | flops | bytes accessed | tf_op | source)
XLA Modules:
  0.0 167.5 jit_solution(6124888175129297094)
XLA Ops:
  1.7 11.4 %score_stats.1 = (f32[2,8,128]{2,1,0:T(8,128)S(1)}, bf16[8,256,576]{2,1,0:T(8,128)(2,1)S(1)}) custom-call(s32[256,1]{1,0:T(8,128)S(1)} %copy.9.pos_ref, bf16[8,576,256]{2,1,0:T(8,128)(2,1)} %bitcast.38, bf16[576,2048]{1,0:T(8,128)(2,1)} %bitcast.31), custom_call_target="tpu_custom_call" | custom-call | flops 4831838208 | bytes 6291456 | tf_op jit(solution)/shard_map/score_stats/pallas_call | solution.py:101
  15.3 24.7 %all_to_all.30.stats_ref.stat_ref = f32[32,1,2176]{2,1,0:T(1,128)S(1)} all-to-all(f32[32,1,2176]{2,1,0:T(1,128)} %get-tuple-element.9), channel_id=1, replica_groups=mesh['yl'=2,'zh'=4,'zl'=2,'x'=4,'yh'=4,'core'=2] {'x','yh','core'}, dimensions={0} | all-to-all | bytes 557056 | tf_op jit(solution)/shard_map/all_to_all | solution.py:365
  40.0 3.4 %head_share.6 = f32[128,1024]{1,0:T(8,128)S(1)} custom-call(s32[1]{0:T(128)} %bitcast.mine_ref.half_ref, f32[32,1,2176]{2,1,0:T(1,128)S(1)} %all_to_all.30.stats_ref.stat_ref, s32[256,1]{1,0:T(8,128)S(1)} %copy.9.pos_ref, bf16[8,256,576]{2,1,0:T(8,128)(2,1)S(1)} %get-tuple-element.10.q_ref, bf16[576,2048]{1,0:T(8,128)(2,1)} %bitcast.32), custom_call_target="tpu_custom_call" | custom-call | flops 1207959552 | bytes 3145728 | tf_op jit(solution)/shard_map/head_share/pallas_call | solution.py:167
  45.4 3.5 %head_share.7 = f32[128,1024]{1,0:T(8,128)S(1)} custom-call(s32[1]{0:T(128)} %bitcast.mine_ref.half_ref, f32[32,1,2176]{2,1,0:T(1,128)S(1)} %all_to_all.30.stats_ref.stat_ref, s32[256,1]{1,0:T(8,128)S(1)} %copy.9.pos_ref, bf16[8,256,576]{2,1,0:T(8,128)(2,1)S(1)} %get-tuple-element.10.q_ref, bf16[576,2048]{1,0:T(8,128)(2,1)} %bitcast.33), custom_call_target="tpu_custom_call" | custom-call | flops 1207959552 | bytes 3145728 | tf_op jit(solution)/shard_map/head_share/pallas_call | solution.py:167
  48.9 9.5 %collective-permute-done.1 = f32[128,1024]{1,0:T(8,128)S(1)} collective-permute-done((f32[128,1024]{1,0:T(8,128)S(1)}, f32[128,1024]{1,0:T(8,128)S(1)}, u32[]{:S(2)}, u32[]{:S(2)}) %collective-permute-start.1) | collective-permute-done | bytes 524320 | tf_op jit(solution)/shard_map/ppermute | solution.py:403
  59.2 10.0 %all-to-all-start.2 = ((f32[8,16,1024]{2,1,0:T(8,128)}), f32[8,16,1024]{2,1,0:T(8,128)}, u32[]{:S(2)}, u32[]{:S(2)}) async-start(f32[8,16,1024]{2,1,0:T(8,128)} %bitcast.36), calls=%async_computation.2 | async-start | bytes 1048576 | tf_op jit(solution)/shard_map/all_to_all | solution.py:365
  69.3 3.5 %head_share.4 = f32[128,1024]{1,0:T(8,128)S(1)} custom-call(s32[1]{0:T(128)} %bitcast.mine_ref.half_ref, f32[32,1,2176]{2,1,0:T(1,128)S(1)} %all_to_all.30.stats_ref.stat_ref, s32[256,1]{1,0:T(8,128)S(1)} %copy.9.pos_ref, bf16[8,256,576]{2,1,0:T(8,128)(2,1)S(1)} %get-tuple-element.10.q_ref, bf16[576,2048]{1,0:T(8,128)(2,1)} %bitcast.34), custom_call_target="tpu_custom_call" | custom-call | flops 1207959552 | bytes 3145728 | tf_op jit(solution)/shard_map/head_share/pallas_call | solution.py:167
  72.7 2.3 %collective-permute-start = (f32[128,1024]{1,0:T(8,128)S(1)}, f32[128,1024]{1,0:T(8,128)S(1)}, u32[]{:S(2)}, u32[]{:S(2)}) collective-permute-start(f32[128,1024]{1,0:T(8,128)S(1)} %head_share.4), channel_id=1, source_target_pairs={{0,256},{256,0},{1,257},{257,1},{2,258},{258,2},{3,259},{259,3},{4... | collective-permute-start | bytes 1572872 | tf_op jit(solution)/shard_map/ppermute | solution.py:403
  75.1 3.5 %head_share.5 = f32[128,1024]{1,0:T(8,128)S(1)} custom-call(s32[1]{0:T(128)} %bitcast.mine_ref.half_ref, f32[32,1,2176]{2,1,0:T(1,128)S(1)} %all_to_all.30.stats_ref.stat_ref, s32[256,1]{1,0:T(8,128)S(1)} %copy.9.pos_ref, bf16[8,256,576]{2,1,0:T(8,128)(2,1)S(1)} %get-tuple-element.10.q_ref, bf16[576,2048]{1,0:T(8,128)(2,1)} %bitcast.35), custom_call_target="tpu_custom_call" | custom-call | flops 1207959552 | bytes 3145728 | tf_op jit(solution)/shard_map/head_share/pallas_call | solution.py:167
  78.6 8.1 %collective-permute-done = f32[128,1024]{1,0:T(8,128)S(1)} collective-permute-done((f32[128,1024]{1,0:T(8,128)S(1)}, f32[128,1024]{1,0:T(8,128)S(1)}, u32[]{:S(2)}, u32[]{:S(2)}) %collective-permute-start) | collective-permute-done | bytes 524320 | tf_op jit(solution)/shard_map/ppermute | solution.py:403
  87.5 6.4 %all-to-all-start.1 = ((f32[8,16,1024]{2,1,0:T(8,128)}), f32[8,16,1024]{2,1,0:T(8,128)S(1)}, u32[]{:S(2)}, u32[]{:S(2)}) async-start(f32[8,16,1024]{2,1,0:T(8,128)} %bitcast.6), calls=%async_computation.1 | async-start | bytes 1048576 | tf_op jit(solution)/shard_map/all_to_all | solution.py:365
  94.0 3.5 %gradients.3 = (f32[1024,128]{1,0:T(8,128)S(1)}, f32[2,4,128,128]{3,2,1,0:T(8,128)S(1)}) custom-call(s32[1]{0:T(128)} %bitcast.mine_ref.half_ref, f32[8,16,1024]{2,1,0:T(8,128)} %all-to-all-done.2.parts_ref, f32[16,2048]{1,0:T(8,128)} %get-tuple-element.11.logit_ref, f32[32,1,2176]{2,1,0:T(1,128)S(1)} %all_to_all.30.stats_ref.stat_ref, ...), custom_call_target="tpu_custom_call" | custom-call | flops 805306368 | bytes 2097152 | tf_op jit(solution)/shard_map/gradients/pallas_call | solution.py:323
  97.4 2.6 %collective-permute-start.2 = (f32[2,4,128,128]{3,2,1,0:T(8,128)S(1)}, f32[2,4,128,128]{3,2,1,0:T(8,128)S(1)}, u32[]{:S(2)}, u32[]{:S(2)}) collective-permute-start(f32[2,4,128,128]{3,2,1,0:T(8,128)S(1)} %get-tuple-element.13), channel_id=1, source_target_pairs={{0,256},{256,0},{1,257},{257,1},{2,258},{258,2},{3,259},{259,3},{4... | collective-permute-start | bytes 1572872 | tf_op jit(solution)/shard_map/ppermute | solution.py:420
  100.1 8.5 %all-to-all-done.1.parts_ref = f32[8,16,1024]{2,1,0:T(8,128)S(1)} async-done(((f32[8,16,1024]{2,1,0:T(8,128)}), f32[8,16,1024]{2,1,0:T(8,128)S(1)}, u32[]{:S(2)}, u32[]{:S(2)}) %all-to-all-start.1) | async-done | bytes 524320 | tf_op jit(solution)/shard_map/all_to_all | solution.py:365
  108.5 2.9 %gradients.4 = f32[1024,128]{1,0:T(8,128)} custom-call(s32[1]{0:T(128)} %bitcast.mine_ref.half_ref, f32[8,16,1024]{2,1,0:T(8,128)S(1)} %all-to-all-done.1.parts_ref, f32[16,2048]{1,0:T(8,128)} %get-tuple-element.11.logit_ref, f32[32,1,2176]{2,1,0:T(1,128)S(1)} %all_to_all.30.stats_ref.stat_ref, bf16[1024,128]{1,0:T(8,128)(2,1)S(1)} %bitcast.29, ...), custom_call_target="tpu_custom_call" | custom-call | flops 536870912 | bytes 2097152 | tf_op jit(solution)/shard_map/gradients/pallas_call | solution.py:323
  111.4 8.3 %all-to-all-start.3 = ((f32[8,128,128]{2,1,0:T(8,128)}), f32[8,128,128]{2,1,0:T(8,128)S(1)}, u32[]{:S(2)}, u32[]{:S(2)}) async-start(f32[8,128,128]{2,1,0:T(8,128)} %bitcast.8), calls=%async_computation.3 | async-start | bytes 1048576 | tf_op jit(solution)/shard_map/all_to_all | solution.py:365
  119.8 9.3 %all-to-all-done.3.parts_ref = f32[8,128,128]{2,1,0:T(8,128)S(1)} async-done(((f32[8,128,128]{2,1,0:T(8,128)}), f32[8,128,128]{2,1,0:T(8,128)S(1)}, u32[]{:S(2)}, u32[]{:S(2)}) %all-to-all-start.3) | async-done | bytes 524320 | tf_op jit(solution)/shard_map/all_to_all | solution.py:365
  130.5 3.4 %all-to-all-start.4 = ((f32[4,128,128]{2,1,0:T(8,128)}), f32[4,128,128]{2,1,0:T(8,128)S(1)}, u32[]{:S(2)}, u32[]{:S(2)}) async-start(f32[4,128,128]{2,1,0:T(8,128)} %sum_copies.2), calls=%async_computation.4 | async-start | bytes 524288 | tf_op jit(solution)/shard_map/all_to_all | solution.py:365
  133.9 3.4 %gradients.5 = f32[2,4,128,128]{3,2,1,0:T(8,128)S(1)} custom-call(s32[1]{0:T(128)} %bitcast.mine_ref.half_ref, f32[8,16,1024]{2,1,0:T(8,128)S(1)} %all-to-all-done.1.parts_ref, f32[16,2048]{1,0:T(8,128)} %get-tuple-element.11.logit_ref, f32[32,1,2176]{2,1,0:T(1,128)S(1)} %all_to_all.30.stats_ref.stat_ref, bf16[1024,128]{1,0:T(8,128)(2,1)S(1)} %bitcast.30, ...), custom_call_target="tpu_custom_call" | custom-call | flops 536870912 | bytes 2097152 | tf_op jit(solution)/shard_map/gradients/pallas_call | solution.py:323
  139.7 2.8 %all-to-all-done.4.parts_ref = f32[4,128,128]{2,1,0:T(8,128)S(1)} async-done(((f32[4,128,128]{2,1,0:T(8,128)}), f32[4,128,128]{2,1,0:T(8,128)S(1)}, u32[]{:S(2)}, u32[]{:S(2)}) %all-to-all-start.4) | async-done | bytes 262176 | tf_op jit(solution)/shard_map/all_to_all | solution.py:365
  143.9 6.1 %all-to-all-start.5 = ((f32[16,64,128]{2,1,0:T(8,128)}), f32[16,64,128]{2,1,0:T(8,128)S(1)}, u32[]{:S(2)}, u32[]{:S(2)}) async-start(f32[16,64,128]{2,1,0:T(8,128)} %bitcast.9), calls=%async_computation.5 | async-start | bytes 1048576 | tf_op jit(solution)/shard_map/all_to_all | solution.py:365
  152.1 4.6 %collective-permute-start.5 = (f32[128,128]{1,0:T(8,128)S(1)}, f32[128,128]{1,0:T(8,128)S(1)}, u32[]{:S(2)}, u32[]{:S(2)}) collective-permute-start(f32[128,128]{1,0:T(8,128)S(1)} %get-tuple-element.16), channel_id=1, source_target_pairs={{0,128},{64,192},{128,0},{192,64},{1,129},{65,193},{129,1},{193,65... | collective-permute-start | bytes 196616 | tf_op jit(solution)/shard_map/ppermute | solution.py:375
  156.7 4.7 %collective-permute-start.4 = (f32[128,128]{1,0:T(8,128)S(1)}, f32[128,128]{1,0:T(8,128)S(1)}, u32[]{:S(2)}, u32[]{:S(2)}) collective-permute-start(f32[128,128]{1,0:T(8,128)S(1)} %get-tuple-element.14), channel_id=1, source_target_pairs={{0,64},{64,0},{128,192},{192,128},{1,65},{65,1},{129,193},{193,129... | collective-permute-start | bytes 196616 | tf_op jit(solution)/shard_map/ppermute | solution.py:375
  161.5 4.5 %collective-permute-done.4 = f32[128,128]{1,0:T(8,128)S(1)} collective-permute-done((f32[128,128]{1,0:T(8,128)S(1)}, f32[128,128]{1,0:T(8,128)S(1)}, u32[]{:S(2)}, u32[]{:S(2)}) %collective-permute-start.4) | collective-permute-done | bytes 65568 | tf_op jit(solution)/shard_map/ppermute | solution.py:375
  (34 shorter events, 15.5 us)
Async XLA Ops:
  1.6 11.4 %copy-start = (bf16[2048,128]{1,0:T(8,128)(2,1)S(1)}, bf16[2048,128]{1,0:T(8,128)(2,1)}, u32[]{:S(2)}) copy-start(bf16[2048,128]{1,0:T(8,128)(2,1)} %k_ref.7) | copy-start | bytes 1572868
  1.6 11.4 %copy-start.1 = (bf16[16,64,128]{2,1,0:T(8,128)(2,1)S(1)}, bf16[16,64,128]{2,1,0:T(8,128)(2,1)}, u32[]{:S(2)}) copy-start(bf16[16,64,128]{2,1,0:T(8,128)(2,1)} %param.9) | copy-start | bytes 786436
  1.7 11.4 %copy-start.3 = (f32[16,64]{1,0:T(8,128)S(1)}, f32[16,64]{1,0:T(8,128)}, u32[]{:S(2)}) copy-start(f32[16,64]{1,0:T(8,128)} %w_ref.7) | copy-start | bytes 12292
  43.4 14.9 %collective-permute-start.1 = (f32[128,1024]{1,0:T(8,128)S(1)}, f32[128,1024]{1,0:T(8,128)S(1)}, u32[]{:S(2)}, u32[]{:S(2)}) collective-permute-start(f32[128,1024]{1,0:T(8,128)S(1)} %head_share.6), channel_id=1, source_target_pairs={{0,256},{256,0},{1,257},{257,1},{2,258},{258,2},{3,259},{259,3},{4... | collective-permute-start | bytes 1572872 | tf_op jit(solution)/shard_map/ppermute | solution.py:403
  59.2 28.3 %all-to-all-start.2 = ((f32[8,16,1024]{2,1,0:T(8,128)}), f32[8,16,1024]{2,1,0:T(8,128)}, u32[]{:S(2)}, u32[]{:S(2)}) async-start(f32[8,16,1024]{2,1,0:T(8,128)} %bitcast.36), calls=%async_computation.2 | async-start | bytes 1048576 | tf_op jit(solution)/shard_map/all_to_all | solution.py:365
  72.7 13.9 %collective-permute-start = (f32[128,1024]{1,0:T(8,128)S(1)}, f32[128,1024]{1,0:T(8,128)S(1)}, u32[]{:S(2)}, u32[]{:S(2)}) collective-permute-start(f32[128,1024]{1,0:T(8,128)S(1)} %head_share.4), channel_id=1, source_target_pairs={{0,256},{256,0},{1,257},{257,1},{2,258},{258,2},{3,259},{259,3},{4... | collective-permute-start | bytes 1572872 | tf_op jit(solution)/shard_map/ppermute | solution.py:403
  78.5 15.4 %copy-start.2 = (bf16[16,64,128]{2,1,0:T(8,128)(2,1)S(1)}, bf16[16,64,128]{2,1,0:T(8,128)(2,1)}, u32[]{:S(2)}) copy-start(bf16[16,64,128]{2,1,0:T(8,128)(2,1)} %param.9) | copy-start | bytes 786436
  78.6 15.4 %copy-start.4 = (f32[16,64]{1,0:T(8,128)S(1)}, f32[16,64]{1,0:T(8,128)}, u32[]{:S(2)}) copy-start(f32[16,64]{1,0:T(8,128)} %w_ref.7) | copy-start | bytes 12292
  87.5 21.0 %all-to-all-start.1 = ((f32[8,16,1024]{2,1,0:T(8,128)}), f32[8,16,1024]{2,1,0:T(8,128)S(1)}, u32[]{:S(2)}, u32[]{:S(2)}) async-start(f32[8,16,1024]{2,1,0:T(8,128)} %bitcast.6), calls=%async_computation.1 | async-start | bytes 1048576 | tf_op jit(solution)/shard_map/all_to_all | solution.py:365
  97.4 39.9 %collective-permute-start.2 = (f32[2,4,128,128]{3,2,1,0:T(8,128)S(1)}, f32[2,4,128,128]{3,2,1,0:T(8,128)S(1)}, u32[]{:S(2)}, u32[]{:S(2)}) collective-permute-start(f32[2,4,128,128]{3,2,1,0:T(8,128)S(1)} %get-tuple-element.13), channel_id=1, source_target_pairs={{0,256},{256,0},{1,257},{257,1},{2,258},{258,2},{3,259},{259,3},{4... | collective-permute-start | bytes 1572872 | tf_op jit(solution)/shard_map/ppermute | solution.py:420
  111.4 17.7 %all-to-all-start.3 = ((f32[8,128,128]{2,1,0:T(8,128)}), f32[8,128,128]{2,1,0:T(8,128)S(1)}, u32[]{:S(2)}, u32[]{:S(2)}) async-start(f32[8,128,128]{2,1,0:T(8,128)} %bitcast.8), calls=%async_computation.3 | async-start | bytes 1048576 | tf_op jit(solution)/shard_map/all_to_all | solution.py:365
  130.5 12.0 %all-to-all-start.4 = ((f32[4,128,128]{2,1,0:T(8,128)}), f32[4,128,128]{2,1,0:T(8,128)S(1)}, u32[]{:S(2)}, u32[]{:S(2)}) async-start(f32[4,128,128]{2,1,0:T(8,128)} %sum_copies.2), calls=%async_computation.4 | async-start | bytes 524288 | tf_op jit(solution)/shard_map/all_to_all | solution.py:365
  137.5 12.5 %collective-permute-start.3 = (f32[4,128,128]{2,1,0:T(8,128)S(1)}, f32[4,128,128]{2,1,0:T(8,128)S(1)}, u32[]{:S(2)}, u32[]{:S(2)}) collective-permute-start(f32[4,128,128]{2,1,0:T(8,128)S(1)} %dynamic-slice_bitcast_fusion), channel_id=1, source_target_pairs={{0,32},{32,0},{1,33},{33,1},{2,34},{34,2},{3,35},{35,3},{4,36},{36... | collective-permute-start | bytes 786440 | tf_op jit(solution)/shard_map/ppermute | solution.py:375
  143.9 22.8 %all-to-all-start.5 = ((f32[16,64,128]{2,1,0:T(8,128)}), f32[16,64,128]{2,1,0:T(8,128)S(1)}, u32[]{:S(2)}, u32[]{:S(2)}) async-start(f32[16,64,128]{2,1,0:T(8,128)} %bitcast.9), calls=%async_computation.5 | async-start | bytes 1048576 | tf_op jit(solution)/shard_map/all_to_all | solution.py:365
  150.1 11.4 %collective-permute-start.6 = (f32[128,128]{1,0:T(8,128)S(1)}, f32[128,128]{1,0:T(8,128)S(1)}, u32[]{:S(2)}, u32[]{:S(2)}) collective-permute-start(f32[128,128]{1,0:T(8,128)S(1)} %get-tuple-element.15), channel_id=1, source_target_pairs={{0,192},{64,128},{128,64},{192,0},{1,193},{65,129},{129,65},{193,1... | collective-permute-start | bytes 196616 | tf_op jit(solution)/shard_map/ppermute | solution.py:375
  152.1 9.4 %collective-permute-start.5 = (f32[128,128]{1,0:T(8,128)S(1)}, f32[128,128]{1,0:T(8,128)S(1)}, u32[]{:S(2)}, u32[]{:S(2)}) collective-permute-start(f32[128,128]{1,0:T(8,128)S(1)} %get-tuple-element.16), channel_id=1, source_target_pairs={{0,128},{64,192},{128,0},{192,64},{1,129},{65,193},{129,1},{193,65... | collective-permute-start | bytes 196616 | tf_op jit(solution)/shard_map/ppermute | solution.py:375
  156.7 9.3 %collective-permute-start.4 = (f32[128,128]{1,0:T(8,128)S(1)}, f32[128,128]{1,0:T(8,128)S(1)}, u32[]{:S(2)}, u32[]{:S(2)}) collective-permute-start(f32[128,128]{1,0:T(8,128)S(1)} %get-tuple-element.14), channel_id=1, source_target_pairs={{0,64},{64,0},{128,192},{192,128},{1,65},{65,1},{129,193},{193,129... | collective-permute-start | bytes 196616 | tf_op jit(solution)/shard_map/ppermute | solution.py:375
